TPU v7x, 128 devices: a whole 4x4x4 slice. The times are simulated.
128 devices in a mesh: occ: 16 (over y, z_hi, core), vir: 8 (over x, z_lo).
Axes of the slice: x: 4, y: 4, z: 4 (z_hi: 2, z_lo: 2; z = z_hi * 2 + z_lo), core: 2. Of those that a mesh axis runs over, the one named last changes fastest.
Arguments:
- three_index: bfloat16 [2048, 128, 640], P(('occ', 'vir')), may hold values from -0.69921875 to 0.69921875
- virt_coeff: bfloat16 [640, 512], replicated, may hold values from -0.25 to 0.25
- metric_root: bfloat16 [2048, 2048], P(('occ', 'vir')), may hold values from -0.125 to 0.125
- owner_table: int32 [128], replicated, may hold values from 0 to 127, each once
- pair_order: int32 [4], replicated, may hold values from 0 to 15
- occ_energy: float32 [128], replicated, may hold values from -1.5 to -0.3
- vir_energy: float32 [512], replicated, may hold values from 0.1 to 2.5
Outputs:
- density: float32 [128, 512, 2048], P('occ', 'vir')
Inputs may be any that keep to these rules, and one draw needn't show every extreme that they name: `owner_table`: each orbital once.
All inputs are finite; a program needn't handle non-finite values.
Results may differ from a plain program's by a relative error of at most 0.0045.
Values may be sent and summed in bfloat16 or wider, within the bound.
No kernel may reach another device: no remote copies, remote signals or barrier semaphores. Data moves between devices by JAX's collectives and lax.ppermute only.
A program may use at most 128 MiB of HBM per device.

v0:
```python
import numpy as np
import jax
import jax.numpy as jnp
from jax import lax
from jax.experimental import pallas as pl
from jax.experimental.pallas import tpu as pltpu
from jax.sharding import PartitionSpec as P


AXES = ("occ", "vir")
SIZE = {"x": 4, "y": 4, "z": 4}
ORDER = (("z", "x", "y"), ("y", "z", "x"))


def line(p):
    return ((p["y"] * 2 + p["z"] // 2) * 2 + p["c"]) * 8 + p["x"] * 2 + p["z"] % 2


def places():
    return [
        dict(x=x, y=y, z=z, c=c)
        for x in range(4)
        for y in range(4)
        for z in range(4)
        for c in range(2)
    ]


def moved(p, dim, by):
    q = dict(p)
    q[dim] = (q[dim] + by) % SIZE[dim]
    return q


def shifted(value, dims, by):
    pairs = [(line(p), line(moved(p, dims[p["c"]], by))) for p in places()]
    return lax.ppermute(value, AXES, pairs)


def swapped(value):
    pairs = [(line(p), line(dict(p, c=1 - p["c"]))) for p in places()]
    return lax.ppermute(value, AXES, pairs)


def metric_table():
    table = np.zeros((128, 8, 16), np.int32)
    for p in places():
        for buf in range(8):
            core = p["c"] if buf < 4 else 1 - p["c"]
            first, second, third = ORDER[core]
            for k2 in range(4):
                for k1 in range(4):
                    q = dict(p, c=core)
                    for dim, by in ((third, buf % 4), (second, k2), (first, k1)):
                        q = moved(q, dim, -by)
                    table[line(p), buf, k2 * 4 + k1] = line(q)
    return table


FIRST = ((("l", 0, 0), ("e", 0, 0), ("e", 0, 1)), (("l", 0, 1),))
SECOND = (
    (("e", 1, 0), ("e", 3, 0), ("e", 1, 1), ("e", 3, 1)),
    (("e", 2, 0), ("e", 2, 1), ("l", 1, 0)),
    (("l", 1, 1),),
)


def partner_table():
    chunk = np.zeros((128, 64), np.int32)
    step = np.zeros((64,), np.int32)
    for p in places():
        at = 0
        for kind, by, other in [key for group in FIRST + SECOND for key in group]:
            core = 1 - p["c"] if other else p["c"]
            if kind == "e":
                inner = [(by, kz, s) for kz in range(2) for s in (0, 1)]
            else:
                inner = [(ky, by, s) for ky in range(4) for s in (2, 3)]
            for ky, kz, s in inner:
                q = moved(moved(dict(p, c=core), "y", -ky), "z", 2 * kz)
                chunk[line(p), at] = line(q) // 8
                step[at] = s
                at += 1
    return chunk, step


def gathered_metric(rows):
    for stage in (0, 1):
        dims = (ORDER[0][stage], ORDER[1][stage])
        got = [shifted(rows, dims, by) for by in (1, 2, 3)]
        rows = jnp.concatenate([rows] + got, axis=0)
    dims = (ORDER[0][2], ORDER[1][2])
    mine = [rows] + [shifted(rows, dims, by) for by in (1, 2, 3)]
    return mine + [swapped(part) for part in mine]


def half_kernel(order_ref, owner_ref, ints_ref, coeff_ref, out_ref, scratch, pick_ref):
    owners = jnp.broadcast_to(owner_ref[...].astype(jnp.float32), (128, 128)).T
    orbital = lax.broadcasted_iota(jnp.int32, (128, 128), 1).astype(jnp.float32)
    pick_ref[0:128, :] = jnp.where(owners == orbital, 1.0, 0.0)
    for s in range(4):
        first = pl.multiple_of(order_ref[s] * 8, 8)
        pick_ref[128 + 8 * s:136 + 8 * s, :] = pick_ref[pl.ds(first, 8), :]
    pick = pick_ref[...].astype(jnp.bfloat16)

    def select(c, carry):
        half = jnp.dot(
            ints_ref[pl.ds(c * 4, 4)].reshape(512, 640),
            coeff_ref[...],
            preferred_element_type=jnp.float32,
        ).astype(jnp.bfloat16)
        for i in range(4):
            rows = jnp.dot(
                pick, half[i * 128:i * 128 + 128], preferred_element_type=jnp.float32
            )
            for t in range(4):
                at = pl.ds(c * 4 + i, 160, stride=16)
                scratch.at[t][at, :] = rows[:, t * 128:t * 128 + 128]
        return carry

    lax.fori_loop(0, 4, select, 0)
    lane = lax.broadcasted_iota(jnp.int32, (16, 128), 1)
    low = lane < 64

    def emit(group, carry):
        first_row = pl.multiple_of(group * 128, 128)
        to = pl.multiple_of(group * 8, 8)
        for t in range(4):
            for j in range(4):
                even = scratch[t, pl.ds(first_row + 32 * j, 16), :]
                odd = scratch[t, pl.ds(first_row + 32 * j + 16, 16), :]
                first = jnp.where(low, even, pltpu.roll(odd, 64, 1))
                second = jnp.where(low, pltpu.roll(even, 64, 1), odd)
                at = slice(j * 128, j * 128 + 128)
                out_ref[to + 2 * t, :, at] = first.astype(out_ref.dtype)
                out_ref[to + 2 * t + 1, :, at] = second.astype(out_ref.dtype)
        return carry

    lax.fori_loop(0, 16, emit, 0)

    def emit_partner(v, carry):
        for t in range(4):
            tiles = [
                scratch[t, pl.ds(pl.multiple_of((128 + s * 8 + v) * 16, 16), 16), :]
                for s in range(4)
            ]
            for g in range(4):
                total = jnp.zeros((16, 128), jnp.float32)
                for s in range(4):
                    by = (s - g) * 32 % 128
                    tile = pltpu.roll(tiles[s], by, 1) if by else tiles[s]
                    total = jnp.where(lane // 32 == s, tile, total)
                out_ref[(t * 4 + g) * 8 + v, :, 512:640] = total.astype(out_ref.dtype)
        return carry

    lax.fori_loop(0, 8, emit_partner, 0)


def transformed(pair_order, owner_table, three_index, virt_coeff):
    vmem = pl.BlockSpec(memory_space=pltpu.VMEM)
    return pl.pallas_call(
        half_kernel,
        in_specs=[pl.BlockSpec(memory_space=pltpu.SMEM)] + [vmem] * 3,
        out_specs=vmem,
        out_shape=jax.ShapeDtypeStruct((128, 16, 640), jnp.bfloat16),
        scratch_shapes=[
            pltpu.VMEM((4, 160 * 16, 128), jnp.float32),
            pltpu.VMEM((160, 128), jnp.float32),
        ],
        name="half",
    )(pair_order, owner_table.reshape(1, 128), three_index, virt_coeff)


def fit_kernel(table_ref, rows_ref, *refs, first, width, outs):
    parts, out_refs = refs[:8], refs[8:8 + outs]
    rows, metric, sems, row_sem = refs[8 + outs:]
    take = pltpu.make_async_copy(rows_ref.at[:, pl.ds(first, width)], rows, row_sem)
    take.start()
    for buf in range(8):

        def start(j, carry, buf=buf):
            row = pl.multiple_of(table_ref[buf * 16 + j] * 16, 16)
            pltpu.make_async_copy(
                parts[buf].at[pl.ds(pl.multiple_of(j * 16, 16), 16)],
                metric.at[pl.ds(row, 16)],
                sems.at[buf],
            ).start()
            return carry

        lax.fori_loop(0, 16, start, 0)
    take.wait()
    left = rows[...].T
    for buf in range(8):
        pltpu.make_async_copy(parts[buf], metric.at[pl.ds(0, 256)], sems.at[buf]).wait()
    each = width // outs
    for block in range(4):
        at = slice(block * 512, block * 512 + 512)
        fitted = lax.dot_general(
            left, metric[at, :], (((1,), (1,)), ((), ())), preferred_element_type=jnp.float32
        ).astype(jnp.bfloat16)
        for i in range(outs):
            out_refs[i][:, at] = fitted[i * each:i * each + each]


def fit(table, owned, parts, first, width, outs):
    vmem = pl.BlockSpec(memory_space=pltpu.VMEM)
    shape = jax.ShapeDtypeStruct((width // outs, 2048), jnp.bfloat16)

    def body(*refs):
        fit_kernel(*refs, first=first, width=width, outs=outs)

    return pl.pallas_call(
        body,
        in_specs=[pl.BlockSpec(memory_space=pltpu.SMEM)] + [pl.BlockSpec(memory_space=pl.ANY)] * 9,
        out_specs=[vmem] * outs,
        out_shape=[shape] * outs,
        scratch_shapes=[
            pltpu.VMEM((2048, width), jnp.bfloat16),
            pltpu.VMEM((2048, 2048), jnp.bfloat16),
            pltpu.SemaphoreType.DMA((8,)),
            pltpu.SemaphoreType.DMA,
        ],
        name="fit_own" if outs == 1 else "fit_partner",
    )(table, owned, *parts)


def pair_kernel(own_ref, row_ref, col_ref, *refs, groups, chained):
    count = sum(groups)
    if chained:
        total_ref, refs = refs[0], refs[1:]
    parts, (out_ref, own, buf, sems, more) = refs[:count], refs[count:]
    take = pltpu.make_async_copy(own_ref, own, more.at[0])
    take.start()
    copies, at = [], 0
    for i, part in enumerate(parts):
        rows = part.shape[0]
        copies.append(pltpu.make_async_copy(part, buf.at[pl.ds(at, rows)], sems.at[i]))
        copies[-1].start()
        at += rows
    if chained:
        total = pltpu.make_async_copy(total_ref, out_ref, more.at[1])
        total.start()
    row = row_ref[:, :1]
    take.wait()
    start, piece = 0, 0
    for block, size in enumerate(groups):
        rows = 0
        for _ in range(size):
            copies[piece].wait()
            rows += parts[piece].shape[0]
            piece += 1
        part = buf[start:start + rows, :]
        pair = lax.dot_general(
            own[...], part, (((1,), (1,)), ((), ())), preferred_element_type=jnp.float32
        )
        amp = (pair / (row + col_ref[:, start:start + rows])).astype(jnp.bfloat16)
        if block == 0 and chained:
            total.wait()
        term = jnp.dot(amp, part, preferred_element_type=jnp.float32)
        if block == 0 and not chained:
            out_ref[...] = term
        else:
            out_ref[...] += term
        start += rows


def paired(own, row, col, groups, total=None):
    vmem, hbm = pl.BlockSpec(memory_space=pltpu.VMEM), pl.BlockSpec(memory_space=pl.ANY)
    parts = [part for group in groups for part in group]
    chained = total is not None
    more = [total] if chained else []
    rows = sum(part.shape[0] for part in parts)
    sizes = tuple(len(group) for group in groups)

    def body(*refs):
        pair_kernel(*refs, groups=sizes, chained=chained)

    return pl.pallas_call(
        body,
        in_specs=[hbm, vmem, vmem] + [hbm] * (len(parts) + len(more)),
        out_specs=vmem,
        out_shape=jax.ShapeDtypeStruct((512, 2048), jnp.float32),
        scratch_shapes=[
            pltpu.VMEM((512, 2048), jnp.bfloat16),
            pltpu.VMEM((rows, 2048), jnp.bfloat16),
            pltpu.SemaphoreType.DMA((len(parts),)),
            pltpu.SemaphoreType.DMA((2,)),
        ],
        name="pair_more" if chained else "pair",
    )(own, row, col, *more, *parts)


def energies(me, owner_table, pair_order, occ_energy, vir_energy):
    occ_idx, vir_idx = me // 8, me % 8
    one_hot = (owner_table[:, None] == jnp.arange(128, dtype=jnp.int32)[None, :]).astype(jnp.float32)
    eps = jnp.dot(one_hot, occ_energy, precision=lax.Precision.HIGHEST)
    own_eps = lax.dynamic_slice_in_dim(eps, occ_idx * 8, 8, 0)
    block_eps = lax.dynamic_slice_in_dim(vir_energy, vir_idx * 64, 64, 0)
    row = (own_eps[:, None] - block_eps[None, :]).reshape(512, 1)
    row = jnp.broadcast_to(row, (512, 128))
    chunks, steps = partner_table()
    chunk = lax.dynamic_slice_in_dim(jnp.asarray(chunks), me, 1, 0).reshape(64)
    pick = (chunk[:, None] == jnp.arange(16, dtype=jnp.int32)[None, :]).astype(jnp.float32)
    vir_rows = jnp.dot(pick, vir_energy.reshape(16, 32), precision=lax.Precision.HIGHEST)
    partner_eps = jnp.concatenate(
        [lax.dynamic_slice_in_dim(eps, pair_order[s] * 8 + vir_idx, 1, 0) for s in range(4)]
    )
    which = jnp.asarray((steps[:, None] == np.arange(4)[None, :]).astype(np.float32))
    eps_rows = jnp.dot(which, partner_eps[:, None], precision=lax.Precision.HIGHEST)
    return row, (eps_rows - vir_rows).reshape(1, 2048)


def whole(three_index, virt_coeff, metric_root, owner_table, pair_order, occ_energy, vir_energy):
    me = lax.axis_index("occ") * 8 + lax.axis_index("vir")
    metric_parts = gathered_metric(metric_root)
    sent = transformed(pair_order, owner_table, three_index, virt_coeff)
    owned = lax.all_to_all(sent, AXES, split_axis=0, concat_axis=0, tiled=True)
    owned = owned.reshape(2048, 640)

    row, col = energies(me, owner_table, pair_order, occ_energy, vir_energy)
    table = lax.dynamic_slice_in_dim(jnp.asarray(metric_table()), me, 1, 0).reshape(128)
    owned, row, col, table = lax.optimization_barrier((owned, row, col, table))

    early, late = fit(table, owned, metric_parts, 512, 128, 2)
    (own,) = fit(table, owned, metric_parts, 0, 512, 1)

    ydim, zdim = ("y", "y"), ("z", "z")
    early = jnp.concatenate([early, shifted(early, zdim, 2)], axis=0)
    late = jnp.concatenate([late] + [shifted(late, ydim, by) for by in (1, 2, 3)], axis=0)
    have = {("e", 0): early, ("l", 0): late}
    for by in (2, 1, 3):
        have["e", by] = shifted(early, ydim, by)
    have["l", 1] = shifted(late, zdim, 2)
    pieces = {}
    for (kind, by), part in have.items():
        pieces[kind, by, 0] = part
        pieces[kind, by, 1] = swapped(part)

    first = [[pieces[key] for key in group] for group in FIRST]
    second = [[pieces[key] for key in group] for group in SECOND]
    density = paired(own, row, col[:, :768], first)
    density = paired(own, row, col[:, 768:], second, density)
    return density.reshape(8, 64, 2048)


def solution(mesh):
    placed = (P(AXES, None, None), P(), P(AXES, None), P(), P(), P(), P())
    return jax.shard_map(
        whole, mesh=mesh, in_specs=placed, out_specs=P("occ", "vir", None), check_vma=False
    )
```

profile of v0, /device:TPU:1, one launch (start us, length us, event | category | flops | bytes accessed | tf_op | source)
XLA Modules:
  0.0 228.3 jit_solution(13415698903943417652)
XLA Ops:
  0.0 3.7 %collective-permute-start.1 = (bf16[16,2048]{1,0:T(8,128)(2,1)}, bf16[16,2048]{1,0:T(8,128)(2,1)S(1)}, u32[]{:S(2)}, u32[]{:S(2)}) collective-permute-start(bf16[16,2048]{1,0:T(8,128)(2,1)} %param.12), channel_id=1, source_target_pairs={{0,16},{8,72},{1,17},{9,73},{16,0},{24,88},{17,1},{25,89},{32,48},... | collective-permute-start | bytes 196616 | tf_op jit(solution)/shard_map/ppermute | solution.py:37
  3.7 0.4 collective-permute-start
  4.1 2.3 collective-permute-start.2
  6.4 1.5 constant_dynamic-update-slice_fusion.3
  7.9 0.3 collective-permute-done
  8.3 0.6 constant_dynamic-update-slice_fusion.2
  8.9 0.6 constant_dynamic-update-slice_fusion.1
  9.6 0.6 constant_dynamic-update-slice_fusion
  10.2 1.6 collective-permute-start.3
  11.8 3.3 %collective-permute-start.4 = (bf16[64,2048]{1,0:T(8,128)(2,1)S(1)}, bf16[64,2048]{1,0:T(8,128)(2,1)S(1)}, u32[]{:S(2)}, u32[]{:S(2)}) collective-permute-start(bf16[64,2048]{1,0:T(8,128)(2,1)S(1)} %get-tuple-element.17), channel_id=1, source_target_pairs={{0,4},{8,24},{1,5},{9,25},{16,20},{24,8},{17,21},{25,9},{32,36},{4... | collective-permute-start | bytes 786440 | tf_op jit(solution)/shard_map/ppermute | solution.py:37
  15.1 11.2 %half.1 = bf16[128,16,640]{2,1,0:T(8,128)(2,1)} custom-call(s32[4]{0:T(128)} %order_ref.1, s32[1,128]{1,0:T(1,128)} %bitcast.23, bf16[16,128,640]{2,1,0:T(8,128)(2,1)} %ints_ref.1, bf16[640,512]{1,0:T(8,128)(2,1)} %coeff_ref.1), custom_call_target="tpu_custom_call" | custom-call | tf_op jit(solution)/shard_map/half/pallas_call | solution.py:161
  26.4 8.4 %all-to-all-start = ((bf16[128,16,640]{2,1,0:T(8,128)(2,1)}), bf16[128,16,640]{2,1,0:T(8,128)(2,1)S(1)}, u32[]{:S(2)}, u32[]{:S(2)}) async-start(bf16[128,16,640]{2,1,0:T(8,128)(2,1)} %half.1), calls=%async_computation | async-start | bytes 5242880 | tf_op jit(solution)/shard_map/all_to_all | solution.py:317
  34.8 3.3 %collective-permute-start.5 = (bf16[64,2048]{1,0:T(8,128)(2,1)S(1)}, bf16[64,2048]{1,0:T(8,128)(2,1)S(1)}, u32[]{:S(2)}, u32[]{:S(2)}) collective-permute-start(bf16[64,2048]{1,0:T(8,128)(2,1)S(1)} %get-tuple-element.17), channel_id=1, source_target_pairs={{0,6},{8,25},{1,7},{9,8},{16,22},{24,9},{17,23},{25,24},{32,38},{4... | collective-permute-start | bytes 786440 | tf_op jit(solution)/shard_map/ppermute | solution.py:37
  38.1 0.7 constant_dynamic-update-slice_fusion.6
  38.8 0.7 constant_dynamic-update-slice_fusion.5
  39.6 27.3 %collective-permute-done.5 = bf16[64,2048]{1,0:T(8,128)(2,1)S(1)} collective-permute-done((bf16[64,2048]{1,0:T(8,128)(2,1)S(1)}, bf16[64,2048]{1,0:T(8,128)(2,1)S(1)}, u32[]{:S(2)}, u32[]{:S(2)}) %collective-permute-start.5) | collective-permute-done | bytes 262176 | tf_op jit(solution)/shard_map/ppermute | solution.py:37
  66.8 0.7 constant_dynamic-update-slice_fusion.4.refs_2_
  67.5 3.4 %collective-permute-start.8 = (bf16[256,2048]{1,0:T(8,128)(2,1)}, bf16[256,2048]{1,0:T(8,128)(2,1)}, u32[]{:S(2)}, u32[]{:S(2)}) collective-permute-start(bf16[256,2048]{1,0:T(8,128)(2,1)} %constant_dynamic-update-slice_fusion.4.refs_2_), channel_id=1, source_target_pairs={{0,96},{8,14},{1,97},{9,15},{16,112},{24,30},{17,113},{25,31},{32,... | collective-permute-start | bytes 3145736 | tf_op jit(solution)/shard_map/ppermute | solution.py:37
  70.9 0.4 collective-permute-start.7
  71.4 0.8 collective-permute-start.6
  72.2 1.0 collective-permute-start.9
  73.1 21.1 %collective-permute-done.8.refs_5_ = bf16[256,2048]{1,0:T(8,128)(2,1)} collective-permute-done((bf16[256,2048]{1,0:T(8,128)(2,1)}, bf16[256,2048]{1,0:T(8,128)(2,1)}, u32[]{:S(2)}, u32[]{:S(2)}) %collective-permute-start.8) | collective-permute-done | bytes 1048608 | tf_op jit(solution)/shard_map/ppermute | solution.py:37
  94.2 1.2 collective-permute-start.12
  95.4 2.5 %collective-permute-done.6.refs_3_ = bf16[256,2048]{1,0:T(8,128)(2,1)} collective-permute-done((bf16[256,2048]{1,0:T(8,128)(2,1)}, bf16[256,2048]{1,0:T(8,128)(2,1)}, u32[]{:S(2)}, u32[]{:S(2)}) %collective-permute-start.6) | collective-permute-done | bytes 1048608 | tf_op jit(solution)/shard_map/ppermute | solution.py:37
  97.9 1.4 collective-permute-start.10
  99.4 0.6 fusion.5
  102.5 0.1 reshape.51
  102.6 0.2 convolution_bitcast_fusion.1
  102.8 0.1 dynamic_slice.24
  103.0 0.1 sub.36
  103.1 0.7 constant_dynamic-slice_fusion
  103.8 0.6 reshape.53.refs_0_
  104.4 0.7 fusion.4
  105.0 0.7 dynamic-slice_bitcast_fusion
  105.7 2.6 %convolution_bitcast_fusion = f32[64]{0:T(128)S(1)} fusion(f32[64,4]{1,0:T(8,128)S(1)} %copy-done.7, f32[1]{0:T(128)} %get-tuple-element.26, f32[1]{0:T(128)} %get-tuple-element.27, f32[1]{0:T(128)} %get-tuple-element.28, f32[1]{0:T(128)} %get-tuple-element.25), kind=kOutput, calls=%fused_computation.1 | convolution fusion | flops 3084 | bytes 1296 | tf_op jit(solution)/shard_map/dot_general | solution.py:309
  108.4 0.2 convolution_subtract_fusion
  108.6 0.1 copy.12
  108.7 0.1 reshape.52
  108.8 1.0 broadcast_in_dim.2.refs_1_
  109.8 0.6 copy-done.1
  110.4 8.0 %fit_partner.1 = (bf16[64,2048]{1,0:T(8,128)(2,1)}, bf16[64,2048]{1,0:T(8,128)(2,1)}) custom-call(s32[128]{0:T(128)} %reshape.53.refs_0_, bf16[2048,640]{1,0:T(8,128)(2,1)} %bitcast.21, bf16[256,2048]{1,0:T(8,128)(2,1)} %constant_dynamic-update-slice_fusion.4.refs_2_, bf16[256,2048]{1,0:T(8,128)(2,1)} %collective-permute-done.6.refs_3_, ...), custom_call_target="tpu_custom_call" | custom-call | tf_op jit(solution)/shard_map/fit_partner/pallas_call | solution.py:212
  118.5 2.7 %collective-permute-start.15 = (bf16[64,2048]{1,0:T(8,128)(2,1)}, bf16[64,2048]{1,0:T(8,128)(2,1)S(1)}, u32[]{:S(2)}, u32[]{:S(2)}) collective-permute-start(bf16[64,2048]{1,0:T(8,128)(2,1)} %get-tuple-element.15), channel_id=1, source_target_pairs={{0,96},{8,104},{1,97},{9,105},{16,112},{24,120},{17,113},{25,121},... | collective-permute-start | bytes 786440 | tf_op jit(solution)/shard_map/ppermute | solution.py:37
  121.2 1.0 constant_dynamic-update-slice_fusion.14
  122.2 11.2 %collective-permute-done.13 = bf16[64,2048]{1,0:T(8,128)(2,1)S(1)} collective-permute-done((bf16[64,2048]{1,0:T(8,128)(2,1)}, bf16[64,2048]{1,0:T(8,128)(2,1)S(1)}, u32[]{:S(2)}, u32[]{:S(2)}) %collective-permute-start.13) | collective-permute-done | bytes 262176 | tf_op jit(solution)/shard_map/ppermute | solution.py:37
  133.5 3.3 %collective-permute-start.25 = (bf16[256,2048]{1,0:T(8,128)(2,1)S(1)}, bf16[256,2048]{1,0:T(8,128)(2,1)S(1)}, u32[]{:S(2)}, u32[]{:S(2)}) collective-permute-start(bf16[256,2048]{1,0:T(8,128)(2,1)S(1)} %constant_dynamic-update-slice_fusion.11.refs_3_), channel_id=1, source_target_pairs={{0,16},{8,24},{1,17},{9,25},{16,0},{24,8},{17,1},{25,9},{32,48},{4... | collective-permute-start | bytes 3145736 | tf_op jit(solution)/shard_map/ppermute | solution.py:37
  136.8 0.1 collective-permute-start.16
  136.9 1.0 constant_dynamic-update-slice_fusion.16
  137.9 27.2 %collective-permute-done.16 = bf16[64,2048]{1,0:T(8,128)(2,1)S(1)} collective-permute-done((bf16[64,2048]{1,0:T(8,128)(2,1)}, bf16[64,2048]{1,0:T(8,128)(2,1)S(1)}, u32[]{:S(2)}, u32[]{:S(2)}) %collective-permute-start.16) | collective-permute-done | bytes 262176 | tf_op jit(solution)/shard_map/ppermute | solution.py:37
  165.1 0.9 collective-permute-start.23
  166.0 2.1 collective-permute-start.20
  168.2 2.0 collective-permute-start.18
  170.2 8.6 %collective-permute-done.23.refs_8_ = bf16[128,2048]{1,0:T(8,128)(2,1)S(1)} collective-permute-done((bf16[128,2048]{1,0:T(8,128)(2,1)S(1)}, bf16[128,2048]{1,0:T(8,128)(2,1)S(1)}, u32[]{:S(2)}, u32[]{:S(2)}) %collective-permute-start.23) | collective-permute-done | bytes 524320 | tf_op jit(solution)/shard_map/ppermute | solution.py:37
  178.8 4.2 %collective-permute-start.17 = (bf16[128,2048]{1,0:T(8,128)(2,1)S(1)}, bf16[128,2048]{1,0:T(8,128)(2,1)S(1)}, u32[]{:S(2)}, u32[]{:S(2)}) collective-permute-start(bf16[128,2048]{1,0:T(8,128)(2,1)S(1)} %constant_dynamic-update-slice_fusion.15.refs_4_), channel_id=1, source_target_pairs={{0,8},{8,0},{1,9},{9,1},{16,24},{24,16},{17,25},{25,17},{32,40},{4... | collective-permute-start | bytes 1572872 | tf_op jit(solution)/shard_map/ppermute | solution.py:42
  183.0 0.1 collective-permute-start.26
  183.1 7.3 %collective-permute-done.20.refs_5_ = bf16[128,2048]{1,0:T(8,128)(2,1)} collective-permute-done((bf16[128,2048]{1,0:T(8,128)(2,1)S(1)}, bf16[128,2048]{1,0:T(8,128)(2,1)}, u32[]{:S(2)}, u32[]{:S(2)}) %collective-permute-start.20) | collective-permute-done | bytes 524320 | tf_op jit(solution)/shard_map/ppermute | solution.py:37
  190.4 1.7 collective-permute-start.24
  192.1 0.3 collective-permute-start.22
  192.4 0.8 copy-done.6
  193.2 0.2 collective-permute-start.21
  193.4 0.6 slice.23.refs_2_
  194.0 0.6 slice.22.refs_2_
  194.6 10.7 %fit_own.1.refs_0_ = bf16[512,2048]{1,0:T(8,128)(2,1)} custom-call(s32[128]{0:T(128)} %reshape.53.refs_0_, bf16[2048,640]{1,0:T(8,128)(2,1)} %bitcast.22, bf16[256,2048]{1,0:T(8,128)(2,1)} %constant_dynamic-update-slice_fusion.4.refs_2_, bf16[256,2048]{1,0:T(8,128)(2,1)} %collective-permute-done.6.refs_3_, bf16[256,2048]{1,0:T(8,128)(2,1)} %collective-permute-done.7.refs_4_, ...), custom_call_target="tpu_custom_call" | custom-call | tf_op jit(solution)/shard_map/fit_own/pallas_call | solution.py:212
  205.3 9.8 %pair.1.refs_3_ = f32[512,2048]{1,0:T(8,128)} custom-call(bf16[512,2048]{1,0:T(8,128)(2,1)} %fit_own.1.refs_0_, f32[512,128]{1,0:T(8,128)} %broadcast_in_dim.2.refs_1_, f32[1,768]{1,0:T(1,128)} %slice.23.refs_2_, bf16[256,2048]{1,0:T(8,128)(2,1)} %copy-done.2, bf16[128,2048]{1,0:T(8,128)(2,1)} %copy-done.3, bf16[128,2048]{1,0:T(8,128)(2,1)} %copy-done.6, ...), custom_call_target="tpu_custom_call" | custom-call | tf_op jit(solution)/shard_map/pair/pallas_call | solution.py:278
  215.2 12.9 %pair_more.1 = f32[512,2048]{1,0:T(8,128)} custom-call(bf16[512,2048]{1,0:T(8,128)(2,1)} %fit_own.1.refs_0_, f32[512,128]{1,0:T(8,128)} %broadcast_in_dim.2.refs_1_, f32[1,1280]{1,0:T(1,128)} %slice.22.refs_2_, f32[512,2048]{1,0:T(8,128)} %pair.1.refs_3_, bf16[128,2048]{1,0:T(8,128)(2,1)} %collective-permute-done.19.refs_4_, ...), custom_call_target="tpu_custom_call" | custom-call | tf_op jit(solution)/shard_map/pair_more/pallas_call | solution.py:278
  (50 shorter events, 0.4 us)
Async XLA Ops:
  0.0 102.6 %copy-start = (f32[128]{0:T(128)S(1)}, f32[128]{0:T(128)}, u32[]{:S(2)}) copy-start(f32[128]{0:T(128)} %param.15) | copy-start | bytes 1540
  0.0 8.9 %collective-permute-start.1 = (bf16[16,2048]{1,0:T(8,128)(2,1)}, bf16[16,2048]{1,0:T(8,128)(2,1)S(1)}, u32[]{:S(2)}, u32[]{:S(2)}) collective-permute-start(bf16[16,2048]{1,0:T(8,128)(2,1)} %param.12), channel_id=1, source_target_pairs={{0,16},{8,72},{1,17},{9,73},{16,0},{24,88},{17,1},{25,89},{32,48},... | collective-permute-start | bytes 196616 | tf_op jit(solution)/shard_map/ppermute | solution.py:37
  3.7 4.5 %collective-permute-start = (bf16[16,2048]{1,0:T(8,128)(2,1)}, bf16[16,2048]{1,0:T(8,128)(2,1)S(1)}, u32[]{:S(2)}, u32[]{:S(2)}) collective-permute-start(bf16[16,2048]{1,0:T(8,128)(2,1)} %param.12), channel_id=1, source_target_pairs={{0,1},{8,40},{1,16},{9,41},{16,17},{24,56},{17,0},{25,57},{32,33},... | collective-permute-start | bytes 196616 | tf_op jit(solution)/shard_map/ppermute | solution.py:37
  4.1 5.4 %collective-permute-start.2 = (bf16[16,2048]{1,0:T(8,128)(2,1)}, bf16[16,2048]{1,0:T(8,128)(2,1)S(1)}, u32[]{:S(2)}, u32[]{:S(2)}) collective-permute-start(bf16[16,2048]{1,0:T(8,128)(2,1)} %param.12), channel_id=1, source_target_pairs={{0,17},{8,104},{1,0},{9,105},{16,1},{24,120},{17,16},{25,121},{32,... | collective-permute-start | bytes 196616 | tf_op jit(solution)/shard_map/ppermute | solution.py:37
  10.2 27.9 %collective-permute-start.3 = (bf16[64,2048]{1,0:T(8,128)(2,1)S(1)}, bf16[64,2048]{1,0:T(8,128)(2,1)S(1)}, u32[]{:S(2)}, u32[]{:S(2)}) collective-permute-start(bf16[64,2048]{1,0:T(8,128)(2,1)S(1)} %get-tuple-element.17), channel_id=1, source_target_pairs={{0,2},{8,9},{1,3},{9,24},{16,18},{24,25},{17,19},{25,8},{32,34},{4... | collective-permute-start | bytes 786440 | tf_op jit(solution)/shard_map/ppermute | solution.py:37
  11.8 27.0 %collective-permute-start.4 = (bf16[64,2048]{1,0:T(8,128)(2,1)S(1)}, bf16[64,2048]{1,0:T(8,128)(2,1)S(1)}, u32[]{:S(2)}, u32[]{:S(2)}) collective-permute-start(bf16[64,2048]{1,0:T(8,128)(2,1)S(1)} %get-tuple-element.17), channel_id=1, source_target_pairs={{0,4},{8,24},{1,5},{9,25},{16,20},{24,8},{17,21},{25,9},{32,36},{4... | collective-permute-start | bytes 786440 | tf_op jit(solution)/shard_map/ppermute | solution.py:37
  26.4 73.0 %copy-start.8 = (s32[4]{0:T(128)S(1)}, s32[4]{0:T(128)}, u32[]{:S(2)}) copy-start(s32[4]{0:T(128)} %order_ref.1) | copy-start | bytes 52
  26.4 76.1 %copy-start.9 = (f32[512]{0:T(512)S(1)}, f32[512]{0:T(512)}, u32[]{:S(2)}) copy-start(f32[512]{0:T(512)} %param.16) | copy-start | bytes 6148
  26.4 76.3 %copy-start.10 = (s32[128]{0:T(128)S(1)}, s32[128]{0:T(128)}, u32[]{:S(2)}) copy-start(s32[128]{0:T(128)} %param.13) | copy-start | bytes 1540
  26.4 79.4 %copy-start.7 = (f32[64,4]{1,0:T(8,128)S(1)}, f32[64,4]{1,0:T(8,128)}, u32[]{:S(2)}) copy-start(f32[64,4]{1,0:T(8,128)} %constant.54.clone) | copy-start | bytes 3076
  26.4 82.4 %all-to-all-start = ((bf16[128,16,640]{2,1,0:T(8,128)(2,1)}), bf16[128,16,640]{2,1,0:T(8,128)(2,1)S(1)}, u32[]{:S(2)}, u32[]{:S(2)}) async-start(bf16[128,16,640]{2,1,0:T(8,128)(2,1)} %half.1), calls=%async_computation | async-start | bytes 5242880 | tf_op jit(solution)/shard_map/all_to_all | solution.py:317
  34.8 32.0 %collective-permute-start.5 = (bf16[64,2048]{1,0:T(8,128)(2,1)S(1)}, bf16[64,2048]{1,0:T(8,128)(2,1)S(1)}, u32[]{:S(2)}, u32[]{:S(2)}) collective-permute-start(bf16[64,2048]{1,0:T(8,128)(2,1)S(1)} %get-tuple-element.17), channel_id=1, source_target_pairs={{0,6},{8,25},{1,7},{9,8},{16,22},{24,9},{17,23},{25,24},{32,38},{4... | collective-permute-start | bytes 786440 | tf_op jit(solution)/shard_map/ppermute | solution.py:37
  67.5 26.7 %collective-permute-start.8 = (bf16[256,2048]{1,0:T(8,128)(2,1)}, bf16[256,2048]{1,0:T(8,128)(2,1)}, u32[]{:S(2)}, u32[]{:S(2)}) collective-permute-start(bf16[256,2048]{1,0:T(8,128)(2,1)} %constant_dynamic-update-slice_fusion.4.refs_2_), channel_id=1, source_target_pairs={{0,96},{8,14},{1,97},{9,15},{16,112},{24,30},{17,113},{25,31},{32,... | collective-permute-start | bytes 3145736 | tf_op jit(solution)/shard_map/ppermute | solution.py:37
  70.9 24.5 %collective-permute-start.7 = (bf16[256,2048]{1,0:T(8,128)(2,1)}, bf16[256,2048]{1,0:T(8,128)(2,1)}, u32[]{:S(2)}, u32[]{:S(2)}) collective-permute-start(bf16[256,2048]{1,0:T(8,128)(2,1)} %constant_dynamic-update-slice_fusion.4.refs_2_), channel_id=1, source_target_pairs={{0,64},{8,12},{1,65},{9,13},{16,80},{24,28},{17,81},{25,29},{32,96... | collective-permute-start | bytes 3145736 | tf_op jit(solution)/shard_map/ppermute | solution.py:37
  71.4 26.6 %collective-permute-start.6 = (bf16[256,2048]{1,0:T(8,128)(2,1)}, bf16[256,2048]{1,0:T(8,128)(2,1)}, u32[]{:S(2)}, u32[]{:S(2)}) collective-permute-start(bf16[256,2048]{1,0:T(8,128)(2,1)} %constant_dynamic-update-slice_fusion.4.refs_2_), channel_id=1, source_target_pairs={{0,32},{8,10},{1,33},{9,11},{16,48},{24,26},{17,49},{25,27},{32,64... | collective-permute-start | bytes 3145736 | tf_op jit(solution)/shard_map/ppermute | solution.py:37
  72.2 37.6 %collective-permute-start.9 = (bf16[256,2048]{1,0:T(8,128)(2,1)}, bf16[256,2048]{1,0:T(8,128)(2,1)}, u32[]{:S(2)}, u32[]{:S(2)}) collective-permute-start(bf16[256,2048]{1,0:T(8,128)(2,1)} %constant_dynamic-update-slice_fusion.4.refs_2_), channel_id=1, source_target_pairs={{0,8},{8,0},{1,9},{9,1},{16,24},{24,16},{17,25},{25,17},{32,40},{4... | collective-permute-start | bytes 3145736 | tf_op jit(solution)/shard_map/ppermute | solution.py:42
  94.2 15.6 %collective-permute-start.12 = (bf16[256,2048]{1,0:T(8,128)(2,1)}, bf16[256,2048]{1,0:T(8,128)(2,1)}, u32[]{:S(2)}, u32[]{:S(2)}) collective-permute-start(bf16[256,2048]{1,0:T(8,128)(2,1)} %collective-permute-done.8.refs_5_), channel_id=1, source_target_pairs={{0,8},{8,0},{1,9},{9,1},{16,24},{24,16},{17,25},{25,17},{32,40},{4... | collective-permute-start | bytes 3145736 | tf_op jit(solution)/shard_map/ppermute | solution.py:42
  95.4 14.4 %collective-permute-start.11 = (bf16[256,2048]{1,0:T(8,128)(2,1)}, bf16[256,2048]{1,0:T(8,128)(2,1)}, u32[]{:S(2)}, u32[]{:S(2)}) collective-permute-start(bf16[256,2048]{1,0:T(8,128)(2,1)} %collective-permute-done.7.refs_4_), channel_id=1, source_target_pairs={{0,8},{8,0},{1,9},{9,1},{16,24},{24,16},{17,25},{25,17},{32,40},{4... | collective-permute-start | bytes 3145736 | tf_op jit(solution)/shard_map/ppermute | solution.py:42
  97.9 11.9 %collective-permute-start.10 = (bf16[256,2048]{1,0:T(8,128)(2,1)}, bf16[256,2048]{1,0:T(8,128)(2,1)}, u32[]{:S(2)}, u32[]{:S(2)}) collective-permute-start(bf16[256,2048]{1,0:T(8,128)(2,1)} %collective-permute-done.6.refs_3_), channel_id=1, source_target_pairs={{0,8},{8,0},{1,9},{9,1},{16,24},{24,16},{17,25},{25,17},{32,40},{4... | collective-permute-start | bytes 3145736 | tf_op jit(solution)/shard_map/ppermute | solution.py:42
  108.8 1.6 copy-start.1
  118.4 15.0 %collective-permute-start.13 = (bf16[64,2048]{1,0:T(8,128)(2,1)}, bf16[64,2048]{1,0:T(8,128)(2,1)S(1)}, u32[]{:S(2)}, u32[]{:S(2)}) collective-permute-start(bf16[64,2048]{1,0:T(8,128)(2,1)} %get-tuple-element.15), channel_id=1, source_target_pairs={{0,32},{8,40},{1,33},{9,41},{16,48},{24,56},{17,49},{25,57},{32,64... | collective-permute-start | bytes 786440 | tf_op jit(solution)/shard_map/ppermute | solution.py:37
  118.5 15.0 %collective-permute-start.15 = (bf16[64,2048]{1,0:T(8,128)(2,1)}, bf16[64,2048]{1,0:T(8,128)(2,1)S(1)}, u32[]{:S(2)}, u32[]{:S(2)}) collective-permute-start(bf16[64,2048]{1,0:T(8,128)(2,1)} %get-tuple-element.15), channel_id=1, source_target_pairs={{0,96},{8,104},{1,97},{9,105},{16,112},{24,120},{17,113},{25,121},... | collective-permute-start | bytes 786440 | tf_op jit(solution)/shard_map/ppermute | solution.py:37
  121.2 12.3 %collective-permute-start.14 = (bf16[64,2048]{1,0:T(8,128)(2,1)}, bf16[64,2048]{1,0:T(8,128)(2,1)S(1)}, u32[]{:S(2)}, u32[]{:S(2)}) collective-permute-start(bf16[64,2048]{1,0:T(8,128)(2,1)} %get-tuple-element.15), channel_id=1, source_target_pairs={{0,64},{8,72},{1,65},{9,73},{16,80},{24,88},{17,81},{25,89},{32,96... | collective-permute-start | bytes 786440 | tf_op jit(solution)/shard_map/ppermute | solution.py:37
  133.5 71.8 %copy-start.2 = (bf16[256,2048]{1,0:T(8,128)(2,1)}, bf16[256,2048]{1,0:T(8,128)(2,1)S(1)}, u32[]{:S(2)}) copy-start(bf16[256,2048]{1,0:T(8,128)(2,1)S(1)} %constant_dynamic-update-slice_fusion.11.refs_3_) | copy-start | bytes 3145732
  133.5 49.5 %collective-permute-start.25 = (bf16[256,2048]{1,0:T(8,128)(2,1)S(1)}, bf16[256,2048]{1,0:T(8,128)(2,1)S(1)}, u32[]{:S(2)}, u32[]{:S(2)}) collective-permute-start(bf16[256,2048]{1,0:T(8,128)(2,1)S(1)} %constant_dynamic-update-slice_fusion.11.refs_3_), channel_id=1, source_target_pairs={{0,16},{8,24},{1,17},{9,25},{16,0},{24,8},{17,1},{25,9},{32,48},{4... | collective-permute-start | bytes 3145736 | tf_op jit(solution)/shard_map/ppermute | solution.py:37
  136.8 28.3 %collective-permute-start.16 = (bf16[64,2048]{1,0:T(8,128)(2,1)}, bf16[64,2048]{1,0:T(8,128)(2,1)S(1)}, u32[]{:S(2)}, u32[]{:S(2)}) collective-permute-start(bf16[64,2048]{1,0:T(8,128)(2,1)} %get-tuple-element.16), channel_id=1, source_target_pairs={{0,16},{8,24},{1,17},{9,25},{16,0},{24,8},{17,1},{25,9},{32,48},{4... | collective-permute-start | bytes 786440 | tf_op jit(solution)/shard_map/ppermute | solution.py:37
  165.1 40.2 %copy-start.3 = (bf16[128,2048]{1,0:T(8,128)(2,1)}, bf16[128,2048]{1,0:T(8,128)(2,1)S(1)}, u32[]{:S(2)}) copy-start(bf16[128,2048]{1,0:T(8,128)(2,1)S(1)} %constant_dynamic-update-slice_fusion.15.refs_4_) | copy-start | bytes 1572868
  165.1 13.7 %collective-permute-start.23 = (bf16[128,2048]{1,0:T(8,128)(2,1)S(1)}, bf16[128,2048]{1,0:T(8,128)(2,1)S(1)}, u32[]{:S(2)}, u32[]{:S(2)}) collective-permute-start(bf16[128,2048]{1,0:T(8,128)(2,1)S(1)} %constant_dynamic-update-slice_fusion.15.refs_4_), channel_id=1, source_target_pairs={{0,64},{8,72},{1,65},{9,73},{16,80},{24,88},{17,81},{25,89},{32,96... | collective-permute-start | bytes 1572872 | tf_op jit(solution)/shard_map/ppermute | solution.py:37
  166.0 24.4 %collective-permute-start.20 = (bf16[128,2048]{1,0:T(8,128)(2,1)S(1)}, bf16[128,2048]{1,0:T(8,128)(2,1)}, u32[]{:S(2)}, u32[]{:S(2)}) collective-permute-start(bf16[128,2048]{1,0:T(8,128)(2,1)S(1)} %constant_dynamic-update-slice_fusion.15.refs_4_), channel_id=1, source_target_pairs={{0,96},{8,104},{1,97},{9,105},{16,112},{24,120},{17,113},{25,121},... | collective-permute-start | bytes 1572872 | tf_op jit(solution)/shard_map/ppermute | solution.py:37
  168.2 37.2 %collective-permute-start.18 = (bf16[256,2048]{1,0:T(8,128)(2,1)S(1)}, bf16[256,2048]{1,0:T(8,128)(2,1)}, u32[]{:S(2)}, u32[]{:S(2)}) collective-permute-start(bf16[256,2048]{1,0:T(8,128)(2,1)S(1)} %constant_dynamic-update-slice_fusion.11.refs_3_), channel_id=1, source_target_pairs={{0,8},{8,0},{1,9},{9,1},{16,24},{24,16},{17,25},{25,17},{32,40},{4... | collective-permute-start | bytes 3145736 | tf_op jit(solution)/shard_map/ppermute | solution.py:42
  170.2 21.9 %collective-permute-start.19 = (bf16[128,2048]{1,0:T(8,128)(2,1)S(1)}, bf16[128,2048]{1,0:T(8,128)(2,1)}, u32[]{:S(2)}, u32[]{:S(2)}) collective-permute-start(bf16[128,2048]{1,0:T(8,128)(2,1)S(1)} %constant_dynamic-update-slice_fusion.15.refs_4_), channel_id=1, source_target_pairs={{0,32},{8,40},{1,33},{9,41},{16,48},{24,56},{17,49},{25,57},{32,64... | collective-permute-start | bytes 1572872 | tf_op jit(solution)/shard_map/ppermute | solution.py:37
  178.8 26.5 %copy-start.5 = (bf16[128,2048]{1,0:T(8,128)(2,1)}, bf16[128,2048]{1,0:T(8,128)(2,1)S(1)}, u32[]{:S(2)}) copy-start(bf16[128,2048]{1,0:T(8,128)(2,1)S(1)} %collective-permute-done.23.refs_8_) | copy-start | bytes 1572868
  178.8 13.6 %collective-permute-start.17 = (bf16[128,2048]{1,0:T(8,128)(2,1)S(1)}, bf16[128,2048]{1,0:T(8,128)(2,1)S(1)}, u32[]{:S(2)}, u32[]{:S(2)}) collective-permute-start(bf16[128,2048]{1,0:T(8,128)(2,1)S(1)} %constant_dynamic-update-slice_fusion.15.refs_4_), channel_id=1, source_target_pairs={{0,8},{8,0},{1,9},{9,1},{16,24},{24,16},{17,25},{25,17},{32,40},{4... | collective-permute-start | bytes 1572872 | tf_op jit(solution)/shard_map/ppermute | solution.py:42
  183.0 22.3 %copy-start.4 = (bf16[256,2048]{1,0:T(8,128)(2,1)}, bf16[256,2048]{1,0:T(8,128)(2,1)S(1)}, u32[]{:S(2)}) copy-start(bf16[256,2048]{1,0:T(8,128)(2,1)S(1)} %collective-permute-done.25.refs_10_) | copy-start | bytes 3145732
  183.0 32.2 %collective-permute-start.26 = (bf16[256,2048]{1,0:T(8,128)(2,1)S(1)}, bf16[256,2048]{1,0:T(8,128)(2,1)}, u32[]{:S(2)}, u32[]{:S(2)}) collective-permute-start(bf16[256,2048]{1,0:T(8,128)(2,1)S(1)} %collective-permute-done.25.refs_10_), channel_id=1, source_target_pairs={{0,8},{8,0},{1,9},{9,1},{16,24},{24,16},{17,25},{25,17},{32,40},{4... | collective-permute-start | bytes 3145736 | tf_op jit(solution)/shard_map/ppermute | solution.py:42
  190.4 24.8 %collective-permute-start.24 = (bf16[128,2048]{1,0:T(8,128)(2,1)S(1)}, bf16[128,2048]{1,0:T(8,128)(2,1)}, u32[]{:S(2)}, u32[]{:S(2)}) collective-permute-start(bf16[128,2048]{1,0:T(8,128)(2,1)S(1)} %collective-permute-done.23.refs_8_), channel_id=1, source_target_pairs={{0,8},{8,0},{1,9},{9,1},{16,24},{24,16},{17,25},{25,17},{32,40},{4... | collective-permute-start | bytes 1572872 | tf_op jit(solution)/shard_map/ppermute | solution.py:42
  192.1 23.1 %collective-permute-start.22 = (bf16[128,2048]{1,0:T(8,128)(2,1)}, bf16[128,2048]{1,0:T(8,128)(2,1)}, u32[]{:S(2)}, u32[]{:S(2)}) collective-permute-start(bf16[128,2048]{1,0:T(8,128)(2,1)} %collective-permute-done.20.refs_5_), channel_id=1, source_target_pairs={{0,8},{8,0},{1,9},{9,1},{16,24},{24,16},{17,25},{25,17},{32,40},{4... | collective-permute-start | bytes 1572872 | tf_op jit(solution)/shard_map/ppermute | solution.py:42
  192.4 0.8 copy-start.6
  193.2 22.0 %collective-permute-start.21 = (bf16[128,2048]{1,0:T(8,128)(2,1)}, bf16[128,2048]{1,0:T(8,128)(2,1)}, u32[]{:S(2)}, u32[]{:S(2)}) collective-permute-start(bf16[128,2048]{1,0:T(8,128)(2,1)} %collective-permute-done.19.refs_4_), channel_id=1, source_target_pairs={{0,8},{8,0},{1,9},{9,1},{16,24},{24,16},{17,25},{25,17},{32,40},{4... | collective-permute-start | bytes 1572872 | tf_op jit(solution)/shard_map/ppermute | solution.py:42
where the time goes:
time: 229 us; the launch traced here: 228 us
  waiting for transfers between devices  106 us (46%)
  Pallas kernels  52.7 us (23%)
  starting transfers between devices  48.9 us (21%)
  local copies, waits for them, and re-layouts  15.1 us (7%)
  matrix products  3.06 us (1%)
  between operations  2.88 us (1%)
    ppermute x17, waiting for transfers between devices, shifted(): return lax.ppermute(value, AXES, pairs)  106 us
    ppermute x17, starting transfers between devices, shifted(): return lax.ppermute(value, AXES, pairs)  28.5 us
    pallas_call x2, Pallas kernels, paired(): pl.pallas_call(body, in_specs=[hbm, vmem, vmem] + [hbm] * (len(parts) + l...  22.7 us
    pallas_call x2, Pallas kernels, fit(): pl.pallas_call(body, in_specs=[pl.BlockSpec(memory_space=pltpu.SMEM)] + [...  18.7 us
    ppermute x10, starting transfers between devices, swapped(): return lax.ppermute(value, AXES, pairs)  12.1 us
    pallas_call x1, Pallas kernels, transformed(): pl.pallas_call(half_kernel, in_specs=[pl.BlockSpec(memory_space=pltpu.SME...  11.2 us
    all_to_all x1, starting transfers between devices, whole(): owned = lax.all_to_all(sent, AXES, split_axis=0, concat_axis=0, tiled=True)  8.39 us
    unnamed x31, local copies, waits for them, and re-layouts  7.72 us
  transfers between devices with their start and end apart: 28, of which 8 were waited for; matrix products, arithmetic and copies ran while one was open for 7% of the time, Pallas kernels for 14%

commit v1 on v0

--- a/solution.py
+++ b/solution.py
@@ -94,7 +94,16 @@
     return mine + [swapped(part) for part in mine]
 
 
-def half_kernel(order_ref, owner_ref, ints_ref, coeff_ref, out_ref, scratch, pick_ref):
+def half_kernel(order_ref, owner_ref, ints_ref, coeff_ref, part_ref, own_ref, *scratches):
+    ints, scratch, pick_ref, part, own, in_sems, out_sems = scratches
+    takes = [
+        pltpu.make_async_copy(
+            ints_ref.at[pl.ds(c * 4, 4)], ints.at[pl.ds(c * 4, 4)], in_sems.at[c]
+        )
+        for c in range(4)
+    ]
+    for take in takes:
+        take.start()
     owners = jnp.broadcast_to(owner_ref[...].astype(jnp.float32), (128, 128)).T
     orbital = lax.broadcasted_iota(jnp.int32, (128, 128), 1).astype(jnp.float32)
     pick_ref[0:128, :] = jnp.where(owners == orbital, 1.0, 0.0)
@@ -103,9 +112,10 @@
         pick_ref[128 + 8 * s:136 + 8 * s, :] = pick_ref[pl.ds(first, 8), :]
     pick = pick_ref[...].astype(jnp.bfloat16)
 
-    def select(c, carry):
+    for c in range(4):
+        takes[c].wait()
         half = jnp.dot(
-            ints_ref[pl.ds(c * 4, 4)].reshape(512, 640),
+            ints[c * 4:c * 4 + 4].reshape(512, 640),
             coeff_ref[...],
             preferred_element_type=jnp.float32,
         ).astype(jnp.bfloat16)
@@ -116,27 +126,9 @@
             for t in range(4):
                 at = pl.ds(c * 4 + i, 160, stride=16)
                 scratch.at[t][at, :] = rows[:, t * 128:t * 128 + 128]
-        return carry
-
-    lax.fori_loop(0, 4, select, 0)
+
     lane = lax.broadcasted_iota(jnp.int32, (16, 128), 1)
     low = lane < 64
-
-    def emit(group, carry):
-        first_row = pl.multiple_of(group * 128, 128)
-        to = pl.multiple_of(group * 8, 8)
-        for t in range(4):
-            for j in range(4):
-                even = scratch[t, pl.ds(first_row + 32 * j, 16), :]
-                odd = scratch[t, pl.ds(first_row + 32 * j + 16, 16), :]
-                first = jnp.where(low, even, pltpu.roll(odd, 64, 1))
-                second = jnp.where(low, pltpu.roll(even, 64, 1), odd)
-                at = slice(j * 128, j * 128 + 128)
-                out_ref[to + 2 * t, :, at] = first.astype(out_ref.dtype)
-                out_ref[to + 2 * t + 1, :, at] = second.astype(out_ref.dtype)
-        return carry
-
-    lax.fori_loop(0, 16, emit, 0)
 
     def emit_partner(v, carry):
         for t in range(4):
@@ -150,31 +142,67 @@
                     by = (s - g) * 32 % 128
                     tile = pltpu.roll(tiles[s], by, 1) if by else tiles[s]
                     total = jnp.where(lane // 32 == s, tile, total)
-                out_ref[(t * 4 + g) * 8 + v, :, 512:640] = total.astype(out_ref.dtype)
+                part[(t * 4 + g) * 8 + v] = total.astype(part.dtype)
         return carry
 
     lax.fori_loop(0, 8, emit_partner, 0)
+    send_part = pltpu.make_async_copy(part, part_ref, out_sems.at[0])
+    send_part.start()
+
+    def emit(group, carry):
+        first_row = pl.multiple_of(group * 128, 128)
+        to = pl.multiple_of(group * 8, 8)
+        for t in range(4):
+            for j in range(4):
+                even = scratch[t, pl.ds(first_row + 32 * j, 16), :]
+                odd = scratch[t, pl.ds(first_row + 32 * j + 16, 16), :]
+                first = jnp.where(low, even, pltpu.roll(odd, 64, 1))
+                second = jnp.where(low, pltpu.roll(even, 64, 1), odd)
+                at = slice(j * 128, j * 128 + 128)
+                own[to + 2 * t, :, at] = first.astype(own.dtype)
+                own[to + 2 * t + 1, :, at] = second.astype(own.dtype)
+        return carry
+
+    sends = [
+        pltpu.make_async_copy(
+            own.at[pl.ds(h * 64, 64)], own_ref.at[pl.ds(h * 64, 64)], out_sems.at[1 + h]
+        )
+        for h in range(2)
+    ]
+    for h in range(2):
+        lax.fori_loop(8 * h, 8 * h + 8, emit, 0)
+        sends[h].start()
+    send_part.wait()
+    for send in sends:
+        send.wait()
 
 
 def transformed(pair_order, owner_table, three_index, virt_coeff):
-    vmem = pl.BlockSpec(memory_space=pltpu.VMEM)
+    vmem, hbm = pl.BlockSpec(memory_space=pltpu.VMEM), pl.BlockSpec(memory_space=pl.ANY)
+    part = jax.ShapeDtypeStruct((128, 16, 128), jnp.bfloat16)
+    own = jax.ShapeDtypeStruct((128, 16, 512), jnp.bfloat16)
     return pl.pallas_call(
         half_kernel,
-        in_specs=[pl.BlockSpec(memory_space=pltpu.SMEM)] + [vmem] * 3,
-        out_specs=vmem,
-        out_shape=jax.ShapeDtypeStruct((128, 16, 640), jnp.bfloat16),
+        in_specs=[pl.BlockSpec(memory_space=pltpu.SMEM), vmem, hbm, vmem],
+        out_specs=[hbm, hbm],
+        out_shape=[part, own],
         scratch_shapes=[
+            pltpu.VMEM((16, 128, 640), jnp.bfloat16),
             pltpu.VMEM((4, 160 * 16, 128), jnp.float32),
             pltpu.VMEM((160, 128), jnp.float32),
+            pltpu.VMEM(part.shape, part.dtype),
+            pltpu.VMEM(own.shape, own.dtype),
+            pltpu.SemaphoreType.DMA((4,)),
+            pltpu.SemaphoreType.DMA((3,)),
         ],
         name="half",
     )(pair_order, owner_table.reshape(1, 128), three_index, virt_coeff)
 
 
-def fit_kernel(table_ref, rows_ref, *refs, first, width, outs):
+def fit_kernel(table_ref, rows_ref, *refs, width, outs):
     parts, out_refs = refs[:8], refs[8:8 + outs]
     rows, metric, sems, row_sem = refs[8 + outs:]
-    take = pltpu.make_async_copy(rows_ref.at[:, pl.ds(first, width)], rows, row_sem)
+    take = pltpu.make_async_copy(rows_ref, rows, row_sem)
     take.start()
     for buf in range(8):
 
@@ -202,12 +230,13 @@
             out_refs[i][:, at] = fitted[i * each:i * each + each]
 
 
-def fit(table, owned, parts, first, width, outs):
+def fit(table, owned, parts, outs):
+    width = owned.shape[1]
     vmem = pl.BlockSpec(memory_space=pltpu.VMEM)
     shape = jax.ShapeDtypeStruct((width // outs, 2048), jnp.bfloat16)
 
     def body(*refs):
-        fit_kernel(*refs, first=first, width=width, outs=outs)
+        fit_kernel(*refs, width=width, outs=outs)
 
     return pl.pallas_call(
         body,
@@ -313,16 +342,17 @@
 def whole(three_index, virt_coeff, metric_root, owner_table, pair_order, occ_energy, vir_energy):
     me = lax.axis_index("occ") * 8 + lax.axis_index("vir")
     metric_parts = gathered_metric(metric_root)
-    sent = transformed(pair_order, owner_table, three_index, virt_coeff)
-    owned = lax.all_to_all(sent, AXES, split_axis=0, concat_axis=0, tiled=True)
-    owned = owned.reshape(2048, 640)
+    part, own = transformed(pair_order, owner_table, three_index, virt_coeff)
+    part = lax.all_to_all(part, AXES, split_axis=0, concat_axis=0, tiled=True)
+    own = lax.all_to_all(own, AXES, split_axis=0, concat_axis=0, tiled=True)
+    part, own = part.reshape(2048, 128), own.reshape(2048, 512)
 
     row, col = energies(me, owner_table, pair_order, occ_energy, vir_energy)
     table = lax.dynamic_slice_in_dim(jnp.asarray(metric_table()), me, 1, 0).reshape(128)
-    owned, row, col, table = lax.optimization_barrier((owned, row, col, table))
-
-    early, late = fit(table, owned, metric_parts, 512, 128, 2)
-    (own,) = fit(table, owned, metric_parts, 0, 512, 1)
+    part, row, col, table = lax.optimization_barrier((part, row, col, table))
+
+    early, late = fit(table, part, metric_parts, 2)
+    (own,) = fit(table, own, metric_parts, 1)
 
     ydim, zdim = ("y", "y"), ("z", "z")
     early = jnp.concatenate([early, shifted(early, zdim, 2)], axis=0)

time: 229 us -> 227 us (level)
  starting transfers between devices: 48.9 us -> 68 us
  waiting for transfers between devices: 106 us -> 90 us
  local copies, waits for them, and re-layouts: 15.1 us -> 10.2 us
    ppermute x17, waiting for transfers between devices: 106 us -> 86.5 us  [shifted(): return lax.ppermute(value, AXES, pairs)]
    ppermute x10, starting transfers between devices: 12.1 us -> 23.6 us  [swapped(): return lax.ppermute(value, AXES, pairs)]
    all_to_all x1 -> x2, starting transfers between devices: 8.39 us -> 15.8 us  [the longest x1 8.78 us: whole(): part = lax.all_to_all(part, AXES, split_axis=0, concat_axis=0, tiled=True)]
    unnamed x31 -> x35, local copies, waits for them, and re-layouts: 7.72 us -> 4.2 us
    all_to_all x1 -> x2, waiting for transfers between devices: 0.01 us -> 3.43 us  [the longest x1 3.43 us: whole(): part = lax.all_to_all(part, AXES, split_axis=0, concat_axis=0, tiled=True)]
  transfers between devices with their start and end apart: 28 -> 29, of which waited for: 8 -> 10; matrix products, arithmetic and copies ran while one was open for 7% -> 5% of each run, Pallas kernels for 14% -> 14%
where the time goes in v1:
time: 227 us
  waiting for transfers between devices  90 us (40%)
  starting transfers between devices  68 us (30%)
  Pallas kernels  52.4 us (23%)
  local copies, waits for them, and re-layouts  10.2 us (4%)
  matrix products  3.14 us (1%)
  between operations  3.08 us (1%)
    ppermute x17, waiting for transfers between devices, shifted(): return lax.ppermute(value, AXES, pairs)  86.5 us
    ppermute x17, starting transfers between devices, shifted(): return lax.ppermute(value, AXES, pairs)  28.6 us
    ppermute x10, starting transfers between devices, swapped(): return lax.ppermute(value, AXES, pairs)  23.6 us
    pallas_call x2, Pallas kernels, paired(): pl.pallas_call(body, in_specs=[hbm, vmem, vmem] + [hbm] * (len(parts) + l...  22.7 us
    pallas_call x2, Pallas kernels, fit(): pl.pallas_call(body, in_specs=[pl.BlockSpec(memory_space=pltpu.SMEM)] + [...  18.7 us
    pallas_call x1, Pallas kernels, transformed(): pl.pallas_call(half_kernel, in_specs=[pl.BlockSpec(memory_space=pltpu.SME...  11 us
    all_to_all x1, starting transfers between devices, whole(): part = lax.all_to_all(part, AXES, split_axis=0, concat_axis=0, tiled=True)  8.78 us
    all_to_all x1, starting transfers between devices, whole(): own = lax.all_to_all(own, AXES, split_axis=0, concat_axis=0, tiled=True)  7.01 us
  transfers between devices with their start and end apart: 29, of which 10 were waited for; matrix products, arithmetic and copies ran while one was open for 5% of the time, Pallas kernels for 14%

profile of v1, /device:TPU:1, one launch (start us, length us, event | category | flops | bytes accessed | tf_op | source)
XLA Modules:
  0.0 226.8 jit_solution(13933051121636216310)
XLA Ops:
  0.0 3.7 %collective-permute-start.1 = (bf16[16,2048]{1,0:T(8,128)(2,1)}, bf16[16,2048]{1,0:T(8,128)(2,1)S(1)}, u32[]{:S(2)}, u32[]{:S(2)}) collective-permute-start(bf16[16,2048]{1,0:T(8,128)(2,1)} %param.12), channel_id=1, source_target_pairs={{0,16},{8,72},{1,17},{9,73},{16,0},{24,88},{17,1},{25,89},{32,48},... | collective-permute-start | bytes 196616 | tf_op jit(solution)/shard_map/ppermute | solution.py:37
  3.7 0.4 collective-permute-start
  4.1 2.3 %collective-permute-start.2 = (bf16[16,2048]{1,0:T(8,128)(2,1)}, bf16[16,2048]{1,0:T(8,128)(2,1)S(1)}, u32[]{:S(2)}, u32[]{:S(2)}) collective-permute-start(bf16[16,2048]{1,0:T(8,128)(2,1)} %param.12), channel_id=1, source_target_pairs={{0,17},{8,104},{1,0},{9,105},{16,1},{24,120},{17,16},{25,121},{32,... | collective-permute-start | bytes 196616 | tf_op jit(solution)/shard_map/ppermute | solution.py:37
  6.4 0.9 constant_dynamic-update-slice_fusion.3
  7.3 1.0 collective-permute-done
  8.3 1.7 collective-permute-start.3
  10.1 3.3 %collective-permute-start.4 = (bf16[64,2048]{1,0:T(8,128)(2,1)S(1)}, bf16[64,2048]{1,0:T(8,128)(2,1)S(1)}, u32[]{:S(2)}, u32[]{:S(2)}) collective-permute-start(bf16[64,2048]{1,0:T(8,128)(2,1)S(1)} %get-tuple-element.21), channel_id=1, source_target_pairs={{0,4},{8,24},{1,5},{9,25},{16,20},{24,8},{17,21},{25,9},{32,36},{4... | collective-permute-start | bytes 786440 | tf_op jit(solution)/shard_map/ppermute | solution.py:37
  13.4 0.7 collective-permute-start.5
  14.1 2.1 collective-permute-done.3
  16.3 3.9 %collective-permute-done.4 = bf16[64,2048]{1,0:T(8,128)(2,1)S(1)} collective-permute-done((bf16[64,2048]{1,0:T(8,128)(2,1)S(1)}, bf16[64,2048]{1,0:T(8,128)(2,1)S(1)}, u32[]{:S(2)}, u32[]{:S(2)}) %collective-permute-start.4) | collective-permute-done | bytes 262176 | tf_op jit(solution)/shard_map/ppermute | solution.py:37
  20.3 0.0 copy-start.9
  20.3 2.3 collective-permute-start.8
  22.6 0.5 collective-permute-start.7
  23.1 0.6 collective-permute-start.6
  23.7 4.2 %collective-permute-start.9 = (bf16[256,2048]{1,0:T(8,128)(2,1)S(1)}, bf16[256,2048]{1,0:T(8,128)(2,1)}, u32[]{:S(2)}, u32[]{:S(2)}) collective-permute-start(bf16[256,2048]{1,0:T(8,128)(2,1)S(1)} %constant_dynamic-update-slice_fusion.4.refs_2_), channel_id=1, source_target_pairs={{0,8},{8,0},{1,9},{9,1},{16,24},{24,16},{17,25},{25,17},{32,40},{4... | collective-permute-start | bytes 3145736 | tf_op jit(solution)/shard_map/ppermute | solution.py:42
  27.9 17.6 %collective-permute-done.8.refs_5_ = bf16[256,2048]{1,0:T(8,128)(2,1)S(1)} collective-permute-done((bf16[256,2048]{1,0:T(8,128)(2,1)S(1)}, bf16[256,2048]{1,0:T(8,128)(2,1)S(1)}, u32[]{:S(2)}, u32[]{:S(2)}) %collective-permute-start.8) | collective-permute-done | bytes 1048608 | tf_op jit(solution)/shard_map/ppermute | solution.py:37
  45.5 3.8 %collective-permute-start.12 = (bf16[256,2048]{1,0:T(8,128)(2,1)S(1)}, bf16[256,2048]{1,0:T(8,128)(2,1)}, u32[]{:S(2)}, u32[]{:S(2)}) collective-permute-start(bf16[256,2048]{1,0:T(8,128)(2,1)S(1)} %collective-permute-done.8.refs_5_), channel_id=1, source_target_pairs={{0,8},{8,0},{1,9},{9,1},{16,24},{24,16},{17,25},{25,17},{32,40},{4... | collective-permute-start | bytes 3145736 | tf_op jit(solution)/shard_map/ppermute | solution.py:42
  49.3 0.1 collective-permute-start.11
  49.4 4.0 %collective-permute-start.10 = (bf16[256,2048]{1,0:T(8,128)(2,1)}, bf16[256,2048]{1,0:T(8,128)(2,1)}, u32[]{:S(2)}, u32[]{:S(2)}) collective-permute-start(bf16[256,2048]{1,0:T(8,128)(2,1)} %collective-permute-done.6.refs_3_), channel_id=1, source_target_pairs={{0,8},{8,0},{1,9},{9,1},{16,24},{24,16},{17,25},{25,17},{32,40},{4... | collective-permute-start | bytes 3145736 | tf_op jit(solution)/shard_map/ppermute | solution.py:42
  53.4 11.0 %half.1 = (bf16[128,16,128]{2,1,0:T(8,128)(2,1)}, bf16[128,16,512]{2,1,0:T(8,128)(2,1)}) custom-call(s32[4]{0:T(128)} %order_ref.1, s32[1,128]{1,0:T(1,128)} %bitcast.23, bf16[16,128,640]{2,1,0:T(8,128)(2,1)} %ints_ref.1, bf16[640,512]{1,0:T(8,128)(2,1)} %coeff_ref.1), custom_call_target="tpu_custom_call" | custom-call | tf_op jit(solution)/shard_map/half/pallas_call | solution.py:184
  64.4 8.8 %all-to-all-start = ((bf16[128,16,128]{2,1,0:T(8,128)(2,1)}), bf16[128,16,128]{2,1,0:T(8,128)(2,1)}, u32[]{:S(2)}, u32[]{:S(2)}) async-start(bf16[128,16,128]{2,1,0:T(8,128)(2,1)} %get-tuple-element.13), calls=%async_computation | async-start | bytes 1048576 | tf_op jit(solution)/shard_map/all_to_all | solution.py:346
  73.2 0.7 fusion.5
  76.4 0.1 reshape.54
  76.5 0.1 dynamic_slice.25
  76.6 0.2 convolution_bitcast_fusion.1
  76.8 0.1 dynamic_slice.24
  76.9 0.1 broadcast_subtract_fusion
  77.0 0.1 sub.36
  77.0 0.7 constant_dynamic-slice_fusion
  77.8 0.6 reshape.56.refs_0_
  78.4 0.7 fusion.4
  79.0 0.7 dynamic-slice_bitcast_fusion
  79.7 2.7 %convolution_bitcast_fusion = f32[64]{0:T(128)S(1)} fusion(f32[64,4]{1,0:T(8,128)S(1)} %copy-done.9, f32[1]{0:T(128)} %get-tuple-element.30, f32[1]{0:T(128)} %get-tuple-element.31, f32[1]{0:T(128)} %get-tuple-element.32, f32[1]{0:T(128)} %get-tuple-element.29), kind=kOutput, calls=%fused_computation.1 | convolution fusion | flops 3084 | bytes 1296 | tf_op jit(solution)/shard_map/dot_general | solution.py:338
  82.4 0.2 convolution_subtract_fusion
  82.7 0.1 copy.12
  82.8 0.1 reshape.55
  82.9 3.4 %all-to-all-done = bf16[128,16,128]{2,1,0:T(8,128)(2,1)} async-done(((bf16[128,16,128]{2,1,0:T(8,128)(2,1)}), bf16[128,16,128]{2,1,0:T(8,128)(2,1)}, u32[]{:S(2)}, u32[]{:S(2)}) %all-to-all-start) | async-done | bytes 524320 | tf_op jit(solution)/shard_map/all_to_all | solution.py:346
  86.3 0.9 broadcast_in_dim.2.refs_1_
  87.2 8.0 %fit_partner.1 = (bf16[64,2048]{1,0:T(8,128)(2,1)}, bf16[64,2048]{1,0:T(8,128)(2,1)}) custom-call(s32[128]{0:T(128)} %reshape.56.refs_0_, bf16[2048,128]{1,0:T(8,128)(2,1)} %bitcast.1.refs_1_, bf16[256,2048]{1,0:T(8,128)(2,1)} %copy-done.2, bf16[256,2048]{1,0:T(8,128)(2,1)} %collective-permute-done.6.refs_3_, bf16[256,2048]{1,0:T(8,128)(2,1)} %copy-done.4, ...), custom_call_target="tpu_custom_call" | custom-call | tf_op jit(solution)/shard_map/fit_partner/pallas_call | solution.py:241
  95.2 0.4 collective-permute-start.13
  95.6 2.3 %collective-permute-start.15 = (bf16[64,2048]{1,0:T(8,128)(2,1)}, bf16[64,2048]{1,0:T(8,128)(2,1)S(1)}, u32[]{:S(2)}, u32[]{:S(2)}) collective-permute-start(bf16[64,2048]{1,0:T(8,128)(2,1)} %get-tuple-element.19), channel_id=1, source_target_pairs={{0,96},{8,104},{1,97},{9,105},{16,112},{24,120},{17,113},{25,121},... | collective-permute-start | bytes 786440 | tf_op jit(solution)/shard_map/ppermute | solution.py:37
  97.9 1.0 constant_dynamic-update-slice_fusion.14
  99.0 5.5 %collective-permute-done.13 = bf16[64,2048]{1,0:T(8,128)(2,1)S(1)} collective-permute-done((bf16[64,2048]{1,0:T(8,128)(2,1)}, bf16[64,2048]{1,0:T(8,128)(2,1)S(1)}, u32[]{:S(2)}, u32[]{:S(2)}) %collective-permute-start.13) | collective-permute-done | bytes 262176 | tf_op jit(solution)/shard_map/ppermute | solution.py:37
  104.5 4.3 %collective-permute-done.14 = bf16[64,2048]{1,0:T(8,128)(2,1)S(1)} collective-permute-done((bf16[64,2048]{1,0:T(8,128)(2,1)}, bf16[64,2048]{1,0:T(8,128)(2,1)S(1)}, u32[]{:S(2)}, u32[]{:S(2)}) %collective-permute-start.14) | collective-permute-done | bytes 262176 | tf_op jit(solution)/shard_map/ppermute | solution.py:37
  108.9 3.4 %collective-permute-start.25 = (bf16[256,2048]{1,0:T(8,128)(2,1)S(1)}, bf16[256,2048]{1,0:T(8,128)(2,1)}, u32[]{:S(2)}, u32[]{:S(2)}) collective-permute-start(bf16[256,2048]{1,0:T(8,128)(2,1)S(1)} %constant_dynamic-update-slice_fusion.11.refs_3_), channel_id=1, source_target_pairs={{0,16},{8,24},{1,17},{9,25},{16,0},{24,8},{17,1},{25,9},{32,48},{4... | collective-permute-start | bytes 3145736 | tf_op jit(solution)/shard_map/ppermute | solution.py:37
  112.2 7.0 %all-to-all-start.1 = ((bf16[128,16,512]{2,1,0:T(8,128)(2,1)}), bf16[128,16,512]{2,1,0:T(8,128)(2,1)S(1)}, u32[]{:S(2)}, u32[]{:S(2)}) async-start(bf16[128,16,512]{2,1,0:T(8,128)(2,1)} %get-tuple-element.15), calls=%async_computation.1 | async-start | bytes 4194304 | tf_op jit(solution)/shard_map/all_to_all | solution.py:347
  119.3 3.3 %collective-permute-start.16 = (bf16[64,2048]{1,0:T(8,128)(2,1)S(1)}, bf16[64,2048]{1,0:T(8,128)(2,1)S(1)}, u32[]{:S(2)}, u32[]{:S(2)}) collective-permute-start(bf16[64,2048]{1,0:T(8,128)(2,1)S(1)} %copy-done.8), channel_id=1, source_target_pairs={{0,16},{8,24},{1,17},{9,25},{16,0},{24,8},{17,1},{25,9},{32,48},{4... | collective-permute-start | bytes 786440 | tf_op jit(solution)/shard_map/ppermute | solution.py:37
  122.6 39.8 %collective-permute-done.16 = bf16[64,2048]{1,0:T(8,128)(2,1)S(1)} collective-permute-done((bf16[64,2048]{1,0:T(8,128)(2,1)S(1)}, bf16[64,2048]{1,0:T(8,128)(2,1)S(1)}, u32[]{:S(2)}, u32[]{:S(2)}) %collective-permute-start.16) | collective-permute-done | bytes 262176 | tf_op jit(solution)/shard_map/ppermute | solution.py:37
  162.5 1.3 collective-permute-start.23
  163.7 2.4 %collective-permute-start.20 = (bf16[128,2048]{1,0:T(8,128)(2,1)S(1)}, bf16[128,2048]{1,0:T(8,128)(2,1)}, u32[]{:S(2)}, u32[]{:S(2)}) collective-permute-start(bf16[128,2048]{1,0:T(8,128)(2,1)S(1)} %constant_dynamic-update-slice_fusion.15.refs_4_), channel_id=1, source_target_pairs={{0,96},{8,104},{1,97},{9,105},{16,112},{24,120},{17,113},{25,121},... | collective-permute-start | bytes 1572872 | tf_op jit(solution)/shard_map/ppermute | solution.py:37
  166.1 3.0 %collective-permute-start.18 = (bf16[256,2048]{1,0:T(8,128)(2,1)S(1)}, bf16[256,2048]{1,0:T(8,128)(2,1)}, u32[]{:S(2)}, u32[]{:S(2)}) collective-permute-start(bf16[256,2048]{1,0:T(8,128)(2,1)S(1)} %constant_dynamic-update-slice_fusion.11.refs_3_), channel_id=1, source_target_pairs={{0,8},{8,0},{1,9},{9,1},{16,24},{24,16},{17,25},{25,17},{32,40},{4... | collective-permute-start | bytes 3145736 | tf_op jit(solution)/shard_map/ppermute | solution.py:42
  169.1 6.1 %collective-permute-done.23.refs_8_ = bf16[128,2048]{1,0:T(8,128)(2,1)} collective-permute-done((bf16[128,2048]{1,0:T(8,128)(2,1)S(1)}, bf16[128,2048]{1,0:T(8,128)(2,1)}, u32[]{:S(2)}, u32[]{:S(2)}) %collective-permute-start.23) | collective-permute-done | bytes 524320 | tf_op jit(solution)/shard_map/ppermute | solution.py:37
  175.2 6.3 %collective-permute-start.17 = (bf16[128,2048]{1,0:T(8,128)(2,1)S(1)}, bf16[128,2048]{1,0:T(8,128)(2,1)S(1)}, u32[]{:S(2)}, u32[]{:S(2)}) collective-permute-start(bf16[128,2048]{1,0:T(8,128)(2,1)S(1)} %constant_dynamic-update-slice_fusion.15.refs_4_), channel_id=1, source_target_pairs={{0,8},{8,0},{1,9},{9,1},{16,24},{24,16},{17,25},{25,17},{32,40},{4... | collective-permute-start | bytes 1572872 | tf_op jit(solution)/shard_map/ppermute | solution.py:42
  181.5 6.1 %collective-permute-done.20.refs_5_ = bf16[128,2048]{1,0:T(8,128)(2,1)} collective-permute-done((bf16[128,2048]{1,0:T(8,128)(2,1)S(1)}, bf16[128,2048]{1,0:T(8,128)(2,1)}, u32[]{:S(2)}, u32[]{:S(2)}) %collective-permute-start.20) | collective-permute-done | bytes 524320 | tf_op jit(solution)/shard_map/ppermute | solution.py:37
  187.6 1.7 collective-permute-start.24
  189.3 0.4 collective-permute-start.22
  189.7 0.8 copy-done.7
  190.5 0.1 collective-permute-start.21
  190.6 0.6 slice.23.refs_2_
  191.2 0.6 slice.22.refs_2_
  191.8 1.3 copy-done.1
  193.1 10.7 %fit_own.1.refs_0_ = bf16[512,2048]{1,0:T(8,128)(2,1)} custom-call(s32[128]{0:T(128)} %reshape.56.refs_0_, bf16[2048,512]{1,0:T(8,128)(2,1)} %bitcast.22, bf16[256,2048]{1,0:T(8,128)(2,1)} %copy-done.2, bf16[256,2048]{1,0:T(8,128)(2,1)} %collective-permute-done.6.refs_3_, bf16[256,2048]{1,0:T(8,128)(2,1)} %copy-done.4, bf16[256,2048]{1,0:T(8,128)(2,1)} %copy-done.3, ...), custom_call_target="tpu_custom_call" | custom-call | tf_op jit(solution)/shard_map/fit_own/pallas_call | solution.py:241
  203.9 9.8 %pair.1.refs_3_ = f32[512,2048]{1,0:T(8,128)} custom-call(bf16[512,2048]{1,0:T(8,128)(2,1)} %fit_own.1.refs_0_, f32[512,128]{1,0:T(8,128)} %broadcast_in_dim.2.refs_1_, f32[1,768]{1,0:T(1,128)} %slice.23.refs_2_, bf16[256,2048]{1,0:T(8,128)(2,1)} %copy-done.5, bf16[128,2048]{1,0:T(8,128)(2,1)} %copy-done.6, bf16[128,2048]{1,0:T(8,128)(2,1)} %copy-done.7, ...), custom_call_target="tpu_custom_call" | custom-call | tf_op jit(solution)/shard_map/pair/pallas_call | solution.py:307
  213.7 12.9 %pair_more.1 = f32[512,2048]{1,0:T(8,128)} custom-call(bf16[512,2048]{1,0:T(8,128)(2,1)} %fit_own.1.refs_0_, f32[512,128]{1,0:T(8,128)} %broadcast_in_dim.2.refs_1_, f32[1,1280]{1,0:T(1,128)} %slice.22.refs_2_, f32[512,2048]{1,0:T(8,128)} %pair.1.refs_3_, bf16[128,2048]{1,0:T(8,128)(2,1)} %collective-permute-done.19.refs_4_, ...), custom_call_target="tpu_custom_call" | custom-call | tf_op jit(solution)/shard_map/pair_more/pallas_call | solution.py:307
  (56 shorter events, 0.3 us)
Async XLA Ops:
  0.0 76.6 %copy-start = (f32[128]{0:T(128)S(1)}, f32[128]{0:T(128)}, u32[]{:S(2)}) copy-start(f32[128]{0:T(128)} %param.15) | copy-start | bytes 1540
  0.0 8.3 %collective-permute-start.1 = (bf16[16,2048]{1,0:T(8,128)(2,1)}, bf16[16,2048]{1,0:T(8,128)(2,1)S(1)}, u32[]{:S(2)}, u32[]{:S(2)}) collective-permute-start(bf16[16,2048]{1,0:T(8,128)(2,1)} %param.12), channel_id=1, source_target_pairs={{0,16},{8,72},{1,17},{9,73},{16,0},{24,88},{17,1},{25,89},{32,48},... | collective-permute-start | bytes 196616 | tf_op jit(solution)/shard_map/ppermute | solution.py:37
  3.7 4.5 %collective-permute-start = (bf16[16,2048]{1,0:T(8,128)(2,1)}, bf16[16,2048]{1,0:T(8,128)(2,1)S(1)}, u32[]{:S(2)}, u32[]{:S(2)}) collective-permute-start(bf16[16,2048]{1,0:T(8,128)(2,1)} %param.12), channel_id=1, source_target_pairs={{0,1},{8,40},{1,16},{9,41},{16,17},{24,56},{17,0},{25,57},{32,33},... | collective-permute-start | bytes 196616 | tf_op jit(solution)/shard_map/ppermute | solution.py:37
  4.1 4.2 %collective-permute-start.2 = (bf16[16,2048]{1,0:T(8,128)(2,1)}, bf16[16,2048]{1,0:T(8,128)(2,1)S(1)}, u32[]{:S(2)}, u32[]{:S(2)}) collective-permute-start(bf16[16,2048]{1,0:T(8,128)(2,1)} %param.12), channel_id=1, source_target_pairs={{0,17},{8,104},{1,0},{9,105},{16,1},{24,120},{17,16},{25,121},{32,... | collective-permute-start | bytes 196616 | tf_op jit(solution)/shard_map/ppermute | solution.py:37
  8.3 7.9 %collective-permute-start.3 = (bf16[64,2048]{1,0:T(8,128)(2,1)S(1)}, bf16[64,2048]{1,0:T(8,128)(2,1)S(1)}, u32[]{:S(2)}, u32[]{:S(2)}) collective-permute-start(bf16[64,2048]{1,0:T(8,128)(2,1)S(1)} %get-tuple-element.21), channel_id=1, source_target_pairs={{0,2},{8,9},{1,3},{9,24},{16,18},{24,25},{17,19},{25,8},{32,34},{4... | collective-permute-start | bytes 786440 | tf_op jit(solution)/shard_map/ppermute | solution.py:37
  10.1 10.2 %collective-permute-start.4 = (bf16[64,2048]{1,0:T(8,128)(2,1)S(1)}, bf16[64,2048]{1,0:T(8,128)(2,1)S(1)}, u32[]{:S(2)}, u32[]{:S(2)}) collective-permute-start(bf16[64,2048]{1,0:T(8,128)(2,1)S(1)} %get-tuple-element.21), channel_id=1, source_target_pairs={{0,4},{8,24},{1,5},{9,25},{16,20},{24,8},{17,21},{25,9},{32,36},{4... | collective-permute-start | bytes 786440 | tf_op jit(solution)/shard_map/ppermute | solution.py:37
  13.4 6.9 %collective-permute-start.5 = (bf16[64,2048]{1,0:T(8,128)(2,1)S(1)}, bf16[64,2048]{1,0:T(8,128)(2,1)S(1)}, u32[]{:S(2)}, u32[]{:S(2)}) collective-permute-start(bf16[64,2048]{1,0:T(8,128)(2,1)S(1)} %get-tuple-element.21), channel_id=1, source_target_pairs={{0,6},{8,25},{1,7},{9,8},{16,22},{24,9},{17,23},{25,24},{32,38},{4... | collective-permute-start | bytes 786440 | tf_op jit(solution)/shard_map/ppermute | solution.py:37
  16.3 57.0 %copy-start.10 = (s32[4]{0:T(128)S(1)}, s32[4]{0:T(128)}, u32[]{:S(2)}) copy-start(s32[4]{0:T(128)} %order_ref.1) | copy-start | bytes 52
  16.3 60.2 %copy-start.11 = (f32[512]{0:T(512)S(1)}, f32[512]{0:T(512)}, u32[]{:S(2)}) copy-start(f32[512]{0:T(512)} %param.16) | copy-start | bytes 6148
  20.2 56.4 %copy-start.12 = (s32[128]{0:T(128)S(1)}, s32[128]{0:T(128)}, u32[]{:S(2)}) copy-start(s32[128]{0:T(128)} %param.13) | copy-start | bytes 1540
  20.3 59.5 %copy-start.9 = (f32[64,4]{1,0:T(8,128)S(1)}, f32[64,4]{1,0:T(8,128)}, u32[]{:S(2)}) copy-start(f32[64,4]{1,0:T(8,128)} %constant.54.clone) | copy-start | bytes 3076
  20.3 66.9 %copy-start.2 = (bf16[256,2048]{1,0:T(8,128)(2,1)}, bf16[256,2048]{1,0:T(8,128)(2,1)S(1)}, u32[]{:S(2)}) copy-start(bf16[256,2048]{1,0:T(8,128)(2,1)S(1)} %constant_dynamic-update-slice_fusion.4.refs_2_) | copy-start | bytes 3145732
  20.3 25.2 %collective-permute-start.8 = (bf16[256,2048]{1,0:T(8,128)(2,1)S(1)}, bf16[256,2048]{1,0:T(8,128)(2,1)S(1)}, u32[]{:S(2)}, u32[]{:S(2)}) collective-permute-start(bf16[256,2048]{1,0:T(8,128)(2,1)S(1)} %constant_dynamic-update-slice_fusion.4.refs_2_), channel_id=1, source_target_pairs={{0,96},{8,14},{1,97},{9,15},{16,112},{24,30},{17,113},{25,31},{32,... | collective-permute-start | bytes 3145736 | tf_op jit(solution)/shard_map/ppermute | solution.py:37
  22.6 26.8 %collective-permute-start.7 = (bf16[256,2048]{1,0:T(8,128)(2,1)S(1)}, bf16[256,2048]{1,0:T(8,128)(2,1)S(1)}, u32[]{:S(2)}, u32[]{:S(2)}) collective-permute-start(bf16[256,2048]{1,0:T(8,128)(2,1)S(1)} %constant_dynamic-update-slice_fusion.4.refs_2_), channel_id=1, source_target_pairs={{0,64},{8,12},{1,65},{9,13},{16,80},{24,28},{17,81},{25,29},{32,96... | collective-permute-start | bytes 3145736 | tf_op jit(solution)/shard_map/ppermute | solution.py:37
  23.1 26.3 %collective-permute-start.6 = (bf16[256,2048]{1,0:T(8,128)(2,1)S(1)}, bf16[256,2048]{1,0:T(8,128)(2,1)}, u32[]{:S(2)}, u32[]{:S(2)}) collective-permute-start(bf16[256,2048]{1,0:T(8,128)(2,1)S(1)} %constant_dynamic-update-slice_fusion.4.refs_2_), channel_id=1, source_target_pairs={{0,32},{8,10},{1,33},{9,11},{16,48},{24,26},{17,49},{25,27},{32,64... | collective-permute-start | bytes 3145736 | tf_op jit(solution)/shard_map/ppermute | solution.py:37
  23.7 63.5 %collective-permute-start.9 = (bf16[256,2048]{1,0:T(8,128)(2,1)S(1)}, bf16[256,2048]{1,0:T(8,128)(2,1)}, u32[]{:S(2)}, u32[]{:S(2)}) collective-permute-start(bf16[256,2048]{1,0:T(8,128)(2,1)S(1)} %constant_dynamic-update-slice_fusion.4.refs_2_), channel_id=1, source_target_pairs={{0,8},{8,0},{1,9},{9,1},{16,24},{24,16},{17,25},{25,17},{32,40},{4... | collective-permute-start | bytes 3145736 | tf_op jit(solution)/shard_map/ppermute | solution.py:42
  45.5 41.6 %copy-start.3 = (bf16[256,2048]{1,0:T(8,128)(2,1)}, bf16[256,2048]{1,0:T(8,128)(2,1)S(1)}, u32[]{:S(2)}) copy-start(bf16[256,2048]{1,0:T(8,128)(2,1)S(1)} %collective-permute-done.8.refs_5_) | copy-start | bytes 3145732
  45.5 41.6 %collective-permute-start.12 = (bf16[256,2048]{1,0:T(8,128)(2,1)S(1)}, bf16[256,2048]{1,0:T(8,128)(2,1)}, u32[]{:S(2)}, u32[]{:S(2)}) collective-permute-start(bf16[256,2048]{1,0:T(8,128)(2,1)S(1)} %collective-permute-done.8.refs_5_), channel_id=1, source_target_pairs={{0,8},{8,0},{1,9},{9,1},{16,24},{24,16},{17,25},{25,17},{32,40},{4... | collective-permute-start | bytes 3145736 | tf_op jit(solution)/shard_map/ppermute | solution.py:42
  49.3 37.9 %copy-start.4 = (bf16[256,2048]{1,0:T(8,128)(2,1)}, bf16[256,2048]{1,0:T(8,128)(2,1)S(1)}, u32[]{:S(2)}) copy-start(bf16[256,2048]{1,0:T(8,128)(2,1)S(1)} %collective-permute-done.7.refs_4_) | copy-start | bytes 3145732
  49.3 37.8 %collective-permute-start.11 = (bf16[256,2048]{1,0:T(8,128)(2,1)S(1)}, bf16[256,2048]{1,0:T(8,128)(2,1)}, u32[]{:S(2)}, u32[]{:S(2)}) collective-permute-start(bf16[256,2048]{1,0:T(8,128)(2,1)S(1)} %collective-permute-done.7.refs_4_), channel_id=1, source_target_pairs={{0,8},{8,0},{1,9},{9,1},{16,24},{24,16},{17,25},{25,17},{32,40},{4... | collective-permute-start | bytes 3145736 | tf_op jit(solution)/shard_map/ppermute | solution.py:42
  49.4 37.8 %collective-permute-start.10 = (bf16[256,2048]{1,0:T(8,128)(2,1)}, bf16[256,2048]{1,0:T(8,128)(2,1)}, u32[]{:S(2)}, u32[]{:S(2)}) collective-permute-start(bf16[256,2048]{1,0:T(8,128)(2,1)} %collective-permute-done.6.refs_3_), channel_id=1, source_target_pairs={{0,8},{8,0},{1,9},{9,1},{16,24},{24,16},{17,25},{25,17},{32,40},{4... | collective-permute-start | bytes 3145736 | tf_op jit(solution)/shard_map/ppermute | solution.py:42
  64.4 21.9 %all-to-all-start = ((bf16[128,16,128]{2,1,0:T(8,128)(2,1)}), bf16[128,16,128]{2,1,0:T(8,128)(2,1)}, u32[]{:S(2)}, u32[]{:S(2)}) async-start(bf16[128,16,128]{2,1,0:T(8,128)(2,1)} %get-tuple-element.13), calls=%async_computation | async-start | bytes 1048576 | tf_op jit(solution)/shard_map/all_to_all | solution.py:346
  95.2 9.3 %collective-permute-start.13 = (bf16[64,2048]{1,0:T(8,128)(2,1)}, bf16[64,2048]{1,0:T(8,128)(2,1)S(1)}, u32[]{:S(2)}, u32[]{:S(2)}) collective-permute-start(bf16[64,2048]{1,0:T(8,128)(2,1)} %get-tuple-element.19), channel_id=1, source_target_pairs={{0,32},{8,40},{1,33},{9,41},{16,48},{24,56},{17,49},{25,57},{32,64... | collective-permute-start | bytes 786440 | tf_op jit(solution)/shard_map/ppermute | solution.py:37
  95.6 13.2 %collective-permute-start.15 = (bf16[64,2048]{1,0:T(8,128)(2,1)}, bf16[64,2048]{1,0:T(8,128)(2,1)S(1)}, u32[]{:S(2)}, u32[]{:S(2)}) collective-permute-start(bf16[64,2048]{1,0:T(8,128)(2,1)} %get-tuple-element.19), channel_id=1, source_target_pairs={{0,96},{8,104},{1,97},{9,105},{16,112},{24,120},{17,113},{25,121},... | collective-permute-start | bytes 786440 | tf_op jit(solution)/shard_map/ppermute | solution.py:37
  97.9 10.8 %collective-permute-start.14 = (bf16[64,2048]{1,0:T(8,128)(2,1)}, bf16[64,2048]{1,0:T(8,128)(2,1)S(1)}, u32[]{:S(2)}, u32[]{:S(2)}) collective-permute-start(bf16[64,2048]{1,0:T(8,128)(2,1)} %get-tuple-element.19), channel_id=1, source_target_pairs={{0,64},{8,72},{1,65},{9,73},{16,80},{24,88},{17,81},{25,89},{32,96... | collective-permute-start | bytes 786440 | tf_op jit(solution)/shard_map/ppermute | solution.py:37
  104.5 14.8 %copy-start.8 = (bf16[64,2048]{1,0:T(8,128)(2,1)S(1)}, bf16[64,2048]{1,0:T(8,128)(2,1)}, u32[]{:S(2)}) copy-start(bf16[64,2048]{1,0:T(8,128)(2,1)} %get-tuple-element.20) | copy-start | bytes 786436
  108.8 57.2 %copy-start.5 = (bf16[256,2048]{1,0:T(8,128)(2,1)}, bf16[256,2048]{1,0:T(8,128)(2,1)S(1)}, u32[]{:S(2)}) copy-start(bf16[256,2048]{1,0:T(8,128)(2,1)S(1)} %constant_dynamic-update-slice_fusion.11.refs_3_) | copy-start | bytes 3145732
  108.9 72.6 %collective-permute-start.25 = (bf16[256,2048]{1,0:T(8,128)(2,1)S(1)}, bf16[256,2048]{1,0:T(8,128)(2,1)}, u32[]{:S(2)}, u32[]{:S(2)}) collective-permute-start(bf16[256,2048]{1,0:T(8,128)(2,1)S(1)} %constant_dynamic-update-slice_fusion.11.refs_3_), channel_id=1, source_target_pairs={{0,16},{8,24},{1,17},{9,25},{16,0},{24,8},{17,1},{25,9},{32,48},{4... | collective-permute-start | bytes 3145736 | tf_op jit(solution)/shard_map/ppermute | solution.py:37
  112.2 79.6 %all-to-all-start.1 = ((bf16[128,16,512]{2,1,0:T(8,128)(2,1)}), bf16[128,16,512]{2,1,0:T(8,128)(2,1)S(1)}, u32[]{:S(2)}, u32[]{:S(2)}) async-start(bf16[128,16,512]{2,1,0:T(8,128)(2,1)} %get-tuple-element.15), calls=%async_computation.1 | async-start | bytes 4194304 | tf_op jit(solution)/shard_map/all_to_all | solution.py:347
  119.3 43.2 %collective-permute-start.16 = (bf16[64,2048]{1,0:T(8,128)(2,1)S(1)}, bf16[64,2048]{1,0:T(8,128)(2,1)S(1)}, u32[]{:S(2)}, u32[]{:S(2)}) collective-permute-start(bf16[64,2048]{1,0:T(8,128)(2,1)S(1)} %copy-done.8), channel_id=1, source_target_pairs={{0,16},{8,24},{1,17},{9,25},{16,0},{24,8},{17,1},{25,9},{32,48},{4... | collective-permute-start | bytes 786440 | tf_op jit(solution)/shard_map/ppermute | solution.py:37
  162.4 28.8 %copy-start.6 = (bf16[128,2048]{1,0:T(8,128)(2,1)}, bf16[128,2048]{1,0:T(8,128)(2,1)S(1)}, u32[]{:S(2)}) copy-start(bf16[128,2048]{1,0:T(8,128)(2,1)S(1)} %constant_dynamic-update-slice_fusion.15.refs_4_) | copy-start | bytes 1572868
  162.5 12.7 %collective-permute-start.23 = (bf16[128,2048]{1,0:T(8,128)(2,1)S(1)}, bf16[128,2048]{1,0:T(8,128)(2,1)}, u32[]{:S(2)}, u32[]{:S(2)}) collective-permute-start(bf16[128,2048]{1,0:T(8,128)(2,1)S(1)} %constant_dynamic-update-slice_fusion.15.refs_4_), channel_id=1, source_target_pairs={{0,64},{8,72},{1,65},{9,73},{16,80},{24,88},{17,81},{25,89},{32,96... | collective-permute-start | bytes 1572872 | tf_op jit(solution)/shard_map/ppermute | solution.py:37
  163.7 23.9 %collective-permute-start.20 = (bf16[128,2048]{1,0:T(8,128)(2,1)S(1)}, bf16[128,2048]{1,0:T(8,128)(2,1)}, u32[]{:S(2)}, u32[]{:S(2)}) collective-permute-start(bf16[128,2048]{1,0:T(8,128)(2,1)S(1)} %constant_dynamic-update-slice_fusion.15.refs_4_), channel_id=1, source_target_pairs={{0,96},{8,104},{1,97},{9,105},{16,112},{24,120},{17,113},{25,121},... | collective-permute-start | bytes 1572872 | tf_op jit(solution)/shard_map/ppermute | solution.py:37
  166.1 37.8 %collective-permute-start.18 = (bf16[256,2048]{1,0:T(8,128)(2,1)S(1)}, bf16[256,2048]{1,0:T(8,128)(2,1)}, u32[]{:S(2)}, u32[]{:S(2)}) collective-permute-start(bf16[256,2048]{1,0:T(8,128)(2,1)S(1)} %constant_dynamic-update-slice_fusion.11.refs_3_), channel_id=1, source_target_pairs={{0,8},{8,0},{1,9},{9,1},{16,24},{24,16},{17,25},{25,17},{32,40},{4... | collective-permute-start | bytes 3145736 | tf_op jit(solution)/shard_map/ppermute | solution.py:42
  169.1 20.2 %collective-permute-start.19 = (bf16[128,2048]{1,0:T(8,128)(2,1)S(1)}, bf16[128,2048]{1,0:T(8,128)(2,1)}, u32[]{:S(2)}, u32[]{:S(2)}) collective-permute-start(bf16[128,2048]{1,0:T(8,128)(2,1)S(1)} %constant_dynamic-update-slice_fusion.15.refs_4_), channel_id=1, source_target_pairs={{0,32},{8,40},{1,33},{9,41},{16,48},{24,56},{17,49},{25,57},{32,64... | collective-permute-start | bytes 1572872 | tf_op jit(solution)/shard_map/ppermute | solution.py:37
  175.2 14.6 %collective-permute-start.17 = (bf16[128,2048]{1,0:T(8,128)(2,1)S(1)}, bf16[128,2048]{1,0:T(8,128)(2,1)S(1)}, u32[]{:S(2)}, u32[]{:S(2)}) collective-permute-start(bf16[128,2048]{1,0:T(8,128)(2,1)S(1)} %constant_dynamic-update-slice_fusion.15.refs_4_), channel_id=1, source_target_pairs={{0,8},{8,0},{1,9},{9,1},{16,24},{24,16},{17,25},{25,17},{32,40},{4... | collective-permute-start | bytes 1572872 | tf_op jit(solution)/shard_map/ppermute | solution.py:42
  181.5 32.2 %collective-permute-start.26 = (bf16[256,2048]{1,0:T(8,128)(2,1)}, bf16[256,2048]{1,0:T(8,128)(2,1)}, u32[]{:S(2)}, u32[]{:S(2)}) collective-permute-start(bf16[256,2048]{1,0:T(8,128)(2,1)} %collective-permute-done.25.refs_10_), channel_id=1, source_target_pairs={{0,8},{8,0},{1,9},{9,1},{16,24},{24,16},{17,25},{25,17},{32,40},{4... | collective-permute-start | bytes 3145736 | tf_op jit(solution)/shard_map/ppermute | solution.py:42
  187.6 26.1 %collective-permute-start.24 = (bf16[128,2048]{1,0:T(8,128)(2,1)}, bf16[128,2048]{1,0:T(8,128)(2,1)}, u32[]{:S(2)}, u32[]{:S(2)}) collective-permute-start(bf16[128,2048]{1,0:T(8,128)(2,1)} %collective-permute-done.23.refs_8_), channel_id=1, source_target_pairs={{0,8},{8,0},{1,9},{9,1},{16,24},{24,16},{17,25},{25,17},{32,40},{4... | collective-permute-start | bytes 1572872 | tf_op jit(solution)/shard_map/ppermute | solution.py:42
  189.3 24.4 %collective-permute-start.22 = (bf16[128,2048]{1,0:T(8,128)(2,1)}, bf16[128,2048]{1,0:T(8,128)(2,1)}, u32[]{:S(2)}, u32[]{:S(2)}) collective-permute-start(bf16[128,2048]{1,0:T(8,128)(2,1)} %collective-permute-done.20.refs_5_), channel_id=1, source_target_pairs={{0,8},{8,0},{1,9},{9,1},{16,24},{24,16},{17,25},{25,17},{32,40},{4... | collective-permute-start | bytes 1572872 | tf_op jit(solution)/shard_map/ppermute | solution.py:42
  189.7 0.8 copy-start.7
  190.5 23.2 %collective-permute-start.21 = (bf16[128,2048]{1,0:T(8,128)(2,1)}, bf16[128,2048]{1,0:T(8,128)(2,1)}, u32[]{:S(2)}, u32[]{:S(2)}) collective-permute-start(bf16[128,2048]{1,0:T(8,128)(2,1)} %collective-permute-done.19.refs_4_), channel_id=1, source_target_pairs={{0,8},{8,0},{1,9},{9,1},{16,24},{24,16},{17,25},{25,17},{32,40},{4... | collective-permute-start | bytes 1572872 | tf_op jit(solution)/shard_map/ppermute | solution.py:42
  191.8 1.3 copy-start.1

commit v2 on v1

v2 whole, which is shorter than its diff:
```python
import numpy as np
import jax
import jax.numpy as jnp
from jax import lax
from jax.experimental import pallas as pl
from jax.experimental.pallas import tpu as pltpu
from jax.sharding import PartitionSpec as P


AXES = ("occ", "vir")
SIZE = {"x": 4, "y": 4, "z": 4}
ORDER = (("z", "x", "y"), ("y", "z", "x"))


def line(p):
    return ((p["y"] * 2 + p["z"] // 2) * 2 + p["c"]) * 8 + p["x"] * 2 + p["z"] % 2


def places():
    return [
        dict(x=x, y=y, z=z, c=c)
        for x in range(4)
        for y in range(4)
        for z in range(4)
        for c in range(2)
    ]


def moved(p, dim, by):
    q = dict(p)
    q[dim] = (q[dim] + by) % SIZE[dim]
    return q


def shifted(value, dims, by):
    pairs = [(line(p), line(moved(p, dims[p["c"]], by))) for p in places()]
    return lax.ppermute(value, AXES, pairs)


def swapped(value):
    pairs = [(line(p), line(dict(p, c=1 - p["c"]))) for p in places()]
    return lax.ppermute(value, AXES, pairs)


def metric_table():
    table = np.zeros((128, 129), np.int32)
    for p in places():
        for buf in range(8):
            core = p["c"] if buf < 4 else 1 - p["c"]
            first, second, third = ORDER[core]
            for k2 in range(4):
                for k1 in range(4):
                    q = dict(p, c=core)
                    for dim, by in ((third, buf % 4), (second, k2), (first, k1)):
                        q = moved(q, dim, -by)
                    block = line(q) // 16 * 8 + line(q) % 8 + (buf // 4) * 64
                    table[line(p), buf * 16 + k2 * 4 + k1] = block
        table[line(p), 128] = p["c"]
    return table


def gathered_metric(rows):
    for stage in (0, 1):
        dims = (ORDER[0][stage], ORDER[1][stage])
        got = [shifted(rows, dims, by) for by in (1, 2, 3)]
        rows = jnp.concatenate([rows] + got, axis=0)
    dims = (ORDER[0][2], ORDER[1][2])
    mine = [rows] + [shifted(rows, dims, by) for by in (1, 2, 3)]
    return mine, [swapped(part) for part in mine]


PITCH = 168


def half_kernel(order_ref, owner_ref, ints_ref, coeff_ref, part_ref, own_ref, *scratches):
    ints, scratch, pick_ref, part, own, in_sems, out_sems = scratches
    takes = [
        pltpu.make_async_copy(
            ints_ref.at[pl.ds(c * 4, 4)], ints.at[pl.ds(c * 4, 4)], in_sems.at[c]
        )
        for c in range(4)
    ]
    for take in takes:
        take.start()
    owners = jnp.broadcast_to(owner_ref[...].astype(jnp.float32), (128, 128)).T
    orbital = lax.broadcasted_iota(jnp.int32, (128, 128), 1).astype(jnp.float32)
    pick_ref[0:128, :] = jnp.where(owners == orbital, 1.0, 0.0)
    for s in range(4):
        first = pl.multiple_of(order_ref[s] * 8, 8)
        pick_ref[128 + 8 * s:136 + 8 * s, :] = pick_ref[pl.ds(first, 8), :]
    pick = pick_ref[...].astype(jnp.bfloat16)

    for c in range(4):
        takes[c].wait()
        half = jnp.dot(
            ints[c * 4:c * 4 + 4].reshape(512, 640),
            coeff_ref[...],
            preferred_element_type=jnp.float32,
        ).astype(jnp.bfloat16)
        for i in range(4):
            rows = jnp.dot(
                pick, half[i * 128:i * 128 + 128], preferred_element_type=jnp.float32
            )
            at = (c * 4 + i) * PITCH
            for t in range(4):
                scratch[t, at:at + 160, :] = rows[:, t * 128:t * 128 + 128]

    lane = lax.broadcasted_iota(jnp.int32, (16, 128), 1)
    low = lane < 64

    def rows_of(t, position):
        return scratch.at[t][pl.ds(position, 16, stride=PITCH), :]

    def emit_partner(v, carry):
        for t in range(4):
            for s in range(4):
                tile = rows_of(t, 128 + s * 8 + v).astype(part.dtype)
                for far in range(2):
                    for z in range(2):
                        owner = ((t // 2 + 2 * far) * 2 + z) * 2 + t % 2
                        part[owner * 8 + v, :, s * 128:s * 128 + 128] = tile
        return carry

    lax.fori_loop(0, 8, emit_partner, 0)
    send_part = pltpu.make_async_copy(part, part_ref, out_sems.at[0])
    send_part.start()

    def emit(group, carry):
        to = pl.multiple_of(group * 8, 8)
        for t in range(4):
            for j in range(4):
                even = rows_of(t, group * 8 + 2 * j)
                odd = rows_of(t, group * 8 + 2 * j + 1)
                first = jnp.where(low, even, pltpu.roll(odd, 64, 1))
                second = jnp.where(low, pltpu.roll(even, 64, 1), odd)
                at = slice(j * 128, j * 128 + 128)
                own[to + 2 * t, :, at] = first.astype(own.dtype)
                own[to + 2 * t + 1, :, at] = second.astype(own.dtype)
        return carry

    sends = [
        pltpu.make_async_copy(
            own.at[pl.ds(h * 64, 64)], own_ref.at[pl.ds(h * 64, 64)], out_sems.at[1 + h]
        )
        for h in range(2)
    ]
    for h in range(2):
        lax.fori_loop(8 * h, 8 * h + 8, emit, 0)
        sends[h].start()
    send_part.wait()
    for send in sends:
        send.wait()


def transformed(pair_order, owner_table, three_index, virt_coeff):
    vmem, hbm = pl.BlockSpec(memory_space=pltpu.VMEM), pl.BlockSpec(memory_space=pl.ANY)
    part = jax.ShapeDtypeStruct((128, 16, 512), jnp.bfloat16)
    own = jax.ShapeDtypeStruct((128, 16, 512), jnp.bfloat16)
    return pl.pallas_call(
        half_kernel,
        in_specs=[pl.BlockSpec(memory_space=pltpu.SMEM), vmem, hbm, vmem],
        out_specs=[hbm, hbm],
        out_shape=[part, own],
        scratch_shapes=[
            pltpu.VMEM((16, 128, 640), jnp.bfloat16),
            pltpu.VMEM((4, 16 * PITCH, 128), jnp.float32),
            pltpu.VMEM((160, 128), jnp.float32),
            pltpu.VMEM(part.shape, part.dtype),
            pltpu.VMEM(own.shape, own.dtype),
            pltpu.SemaphoreType.DMA((4,)),
            pltpu.SemaphoreType.DMA((3,)),
        ],
        name="half",
    )(pair_order, owner_table.reshape(1, 128), three_index, virt_coeff)


def place(table_ref, parts, first, metric, sems):
    for i, part in enumerate(parts):

        def start(j, carry, i=i, part=part):
            row = pl.multiple_of(table_ref[(first + i) * 16 + j] * 16, 16)
            pltpu.make_async_copy(
                part.at[pl.ds(pl.multiple_of(j * 16, 16), 16)],
                metric.at[pl.ds(row, 16)],
                sems.at[first + i],
            ).start()
            return carry

        lax.fori_loop(0, 16, start, 0)


def placed(parts, first, metric, sems):
    for i, part in enumerate(parts):
        pltpu.make_async_copy(part, metric.at[pl.ds(0, 256)], sems.at[first + i]).wait()


def fitted(left, metric):
    return lax.dot_general(
        left, metric, (((1,), (1,)), ((), ())), preferred_element_type=jnp.float32
    ).astype(jnp.bfloat16)


def partner_kernel(table_ref, mine_ref, other_ref, *refs):
    parts, outs, (rows, metric, sems, row_sems) = refs[:4], refs[4:8], refs[8:]
    core = table_ref[128]
    takes = [
        pltpu.make_async_copy(mine_ref, rows.at[core], row_sems.at[0]),
        pltpu.make_async_copy(other_ref, rows.at[1 - core], row_sems.at[1]),
    ]
    for take in takes:
        take.start()
    place(table_ref, parts, 0, metric, sems)
    for take in takes:
        take.wait()
    left = [rows[c].T for c in range(2)]
    placed(parts, 0, metric, sems)
    for c in range(2):
        for block in range(2):
            at = slice(block * 512, block * 512 + 512)
            got = fitted(left[c], metric[at, :])
            outs[2 * c][:, at] = got[:256]
            outs[2 * c + 1][:, at] = got[256:]


def partner_fit(table, mine, other, parts):
    smem, vmem = pl.BlockSpec(memory_space=pltpu.SMEM), pl.BlockSpec(memory_space=pltpu.VMEM)
    shape = jax.ShapeDtypeStruct((256, 1024), jnp.bfloat16)
    return pl.pallas_call(
        partner_kernel,
        in_specs=[smem] + [pl.BlockSpec(memory_space=pl.ANY)] * 6,
        out_specs=[vmem] * 4,
        out_shape=[shape] * 4,
        scratch_shapes=[
            pltpu.VMEM((2, 2048, 512), jnp.bfloat16),
            pltpu.VMEM((1024, 2048), jnp.bfloat16),
            pltpu.SemaphoreType.DMA((4,)),
            pltpu.SemaphoreType.DMA((2,)),
        ],
        name="fit_partner",
    )(table, mine, other, *parts)


def fetch(groups, buf, sems):
    found, at, used = [], 0, 0
    for group in groups:
        start, copies = at, []
        for piece in group:
            rows = piece[0].shape[0]
            for half in range(2):
                to = buf.at[pl.ds(at, rows), pl.ds(half * 1024, 1024)]
                copies.append(pltpu.make_async_copy(piece[half], to, sems.at[used]))
                used += 1
            at += rows
        for copy in copies:
            copy.start()
        found.append((start, at, copies))
    return found


def contribute(own, part, row, col, total, fresh, carried, finished):
    pair = lax.dot_general(
        own[...], part, (((1,), (1,)), ((), ())), preferred_element_type=jnp.float32
    )
    amp = (pair / (row + col)).astype(jnp.bfloat16)
    if carried is not None:
        carried[1].wait()
    for chunk in range(4):
        at = slice(chunk * 512, chunk * 512 + 512)
        term = jnp.dot(amp, part[:, at], preferred_element_type=jnp.float32)
        if not fresh:
            term = total[:, at] + term
        if carried is not None:
            term = carried[0][:, at] + term
        total[:, at] = term
        finished(chunk)


def grouped(refs, sizes):
    groups, at = [], 0
    for size in sizes:
        groups.append([refs[at + 2 * i:at + 2 * i + 2] for i in range(size)])
        at += 2 * size
    return groups


def own_kernel(table_ref, rows_ref, row_ref, col_ref, *refs, sizes):
    count = 2 * sum(sizes)
    parts, pieces, refs = refs[:8], refs[8:8 + count], refs[8 + count:]
    own_ref, total_ref, rows, metric, own, buf, total, sems, piece_sems, more = refs
    take = pltpu.make_async_copy(rows_ref, rows, more.at[0])
    take.start()
    place(table_ref, parts, 0, metric, sems)
    groups = fetch(grouped(pieces, sizes), buf, piece_sems)
    take.wait()
    left = rows[...].T
    for half in range(2):
        placed(parts[half * 4:half * 4 + 4], half * 4, metric, sems)
        for block in range(2):
            first = half * 1024 + block * 512
            at = slice(first, first + 512)
            own[:, at] = fitted(left, metric[at, :])
    sends = [pltpu.make_async_copy(own, own_ref, more.at[1])]
    sends[0].start()
    row = row_ref[:, :1]
    for index, (start, stop, copies) in enumerate(groups):
        for copy in copies:
            copy.wait()

        def finished(chunk, last=index == len(groups) - 1):
            if last:
                at = pl.ds(chunk * 512, 512)
                sends.append(
                    pltpu.make_async_copy(total.at[:, at], total_ref.at[:, at], more.at[2 + chunk])
                )
                sends[-1].start()

        contribute(
            own, buf[start:stop, :], row, col_ref[:, start:stop], total,
            index == 0, None, finished,
        )
    for send in sends:
        send.wait()


def own_and_pair(table, own, row, col, parts, groups):
    smem, vmem = pl.BlockSpec(memory_space=pltpu.SMEM), pl.BlockSpec(memory_space=pltpu.VMEM)
    hbm = pl.BlockSpec(memory_space=pl.ANY)
    sizes = tuple(len(group) for group in groups)
    pieces = [half for group in groups for piece in group for half in piece]
    count = sum(piece.shape[0] for piece in pieces) // 2

    def body(*refs):
        own_kernel(*refs, sizes=sizes)

    return pl.pallas_call(
        body,
        in_specs=[smem, hbm, vmem, vmem] + [hbm] * (8 + len(pieces)),
        out_specs=[hbm] * 2,
        out_shape=[
            jax.ShapeDtypeStruct((512, 2048), jnp.bfloat16),
            jax.ShapeDtypeStruct((512, 2048), jnp.float32),
        ],
        scratch_shapes=[
            pltpu.VMEM((2048, 512), jnp.bfloat16),
            pltpu.VMEM((2048, 2048), jnp.bfloat16),
            pltpu.VMEM((512, 2048), jnp.bfloat16),
            pltpu.VMEM((count, 2048), jnp.bfloat16),
            pltpu.VMEM((512, 2048), jnp.float32),
            pltpu.SemaphoreType.DMA((8,)),
            pltpu.SemaphoreType.DMA((len(pieces),)),
            pltpu.SemaphoreType.DMA((6,)),
        ],
        name="own_and_pair",
    )(table, own, row, col, *parts, *pieces)


def pair_kernel(table_ref, own_ref, total_ref, row_ref, col_ref, *refs, sizes):
    count = 2 * sum(sizes)
    pieces, (out_ref, own, buf, before, total, piece_sems, more) = refs[:count], refs[count:]
    core = table_ref[128]
    take = pltpu.make_async_copy(own_ref, own, more.at[0])
    take.start()
    groups = fetch(grouped(pieces, sizes), buf, piece_sems)
    carried = pltpu.make_async_copy(total_ref, before, more.at[1])
    carried.start()
    row = row_ref[:, :1]
    take.wait()
    sends = []

    for index, (start, stop, copies) in enumerate(groups):
        for copy in copies:
            copy.wait()

        def finished(chunk, last=index == len(groups) - 1):
            if last:
                for tile in range(chunk * 4, chunk * 4 + 4):
                    half = core if tile < 8 else 1 - core
                    to = pl.multiple_of(((tile % 8) * 2 + half) * 128, 128)
                    sends.append(
                        pltpu.make_async_copy(
                            total.at[:, pl.ds(tile * 128, 128)],
                            out_ref.at[:, pl.ds(to, 128)],
                            more.at[2 + tile],
                        )
                    )
                    sends[-1].start()

        contribute(
            own, buf[start:stop, :], row, col_ref[:, start:stop], total,
            index == 0, (before, carried) if index == len(groups) - 1 else None, finished,
        )
    for send in sends:
        send.wait()


def paired(table, own, total, row, col, groups):
    smem, vmem = pl.BlockSpec(memory_space=pltpu.SMEM), pl.BlockSpec(memory_space=pltpu.VMEM)
    hbm = pl.BlockSpec(memory_space=pl.ANY)
    sizes = tuple(len(group) for group in groups)
    pieces = [half for group in groups for piece in group for half in piece]
    count = sum(piece.shape[0] for piece in pieces) // 2

    def body(*refs):
        pair_kernel(*refs, sizes=sizes)

    return pl.pallas_call(
        body,
        in_specs=[smem, hbm, hbm, vmem, vmem] + [hbm] * len(pieces),
        out_specs=hbm,
        out_shape=jax.ShapeDtypeStruct((512, 2048), jnp.float32),
        scratch_shapes=[
            pltpu.VMEM((512, 2048), jnp.bfloat16),
            pltpu.VMEM((count, 2048), jnp.bfloat16),
            pltpu.VMEM((512, 2048), jnp.float32),
            pltpu.VMEM((512, 2048), jnp.float32),
            pltpu.SemaphoreType.DMA((len(pieces),)),
            pltpu.SemaphoreType.DMA((18,)),
        ],
        name="pair",
    )(table, own, total, row, col, *pieces)


def energies(me, owner_table, pair_order, occ_energy, vir_energy):
    occ_idx, vir_idx = me // 8, me % 8
    one_hot = (owner_table[:, None] == jnp.arange(128, dtype=jnp.int32)[None, :]).astype(jnp.float32)
    eps = jnp.dot(one_hot, occ_energy, precision=lax.Precision.HIGHEST)
    own_eps = lax.dynamic_slice_in_dim(eps, occ_idx * 8, 8, 0)
    block_eps = lax.dynamic_slice_in_dim(vir_energy, vir_idx * 64, 64, 0)
    row = (own_eps[:, None] - block_eps[None, :]).reshape(512, 1)
    row = jnp.broadcast_to(row, (512, 128))
    partner_eps = jnp.concatenate(
        [lax.dynamic_slice_in_dim(eps, pair_order[s] * 8 + vir_idx, 1, 0) for s in range(4)]
    )
    blocks = partner_eps[None, None, :, None] - vir_energy.reshape(2, 2, 1, 128)
    odd = occ_idx // 4 % 2 == 1
    near = jnp.where(odd, blocks[1], blocks[0])
    far = jnp.where(odd, blocks[0], blocks[1])
    far = far.reshape(2, 2, 2, 128).transpose(1, 0, 2, 3)
    return row, near.reshape(1, 1024), far.reshape(1, 1024)


def whole(three_index, virt_coeff, metric_root, owner_table, pair_order, occ_energy, vir_energy):
    me = lax.axis_index("occ") * 8 + lax.axis_index("vir")
    mine_parts, other_parts = gathered_metric(metric_root)
    part, own = transformed(pair_order, owner_table, three_index, virt_coeff)
    part = lax.all_to_all(part, AXES, split_axis=0, concat_axis=0, tiled=True)
    own = lax.all_to_all(own, AXES, split_axis=0, concat_axis=0, tiled=True)
    part, own = part.reshape(2048, 512), own.reshape(2048, 512)

    row, near, far = energies(me, owner_table, pair_order, occ_energy, vir_energy)
    table = lax.dynamic_slice_in_dim(jnp.asarray(metric_table()), me, 1, 0).reshape(129)
    part, row, near, far, table = lax.optimization_barrier((part, row, near, far, table))
    other = swapped(part)
    here = partner_fit(table, part, other, mine_parts)

    there = []
    for i, by in ((0, 1), (2, 3), (1, 1), (3, 3)):
        there.append(shifted(here[i], ("y", "y"), by))

    def whole_rows(part):
        return part, swapped(part)

    here, there = [whole_rows(part) for part in here], [whole_rows(part) for part in there]
    own, density = own_and_pair(
        table, own, row, near, mine_parts + other_parts, [here[:2], here[2:]]
    )
    density = paired(table, own, density, row, far, [there[:2], there[2:]])
    return density.reshape(8, 64, 2048)


def solution(mesh):
    placed = (P(AXES, None, None), P(), P(AXES, None), P(), P(), P(), P())
    return jax.shard_map(
        whole, mesh=mesh, in_specs=placed, out_specs=P("occ", "vir", None), check_vma=False
    )
```

time: 227 us -> 173 us (0.76)
  waiting for transfers between devices: 90 us -> 59.4 us
  starting transfers between devices: 68 us -> 54.7 us
  Pallas kernels: 52.4 us -> 42.6 us
  other arithmetic: 0.07 us -> 3.23 us
  matrix products: 3.14 us -> 0.19 us
    ppermute x17 -> x13, waiting for transfers between devices: 86.5 us -> 59.3 us  [shifted(): return lax.ppermute(value, AXES, pairs)]
    ppermute x17 -> x13, starting transfers between devices: 28.6 us -> 21 us  [shifted(): return lax.ppermute(value, AXES, pairs)]
    pallas_call x4 -> x3, Pallas kernels: 41.4 us -> 34.1 us  [the longest x1 14.7 us: own_and_pair(): pl.pallas_call(body, in_specs=[smem, hbm, vmem, vmem] + [hbm] * (8 + len(...]
    ppermute x10 -> x13, starting transfers between devices: 23.6 us -> 16.4 us  [swapped(): return lax.ppermute(value, AXES, pairs)]
    all_to_all x1, waiting for transfers between devices: 3.43 us -> 0.01 us  [whole(): part = lax.all_to_all(part, AXES, split_axis=0, concat_axis=0, tiled=True)]
    dot_general x2 -> x0, matrix products: 2.94 us -> none  [the longest x1 2.71 us: energies(): jnp.dot(which, partner_eps[:, None], precision=lax.Precision.HIGHEST)]
    all_to_all x1, starting transfers between devices: 8.78 us -> 11.5 us  [whole(): part = lax.all_to_all(part, AXES, split_axis=0, concat_axis=0, tiled=True)]
    concatenate x0 -> x1, other arithmetic: none -> 2.49 us  [energies(): jnp.concatenate([lax.dynamic_slice_in_dim(eps, pair_order[s] * 8 + vir_id...]
  transfers between devices with their start and end apart: 29 -> 28, of which waited for: 10 -> 7; matrix products, arithmetic and copies ran while one was open for 5% -> 7% of each run, Pallas kernels for 14% -> 14%
where the time goes in v2:
time: 173 us; the launch traced here: 172 us
  waiting for transfers between devices  59.4 us (34%)
  starting transfers between devices  54.7 us (32%)
  Pallas kernels  42.6 us (25%)
  local copies, waits for them, and re-layouts  8.92 us (5%)
  other arithmetic  3.23 us (2%)
  between operations  2.91 us (2%)
    ppermute x13, waiting for transfers between devices, shifted(): return lax.ppermute(value, AXES, pairs)  59.3 us
    ppermute x13, starting transfers between devices, shifted(): return lax.ppermute(value, AXES, pairs)  21 us
    ppermute x13, starting transfers between devices, swapped(): return lax.ppermute(value, AXES, pairs)  16.4 us
    pallas_call x1, Pallas kernels, own_and_pair(): pl.pallas_call(body, in_specs=[smem, hbm, vmem, vmem] + [hbm] * (8 + len(...  14.7 us
    all_to_all x1, starting transfers between devices, whole(): part = lax.all_to_all(part, AXES, split_axis=0, concat_axis=0, tiled=True)  11.5 us
    pallas_call x1, Pallas kernels, paired(): pl.pallas_call(body, in_specs=[smem, hbm, hbm, vmem, vmem] + [hbm] * len(...  9.86 us
    pallas_call x1, Pallas kernels, partner_fit(): pl.pallas_call(partner_kernel, in_specs=[smem] + [pl.BlockSpec(memory_spa...  9.54 us
    pallas_call x1, Pallas kernels, transformed(): pl.pallas_call(half_kernel, in_specs=[pl.BlockSpec(memory_space=pltpu.SME...  8.57 us
  transfers between devices with their start and end apart: 28, of which 7 were waited for; matrix products, arithmetic and copies ran while one was open for 7% of the time, Pallas kernels for 14%

profile of v2, /device:TPU:1, one launch (start us, length us, event | category | flops | bytes accessed | tf_op | source)
XLA Modules:
  0.0 172.0 jit_solution(14335050422337952914)
XLA Ops:
  0.0 8.6 %half.1 = (bf16[128,16,512]{2,1,0:T(8,128)(2,1)}, bf16[128,16,512]{2,1,0:T(8,128)(2,1)}) custom-call(s32[4]{0:T(128)} %order_ref.1, s32[1,128]{1,0:T(1,128)} %bitcast.29, bf16[16,128,640]{2,1,0:T(8,128)(2,1)} %ints_ref.1, bf16[640,512]{1,0:T(8,128)(2,1)} %coeff_ref.1), custom_call_target="tpu_custom_call" | custom-call | tf_op jit(solution)/shard_map/half/pallas_call | solution.py:159
  8.6 0.0 copy-start.9
  8.6 0.0 copy-start.10
  8.6 0.0 copy-start.12
  8.6 0.0 copy-start.11
  8.6 11.5 %all-to-all-start = ((bf16[128,16,512]{2,1,0:T(8,128)(2,1)}), bf16[128,16,512]{2,1,0:T(8,128)(2,1)S(1)}, u32[]{:S(2)}, u32[]{:S(2)}) async-start(bf16[128,16,512]{2,1,0:T(8,128)(2,1)} %get-tuple-element.18), calls=%async_computation | async-start | bytes 4194304 | tf_op jit(solution)/shard_map/all_to_all | solution.py:446
  20.2 1.4 collective-permute-start
  21.6 2.5 %collective-permute-start.1 = (bf16[16,2048]{1,0:T(8,128)(2,1)S(1)}, bf16[16,2048]{1,0:T(8,128)(2,1)S(1)}, u32[]{:S(2)}, u32[]{:S(2)}) collective-permute-start(bf16[16,2048]{1,0:T(8,128)(2,1)S(1)} %copy-done.9), channel_id=1, source_target_pairs={{0,16},{8,72},{1,17},{9,73},{16,0},{24,88},{17,1},{25,89},{32,48},... | collective-permute-start | bytes 196616 | tf_op jit(solution)/shard_map/ppermute | solution.py:37
  24.0 1.1 collective-permute-start.2
  25.2 0.6 fusion.3
  28.3 0.2 convolution_bitcast_fusion
  28.5 0.7 fusion.2
  29.2 2.5 %pad_maximum_fusion = f32[4]{0:T(128)S(1)} fusion(f32[1]{0:T(128)} %get-tuple-element.42, f32[1]{0:T(128)} %get-tuple-element.43, f32[1]{0:T(128)} %get-tuple-element.44, f32[1]{0:T(128)} %get-tuple-element.41), kind=kLoop, calls=%fused_computation.18 | loop fusion | flops 12 | bytes 32 | tf_op jit(solution)/shard_map/concatenate | solution.py:431
  31.7 0.1 broadcast_subtract_fusion
  31.7 0.7 constant_dynamic-update-slice_fusion.3
  32.4 0.6 slice_select_fusion
  33.0 0.1 dynamic_slice.22
  33.1 0.1 dynamic_slice.21
  33.1 9.9 %collective-permute-done = bf16[16,2048]{1,0:T(8,128)(2,1)S(1)} collective-permute-done((bf16[16,2048]{1,0:T(8,128)(2,1)S(1)}, bf16[16,2048]{1,0:T(8,128)(2,1)S(1)}, u32[]{:S(2)}, u32[]{:S(2)}) %collective-permute-start) | collective-permute-done | bytes 65568 | tf_op jit(solution)/shard_map/ppermute | solution.py:37
  43.0 0.6 constant_dynamic-update-slice_fusion.2
  43.7 2.8 %collective-permute-done.1 = bf16[16,2048]{1,0:T(8,128)(2,1)S(1)} collective-permute-done((bf16[16,2048]{1,0:T(8,128)(2,1)S(1)}, bf16[16,2048]{1,0:T(8,128)(2,1)S(1)}, u32[]{:S(2)}, u32[]{:S(2)}) %collective-permute-start.1) | collective-permute-done | bytes 65568 | tf_op jit(solution)/shard_map/ppermute | solution.py:37
  46.5 0.6 constant_dynamic-update-slice_fusion.1
  47.1 0.6 constant_dynamic-update-slice_fusion
  47.8 1.4 collective-permute-start.3
  49.1 0.1 broadcast_subtract_fusion.1
  49.2 2.9 %collective-permute-start.4 = (bf16[64,2048]{1,0:T(8,128)(2,1)}, bf16[64,2048]{1,0:T(8,128)(2,1)}, u32[]{:S(2)}, u32[]{:S(2)}) collective-permute-start(bf16[64,2048]{1,0:T(8,128)(2,1)} %get-tuple-element.31), channel_id=1, source_target_pairs={{0,4},{8,24},{1,5},{9,25},{16,20},{24,8},{17,21},{25,9},{32,36},{4... | collective-permute-start | bytes 786440 | tf_op jit(solution)/shard_map/ppermute | solution.py:37
  52.1 1.2 constant_dynamic-slice_fusion
  53.4 0.6 copy.9
  54.0 0.1 sub.46
  54.0 1.0 collective-permute-start.5
  55.1 0.0 all-to-all-done
  55.1 1.0 broadcast_in_dim.2.refs_2_.refs_3_
  56.0 0.9 collective-permute-start.13
  57.0 0.0 collective-permute-done.3
  57.0 2.2 %collective-permute-done.4 = bf16[64,2048]{1,0:T(8,128)(2,1)} collective-permute-done((bf16[64,2048]{1,0:T(8,128)(2,1)}, bf16[64,2048]{1,0:T(8,128)(2,1)}, u32[]{:S(2)}, u32[]{:S(2)}) %collective-permute-start.4) | collective-permute-done | bytes 262176 | tf_op jit(solution)/shard_map/ppermute | solution.py:37
  59.2 1.0 constant_dynamic-update-slice_fusion.5
  60.2 1.0 constant_dynamic-update-slice_fusion.4.refs_0_.refs_4_
  61.2 1.7 collective-permute-start.6
  62.9 2.5 %collective-permute-start.7 = (bf16[256,2048]{1,0:T(8,128)(2,1)S(1)}, bf16[256,2048]{1,0:T(8,128)(2,1)}, u32[]{:S(2)}, u32[]{:S(2)}) collective-permute-start(bf16[256,2048]{1,0:T(8,128)(2,1)S(1)} %constant_dynamic-update-slice_fusion.4.refs_0_.refs_4_), channel_id=1, source_target_pairs={{0,64},{8,12},{1,65},{9,13},{16,80},{24,28},{17,81},{25,29},{32,96... | collective-permute-start | bytes 3145736 | tf_op jit(solution)/shard_map/ppermute | solution.py:37
  65.4 1.1 collective-permute-start.8
  66.5 3.5 %collective-permute-start.9 = (bf16[256,2048]{1,0:T(8,128)(2,1)S(1)}, bf16[256,2048]{1,0:T(8,128)(2,1)}, u32[]{:S(2)}, u32[]{:S(2)}) collective-permute-start(bf16[256,2048]{1,0:T(8,128)(2,1)S(1)} %constant_dynamic-update-slice_fusion.4.refs_0_.refs_4_), channel_id=1, source_target_pairs={{0,8},{8,0},{1,9},{9,1},{16,24},{24,16},{17,25},{25,17},{32,40},{4... | collective-permute-start | bytes 3145736 | tf_op jit(solution)/shard_map/ppermute | solution.py:42
  70.1 6.7 %collective-permute-done.6.refs_1_.refs_5_ = bf16[256,2048]{1,0:T(8,128)(2,1)} collective-permute-done((bf16[256,2048]{1,0:T(8,128)(2,1)S(1)}, bf16[256,2048]{1,0:T(8,128)(2,1)}, u32[]{:S(2)}, u32[]{:S(2)}) %collective-permute-start.6) | collective-permute-done | bytes 1048608 | tf_op jit(solution)/shard_map/ppermute | solution.py:37
  76.8 3.3 %collective-permute-start.10 = (bf16[256,2048]{1,0:T(8,128)(2,1)}, bf16[256,2048]{1,0:T(8,128)(2,1)}, u32[]{:S(2)}, u32[]{:S(2)}) collective-permute-start(bf16[256,2048]{1,0:T(8,128)(2,1)} %collective-permute-done.6.refs_1_.refs_5_), channel_id=1, source_target_pairs={{0,8},{8,0},{1,9},{9,1},{16,24},{24,16},{17,25},{25,17},{32,40},{4... | collective-permute-start | bytes 3145736 | tf_op jit(solution)/shard_map/ppermute | solution.py:42
  80.1 9.1 %collective-permute-done.7.refs_2_.refs_6_ = bf16[256,2048]{1,0:T(8,128)(2,1)} collective-permute-done((bf16[256,2048]{1,0:T(8,128)(2,1)S(1)}, bf16[256,2048]{1,0:T(8,128)(2,1)}, u32[]{:S(2)}, u32[]{:S(2)}) %collective-permute-start.7) | collective-permute-done | bytes 1048608 | tf_op jit(solution)/shard_map/ppermute | solution.py:37
  89.2 3.6 %collective-permute-start.11 = (bf16[256,2048]{1,0:T(8,128)(2,1)}, bf16[256,2048]{1,0:T(8,128)(2,1)}, u32[]{:S(2)}, u32[]{:S(2)}) collective-permute-start(bf16[256,2048]{1,0:T(8,128)(2,1)} %collective-permute-done.7.refs_2_.refs_6_), channel_id=1, source_target_pairs={{0,8},{8,0},{1,9},{9,1},{16,24},{24,16},{17,25},{25,17},{32,40},{4... | collective-permute-start | bytes 3145736 | tf_op jit(solution)/shard_map/ppermute | solution.py:42
  92.8 0.0 collective-permute-start.12
  92.8 5.9 %all-to-all-start.1 = ((bf16[128,16,512]{2,1,0:T(8,128)(2,1)}), bf16[128,16,512]{2,1,0:T(8,128)(2,1)}, u32[]{:S(2)}, u32[]{:S(2)}) async-start(bf16[128,16,512]{2,1,0:T(8,128)(2,1)} %get-tuple-element.20), calls=%async_computation.1 | async-start | bytes 4194304 | tf_op jit(solution)/shard_map/all_to_all | solution.py:447
  98.7 0.0 collective-permute-done.13.other_ref
  98.7 9.5 %fit_partner.1 = (bf16[256,1024]{1,0:T(8,128)(2,1)}, bf16[256,1024]{1,0:T(8,128)(2,1)}, bf16[256,1024]{1,0:T(8,128)(2,1)}, bf16[256,1024]{1,0:T(8,128)(2,1)}) custom-call(s32[129]{0:T(256)} %bitcast.22, bf16[2048,512]{1,0:T(8,128)(2,1)} %bitcast.21, bf16[2048,512]{1,0:T(8,128)(2,1)} %collective-permute-done.13.other_ref, bf16[256,2048]{1,0:T(8,128)(2,1)} %copy-done.2, ...), custom_call_target="tpu_custom_call" | custom-call | tf_op jit(solution)/shard_map/fit_partner/pallas_call | solution.py:228
  108.2 1.4 collective-permute-start.14
  109.6 0.1 collective-permute-start.15
  109.7 0.4 collective-permute-start.16
  110.1 0.4 collective-permute-start.18
  110.6 2.2 %collective-permute-start.20 = (bf16[256,1024]{1,0:T(8,128)(2,1)}, bf16[256,1024]{1,0:T(8,128)(2,1)S(1)}, u32[]{:S(2)}, u32[]{:S(2)}) collective-permute-start(bf16[256,1024]{1,0:T(8,128)(2,1)} %get-tuple-element.26.refs_16_), channel_id=1, source_target_pairs={{0,96},{8,104},{1,97},{9,105},{16,112},{24,120},{17,113},{25,121},... | collective-permute-start | bytes 1572872 | tf_op jit(solution)/shard_map/ppermute | solution.py:37
  112.9 2.7 %collective-permute-start.24 = (bf16[256,1024]{1,0:T(8,128)(2,1)}, bf16[256,1024]{1,0:T(8,128)(2,1)}, u32[]{:S(2)}, u32[]{:S(2)}) collective-permute-start(bf16[256,1024]{1,0:T(8,128)(2,1)} %get-tuple-element.27.refs_18_), channel_id=1, source_target_pairs={{0,96},{8,104},{1,97},{9,105},{16,112},{24,120},{17,113},{25,121},... | collective-permute-start | bytes 1572872 | tf_op jit(solution)/shard_map/ppermute | solution.py:37
  115.5 1.2 collective-permute-start.17
  116.7 18.3 %collective-permute-done.18.refs_5_ = bf16[256,1024]{1,0:T(8,128)(2,1)S(1)} collective-permute-done((bf16[256,1024]{1,0:T(8,128)(2,1)}, bf16[256,1024]{1,0:T(8,128)(2,1)S(1)}, u32[]{:S(2)}, u32[]{:S(2)}) %collective-permute-start.18) | collective-permute-done | bytes 524320 | tf_op jit(solution)/shard_map/ppermute | solution.py:37
  135.0 0.9 collective-permute-start.19
  135.9 0.1 collective-permute-start.21
  135.9 10.3 %collective-permute-done.22.refs_9_ = bf16[256,1024]{1,0:T(8,128)(2,1)S(1)} collective-permute-done((bf16[256,1024]{1,0:T(8,128)(2,1)}, bf16[256,1024]{1,0:T(8,128)(2,1)S(1)}, u32[]{:S(2)}, u32[]{:S(2)}) %collective-permute-start.22) | collective-permute-done | bytes 524320 | tf_op jit(solution)/shard_map/ppermute | solution.py:37
  146.2 0.6 collective-permute-start.23
  146.9 0.3 collective-permute-start.25
  147.2 14.7 %own_and_pair.1 = (bf16[512,2048]{1,0:T(8,128)(2,1)}, f32[512,2048]{1,0:T(8,128)}) custom-call(s32[129]{0:T(256)} %bitcast.23, bf16[2048,512]{1,0:T(8,128)(2,1)} %bitcast.14.refs_1_, f32[512,128]{1,0:T(8,128)} %broadcast_in_dim.2.refs_2_.refs_3_, f32[1,1024]{1,0:T(1,128)} %bitcast.26, bf16[256,2048]{1,0:T(8,128)(2,1)} %copy-done.2, ...), custom_call_target="tpu_custom_call" | custom-call | tf_op jit(solution)/shard_map/own_and_pair/pallas_call | solution.py:335
  161.9 9.9 %pair.1 = f32[512,2048]{1,0:T(8,128)} custom-call(s32[129]{0:T(256)} %bitcast.24, bf16[512,2048]{1,0:T(8,128)(2,1)} %get-tuple-element.28.refs_1_, f32[512,2048]{1,0:T(8,128)} %get-tuple-element.29.refs_2_, f32[512,128]{1,0:T(8,128)} %broadcast_in_dim.2.refs_2_.refs_3_, f32[1,1024]{1,0:T(1,128)} %bitcast.25, bf16[256,1024]{1,0:T(8,128)(2,1)} %copy-done.4, ...), custom_call_target="tpu_custom_call" | custom-call | tf_op jit(solution)/shard_map/pair/pallas_call | solution.py:406
  (42 shorter events, 0.1 us)
Async XLA Ops:
  0.0 28.3 %copy-start = (f32[128]{0:T(128)S(1)}, f32[128]{0:T(128)}, u32[]{:S(2)}) copy-start(f32[128]{0:T(128)} %param.13) | copy-start | bytes 1540
  8.6 11.6 %copy-start.9 = (bf16[16,2048]{1,0:T(8,128)(2,1)S(1)}, bf16[16,2048]{1,0:T(8,128)(2,1)}, u32[]{:S(2)}) copy-start(bf16[16,2048]{1,0:T(8,128)(2,1)} %param.10) | copy-start | bytes 196612
  8.6 16.6 %copy-start.10 = (s32[4]{0:T(128)S(1)}, s32[4]{0:T(128)}, u32[]{:S(2)}) copy-start(s32[4]{0:T(128)} %order_ref.1) | copy-start | bytes 52
  8.6 19.7 %copy-start.12 = (s32[128]{0:T(128)S(1)}, s32[128]{0:T(128)}, u32[]{:S(2)}) copy-start(s32[128]{0:T(128)} %param.11) | copy-start | bytes 1540
  8.6 23.1 %copy-start.11 = (f32[512]{0:T(512)S(1)}, f32[512]{0:T(512)}, u32[]{:S(2)}) copy-start(f32[512]{0:T(512)} %param.14) | copy-start | bytes 6148
  8.6 46.4 %all-to-all-start = ((bf16[128,16,512]{2,1,0:T(8,128)(2,1)}), bf16[128,16,512]{2,1,0:T(8,128)(2,1)S(1)}, u32[]{:S(2)}, u32[]{:S(2)}) async-start(bf16[128,16,512]{2,1,0:T(8,128)(2,1)} %get-tuple-element.18), calls=%async_computation | async-start | bytes 4194304 | tf_op jit(solution)/shard_map/all_to_all | solution.py:446
  20.2 22.9 %collective-permute-start = (bf16[16,2048]{1,0:T(8,128)(2,1)S(1)}, bf16[16,2048]{1,0:T(8,128)(2,1)S(1)}, u32[]{:S(2)}, u32[]{:S(2)}) collective-permute-start(bf16[16,2048]{1,0:T(8,128)(2,1)S(1)} %copy-done.9), channel_id=1, source_target_pairs={{0,1},{8,40},{1,16},{9,41},{16,17},{24,56},{17,0},{25,57},{32,33},... | collective-permute-start | bytes 196616 | tf_op jit(solution)/shard_map/ppermute | solution.py:37
  21.6 24.9 %collective-permute-start.1 = (bf16[16,2048]{1,0:T(8,128)(2,1)S(1)}, bf16[16,2048]{1,0:T(8,128)(2,1)S(1)}, u32[]{:S(2)}, u32[]{:S(2)}) collective-permute-start(bf16[16,2048]{1,0:T(8,128)(2,1)S(1)} %copy-done.9), channel_id=1, source_target_pairs={{0,16},{8,72},{1,17},{9,73},{16,0},{24,88},{17,1},{25,89},{32,48},... | collective-permute-start | bytes 196616 | tf_op jit(solution)/shard_map/ppermute | solution.py:37
  24.0 23.1 %collective-permute-start.2 = (bf16[16,2048]{1,0:T(8,128)(2,1)S(1)}, bf16[16,2048]{1,0:T(8,128)(2,1)S(1)}, u32[]{:S(2)}, u32[]{:S(2)}) collective-permute-start(bf16[16,2048]{1,0:T(8,128)(2,1)S(1)} %copy-done.9), channel_id=1, source_target_pairs={{0,17},{8,104},{1,0},{9,105},{16,1},{24,120},{17,16},{25,121},{32,... | collective-permute-start | bytes 196616 | tf_op jit(solution)/shard_map/ppermute | solution.py:37
  47.8 9.2 %collective-permute-start.3 = (bf16[64,2048]{1,0:T(8,128)(2,1)}, bf16[64,2048]{1,0:T(8,128)(2,1)S(1)}, u32[]{:S(2)}, u32[]{:S(2)}) collective-permute-start(bf16[64,2048]{1,0:T(8,128)(2,1)} %get-tuple-element.31), channel_id=1, source_target_pairs={{0,2},{8,9},{1,3},{9,24},{16,18},{24,25},{17,19},{25,8},{32,34},{4... | collective-permute-start | bytes 786440 | tf_op jit(solution)/shard_map/ppermute | solution.py:37
  49.2 10.0 %collective-permute-start.4 = (bf16[64,2048]{1,0:T(8,128)(2,1)}, bf16[64,2048]{1,0:T(8,128)(2,1)}, u32[]{:S(2)}, u32[]{:S(2)}) collective-permute-start(bf16[64,2048]{1,0:T(8,128)(2,1)} %get-tuple-element.31), channel_id=1, source_target_pairs={{0,4},{8,24},{1,5},{9,25},{16,20},{24,8},{17,21},{25,9},{32,36},{4... | collective-permute-start | bytes 786440 | tf_op jit(solution)/shard_map/ppermute | solution.py:37
  54.0 6.2 %collective-permute-start.5 = (bf16[64,2048]{1,0:T(8,128)(2,1)}, bf16[64,2048]{1,0:T(8,128)(2,1)}, u32[]{:S(2)}, u32[]{:S(2)}) collective-permute-start(bf16[64,2048]{1,0:T(8,128)(2,1)} %get-tuple-element.31), channel_id=1, source_target_pairs={{0,6},{8,25},{1,7},{9,8},{16,22},{24,9},{17,23},{25,24},{32,38},{4... | collective-permute-start | bytes 786440 | tf_op jit(solution)/shard_map/ppermute | solution.py:37
  55.1 37.7 %copy-start.1 = (bf16[128,16,512]{2,1,0:T(8,128)(2,1)}, bf16[128,16,512]{2,1,0:T(8,128)(2,1)S(1)}, u32[]{:S(2)}) copy-start(bf16[128,16,512]{2,1,0:T(8,128)(2,1)S(1)} %all-to-all-done) | copy-start | bytes 6291460
  56.0 42.6 %collective-permute-start.13 = (bf16[2048,512]{1,0:T(8,128)(2,1)S(1)}, bf16[2048,512]{1,0:T(8,128)(2,1)}, u32[]{:S(2)}, u32[]{:S(2)}) collective-permute-start(bf16[2048,512]{1,0:T(8,128)(2,1)S(1)} %bitcast.20), channel_id=1, source_target_pairs={{0,8},{8,0},{1,9},{9,1},{16,24},{24,16},{17,25},{25,17},{32,40},{4... | collective-permute-start | bytes 6291464 | tf_op jit(solution)/shard_map/ppermute | solution.py:42
  61.2 31.6 %copy-start.2 = (bf16[256,2048]{1,0:T(8,128)(2,1)}, bf16[256,2048]{1,0:T(8,128)(2,1)S(1)}, u32[]{:S(2)}) copy-start(bf16[256,2048]{1,0:T(8,128)(2,1)S(1)} %constant_dynamic-update-slice_fusion.4.refs_0_.refs_4_) | copy-start | bytes 3145732
  61.2 15.6 %collective-permute-start.6 = (bf16[256,2048]{1,0:T(8,128)(2,1)S(1)}, bf16[256,2048]{1,0:T(8,128)(2,1)}, u32[]{:S(2)}, u32[]{:S(2)}) collective-permute-start(bf16[256,2048]{1,0:T(8,128)(2,1)S(1)} %constant_dynamic-update-slice_fusion.4.refs_0_.refs_4_), channel_id=1, source_target_pairs={{0,32},{8,10},{1,33},{9,11},{16,48},{24,26},{17,49},{25,27},{32,64... | collective-permute-start | bytes 3145736 | tf_op jit(solution)/shard_map/ppermute | solution.py:37
  62.9 26.3 %collective-permute-start.7 = (bf16[256,2048]{1,0:T(8,128)(2,1)S(1)}, bf16[256,2048]{1,0:T(8,128)(2,1)}, u32[]{:S(2)}, u32[]{:S(2)}) collective-permute-start(bf16[256,2048]{1,0:T(8,128)(2,1)S(1)} %constant_dynamic-update-slice_fusion.4.refs_0_.refs_4_), channel_id=1, source_target_pairs={{0,64},{8,12},{1,65},{9,13},{16,80},{24,28},{17,81},{25,29},{32,96... | collective-permute-start | bytes 3145736 | tf_op jit(solution)/shard_map/ppermute | solution.py:37
  65.4 27.4 %collective-permute-start.8 = (bf16[256,2048]{1,0:T(8,128)(2,1)S(1)}, bf16[256,2048]{1,0:T(8,128)(2,1)}, u32[]{:S(2)}, u32[]{:S(2)}) collective-permute-start(bf16[256,2048]{1,0:T(8,128)(2,1)S(1)} %constant_dynamic-update-slice_fusion.4.refs_0_.refs_4_), channel_id=1, source_target_pairs={{0,96},{8,14},{1,97},{9,15},{16,112},{24,30},{17,113},{25,31},{32,... | collective-permute-start | bytes 3145736 | tf_op jit(solution)/shard_map/ppermute | solution.py:37
  66.5 43.1 %collective-permute-start.9 = (bf16[256,2048]{1,0:T(8,128)(2,1)S(1)}, bf16[256,2048]{1,0:T(8,128)(2,1)}, u32[]{:S(2)}, u32[]{:S(2)}) collective-permute-start(bf16[256,2048]{1,0:T(8,128)(2,1)S(1)} %constant_dynamic-update-slice_fusion.4.refs_0_.refs_4_), channel_id=1, source_target_pairs={{0,8},{8,0},{1,9},{9,1},{16,24},{24,16},{17,25},{25,17},{32,40},{4... | collective-permute-start | bytes 3145736 | tf_op jit(solution)/shard_map/ppermute | solution.py:42
  76.8 32.9 %collective-permute-start.10 = (bf16[256,2048]{1,0:T(8,128)(2,1)}, bf16[256,2048]{1,0:T(8,128)(2,1)}, u32[]{:S(2)}, u32[]{:S(2)}) collective-permute-start(bf16[256,2048]{1,0:T(8,128)(2,1)} %collective-permute-done.6.refs_1_.refs_5_), channel_id=1, source_target_pairs={{0,8},{8,0},{1,9},{9,1},{16,24},{24,16},{17,25},{25,17},{32,40},{4... | collective-permute-start | bytes 3145736 | tf_op jit(solution)/shard_map/ppermute | solution.py:42
  89.2 21.0 %collective-permute-start.11 = (bf16[256,2048]{1,0:T(8,128)(2,1)}, bf16[256,2048]{1,0:T(8,128)(2,1)}, u32[]{:S(2)}, u32[]{:S(2)}) collective-permute-start(bf16[256,2048]{1,0:T(8,128)(2,1)} %collective-permute-done.7.refs_2_.refs_6_), channel_id=1, source_target_pairs={{0,8},{8,0},{1,9},{9,1},{16,24},{24,16},{17,25},{25,17},{32,40},{4... | collective-permute-start | bytes 3145736 | tf_op jit(solution)/shard_map/ppermute | solution.py:42
  92.8 17.8 %collective-permute-start.12 = (bf16[256,2048]{1,0:T(8,128)(2,1)}, bf16[256,2048]{1,0:T(8,128)(2,1)}, u32[]{:S(2)}, u32[]{:S(2)}) collective-permute-start(bf16[256,2048]{1,0:T(8,128)(2,1)} %collective-permute-done.8.refs_3_.refs_7_), channel_id=1, source_target_pairs={{0,8},{8,0},{1,9},{9,1},{16,24},{24,16},{17,25},{25,17},{32,40},{4... | collective-permute-start | bytes 3145736 | tf_op jit(solution)/shard_map/ppermute | solution.py:42
  92.8 54.4 %all-to-all-start.1 = ((bf16[128,16,512]{2,1,0:T(8,128)(2,1)}), bf16[128,16,512]{2,1,0:T(8,128)(2,1)}, u32[]{:S(2)}, u32[]{:S(2)}) async-start(bf16[128,16,512]{2,1,0:T(8,128)(2,1)} %get-tuple-element.20), calls=%async_computation.1 | async-start | bytes 4194304 | tf_op jit(solution)/shard_map/all_to_all | solution.py:447
  108.2 4.6 %collective-permute-start.14 = (bf16[256,1024]{1,0:T(8,128)(2,1)}, bf16[256,1024]{1,0:T(8,128)(2,1)S(1)}, u32[]{:S(2)}, u32[]{:S(2)}) collective-permute-start(bf16[256,1024]{1,0:T(8,128)(2,1)} %get-tuple-element.24.refs_12_), channel_id=1, source_target_pairs={{0,8},{8,0},{1,9},{9,1},{16,24},{24,16},{17,25},{25,17},{32,40},{4... | collective-permute-start | bytes 1572872 | tf_op jit(solution)/shard_map/ppermute | solution.py:42
  109.6 3.2 %collective-permute-start.15 = (bf16[256,1024]{1,0:T(8,128)(2,1)}, bf16[256,1024]{1,0:T(8,128)(2,1)S(1)}, u32[]{:S(2)}, u32[]{:S(2)}) collective-permute-start(bf16[256,1024]{1,0:T(8,128)(2,1)} %get-tuple-element.25.refs_14_), channel_id=1, source_target_pairs={{0,8},{8,0},{1,9},{9,1},{16,24},{24,16},{17,25},{25,17},{32,40},{4... | collective-permute-start | bytes 1572872 | tf_op jit(solution)/shard_map/ppermute | solution.py:42
  109.7 5.8 %collective-permute-start.16 = (bf16[256,1024]{1,0:T(8,128)(2,1)}, bf16[256,1024]{1,0:T(8,128)(2,1)S(1)}, u32[]{:S(2)}, u32[]{:S(2)}) collective-permute-start(bf16[256,1024]{1,0:T(8,128)(2,1)} %get-tuple-element.26.refs_16_), channel_id=1, source_target_pairs={{0,8},{8,0},{1,9},{9,1},{16,24},{24,16},{17,25},{25,17},{32,40},{4... | collective-permute-start | bytes 1572872 | tf_op jit(solution)/shard_map/ppermute | solution.py:42
  110.1 24.9 %collective-permute-start.18 = (bf16[256,1024]{1,0:T(8,128)(2,1)}, bf16[256,1024]{1,0:T(8,128)(2,1)S(1)}, u32[]{:S(2)}, u32[]{:S(2)}) collective-permute-start(bf16[256,1024]{1,0:T(8,128)(2,1)} %get-tuple-element.24.refs_12_), channel_id=1, source_target_pairs={{0,32},{8,40},{1,33},{9,41},{16,48},{24,56},{17,49},{25,57},{32,64... | collective-permute-start | bytes 1572872 | tf_op jit(solution)/shard_map/ppermute | solution.py:37
  110.6 25.3 %collective-permute-start.20 = (bf16[256,1024]{1,0:T(8,128)(2,1)}, bf16[256,1024]{1,0:T(8,128)(2,1)S(1)}, u32[]{:S(2)}, u32[]{:S(2)}) collective-permute-start(bf16[256,1024]{1,0:T(8,128)(2,1)} %get-tuple-element.26.refs_16_), channel_id=1, source_target_pairs={{0,96},{8,104},{1,97},{9,105},{16,112},{24,120},{17,113},{25,121},... | collective-permute-start | bytes 1572872 | tf_op jit(solution)/shard_map/ppermute | solution.py:37
  112.8 34.3 %copy-start.3 = (bf16[256,1024]{1,0:T(8,128)(2,1)}, bf16[256,1024]{1,0:T(8,128)(2,1)S(1)}, u32[]{:S(2)}) copy-start(bf16[256,1024]{1,0:T(8,128)(2,1)S(1)} %collective-permute-done.14.refs_13_) | copy-start | bytes 1572868
  112.8 33.4 %collective-permute-start.22 = (bf16[256,1024]{1,0:T(8,128)(2,1)}, bf16[256,1024]{1,0:T(8,128)(2,1)S(1)}, u32[]{:S(2)}, u32[]{:S(2)}) collective-permute-start(bf16[256,1024]{1,0:T(8,128)(2,1)} %get-tuple-element.25.refs_14_), channel_id=1, source_target_pairs={{0,32},{8,40},{1,33},{9,41},{16,48},{24,56},{17,49},{25,57},{32,64... | collective-permute-start | bytes 1572872 | tf_op jit(solution)/shard_map/ppermute | solution.py:37
  112.8 34.3 %copy-start.5 = (bf16[256,1024]{1,0:T(8,128)(2,1)}, bf16[256,1024]{1,0:T(8,128)(2,1)S(1)}, u32[]{:S(2)}) copy-start(bf16[256,1024]{1,0:T(8,128)(2,1)S(1)} %collective-permute-done.15.refs_15_) | copy-start | bytes 1572868
  112.9 34.0 %collective-permute-start.24 = (bf16[256,1024]{1,0:T(8,128)(2,1)}, bf16[256,1024]{1,0:T(8,128)(2,1)}, u32[]{:S(2)}, u32[]{:S(2)}) collective-permute-start(bf16[256,1024]{1,0:T(8,128)(2,1)} %get-tuple-element.27.refs_18_), channel_id=1, source_target_pairs={{0,96},{8,104},{1,97},{9,105},{16,112},{24,120},{17,113},{25,121},... | collective-permute-start | bytes 1572872 | tf_op jit(solution)/shard_map/ppermute | solution.py:37
  115.5 31.7 %copy-start.7 = (bf16[256,1024]{1,0:T(8,128)(2,1)}, bf16[256,1024]{1,0:T(8,128)(2,1)S(1)}, u32[]{:S(2)}) copy-start(bf16[256,1024]{1,0:T(8,128)(2,1)S(1)} %collective-permute-done.16.refs_17_) | copy-start | bytes 1572868
  115.5 31.7 %collective-permute-start.17 = (bf16[256,1024]{1,0:T(8,128)(2,1)}, bf16[256,1024]{1,0:T(8,128)(2,1)}, u32[]{:S(2)}, u32[]{:S(2)}) collective-permute-start(bf16[256,1024]{1,0:T(8,128)(2,1)} %get-tuple-element.27.refs_18_), channel_id=1, source_target_pairs={{0,8},{8,0},{1,9},{9,1},{16,24},{24,16},{17,25},{25,17},{32,40},{4... | collective-permute-start | bytes 1572872 | tf_op jit(solution)/shard_map/ppermute | solution.py:42
  135.0 26.9 %copy-start.4 = (bf16[256,1024]{1,0:T(8,128)(2,1)}, bf16[256,1024]{1,0:T(8,128)(2,1)S(1)}, u32[]{:S(2)}) copy-start(bf16[256,1024]{1,0:T(8,128)(2,1)S(1)} %collective-permute-done.18.refs_5_) | copy-start | bytes 1572868
  135.0 26.9 %collective-permute-start.19 = (bf16[256,1024]{1,0:T(8,128)(2,1)S(1)}, bf16[256,1024]{1,0:T(8,128)(2,1)}, u32[]{:S(2)}, u32[]{:S(2)}) collective-permute-start(bf16[256,1024]{1,0:T(8,128)(2,1)S(1)} %collective-permute-done.18.refs_5_), channel_id=1, source_target_pairs={{0,8},{8,0},{1,9},{9,1},{16,24},{24,16},{17,25},{25,17},{32,40},{4... | collective-permute-start | bytes 1572872 | tf_op jit(solution)/shard_map/ppermute | solution.py:42
  135.9 26.0 %copy-start.6 = (bf16[256,1024]{1,0:T(8,128)(2,1)}, bf16[256,1024]{1,0:T(8,128)(2,1)S(1)}, u32[]{:S(2)}) copy-start(bf16[256,1024]{1,0:T(8,128)(2,1)S(1)} %collective-permute-done.20.refs_7_) | copy-start | bytes 1572868
  135.9 26.1 %collective-permute-start.21 = (bf16[256,1024]{1,0:T(8,128)(2,1)S(1)}, bf16[256,1024]{1,0:T(8,128)(2,1)}, u32[]{:S(2)}, u32[]{:S(2)}) collective-permute-start(bf16[256,1024]{1,0:T(8,128)(2,1)S(1)} %collective-permute-done.20.refs_7_), channel_id=1, source_target_pairs={{0,8},{8,0},{1,9},{9,1},{16,24},{24,16},{17,25},{25,17},{32,40},{4... | collective-permute-start | bytes 1572872 | tf_op jit(solution)/shard_map/ppermute | solution.py:42
  146.2 15.7 %copy-start.8 = (bf16[256,1024]{1,0:T(8,128)(2,1)}, bf16[256,1024]{1,0:T(8,128)(2,1)S(1)}, u32[]{:S(2)}) copy-start(bf16[256,1024]{1,0:T(8,128)(2,1)S(1)} %collective-permute-done.22.refs_9_) | copy-start | bytes 1572868
  146.2 15.7 %collective-permute-start.23 = (bf16[256,1024]{1,0:T(8,128)(2,1)S(1)}, bf16[256,1024]{1,0:T(8,128)(2,1)}, u32[]{:S(2)}, u32[]{:S(2)}) collective-permute-start(bf16[256,1024]{1,0:T(8,128)(2,1)S(1)} %collective-permute-done.22.refs_9_), channel_id=1, source_target_pairs={{0,8},{8,0},{1,9},{9,1},{16,24},{24,16},{17,25},{25,17},{32,40},{4... | collective-permute-start | bytes 1572872 | tf_op jit(solution)/shard_map/ppermute | solution.py:42
  146.9 15.1 %collective-permute-start.25 = (bf16[256,1024]{1,0:T(8,128)(2,1)}, bf16[256,1024]{1,0:T(8,128)(2,1)}, u32[]{:S(2)}, u32[]{:S(2)}) collective-permute-start(bf16[256,1024]{1,0:T(8,128)(2,1)} %collective-permute-done.24.refs_11_), channel_id=1, source_target_pairs={{0,8},{8,0},{1,9},{9,1},{16,24},{24,16},{17,25},{25,17},{32,40},{4... | collective-permute-start | bytes 1572872 | tf_op jit(solution)/shard_map/ppermute | solution.py:42

commit v3 on v2

--- a/solution.py
+++ b/solution.py
@@ -115,10 +115,10 @@
         for t in range(4):
             for s in range(4):
                 tile = rows_of(t, 128 + s * 8 + v).astype(part.dtype)
-                for far in range(2):
-                    for z in range(2):
-                        owner = ((t // 2 + 2 * far) * 2 + z) * 2 + t % 2
-                        part[owner * 8 + v, :, s * 128:s * 128 + 128] = tile
+                at = slice(s % 2 * 128, s % 2 * 128 + 128)
+                for z in range(2):
+                    owner = ((t + 2 * z) % 4 * 2 + z) * 2 + s // 2
+                    part[owner * 8 + v, :, at] = tile
         return carry
 
     lax.fori_loop(0, 8, emit_partner, 0)
@@ -154,7 +154,7 @@
 
 def transformed(pair_order, owner_table, three_index, virt_coeff):
     vmem, hbm = pl.BlockSpec(memory_space=pltpu.VMEM), pl.BlockSpec(memory_space=pl.ANY)
-    part = jax.ShapeDtypeStruct((128, 16, 512), jnp.bfloat16)
+    part = jax.ShapeDtypeStruct((128, 16, 256), jnp.bfloat16)
     own = jax.ShapeDtypeStruct((128, 16, 512), jnp.bfloat16)
     return pl.pallas_call(
         half_kernel,
@@ -201,7 +201,7 @@
 
 
 def partner_kernel(table_ref, mine_ref, other_ref, *refs):
-    parts, outs, (rows, metric, sems, row_sems) = refs[:4], refs[4:8], refs[8:]
+    parts, outs, (rows, metric, sems, row_sems) = refs[:4], refs[4:7], refs[7:]
     core = table_ref[128]
     takes = [
         pltpu.make_async_copy(mine_ref, rows.at[core], row_sems.at[0]),
@@ -212,26 +212,25 @@
     place(table_ref, parts, 0, metric, sems)
     for take in takes:
         take.wait()
-    left = [rows[c].T for c in range(2)]
+    left = jnp.concatenate([rows[c].T for c in range(2)], axis=0)
     placed(parts, 0, metric, sems)
-    for c in range(2):
-        for block in range(2):
-            at = slice(block * 512, block * 512 + 512)
-            got = fitted(left[c], metric[at, :])
-            outs[2 * c][:, at] = got[:256]
-            outs[2 * c + 1][:, at] = got[256:]
+    for block in range(2):
+        at = slice(block * 512, block * 512 + 512)
+        got = fitted(left, metric[at, :])
+        outs[0][:, at] = got
+        outs[1][:, at] = got[:256]
+        outs[2][:, at] = got[256:]
 
 
 def partner_fit(table, mine, other, parts):
     smem, vmem = pl.BlockSpec(memory_space=pltpu.SMEM), pl.BlockSpec(memory_space=pltpu.VMEM)
-    shape = jax.ShapeDtypeStruct((256, 1024), jnp.bfloat16)
     return pl.pallas_call(
         partner_kernel,
         in_specs=[smem] + [pl.BlockSpec(memory_space=pl.ANY)] * 6,
-        out_specs=[vmem] * 4,
-        out_shape=[shape] * 4,
+        out_specs=[vmem] * 3,
+        out_shape=[jax.ShapeDtypeStruct((rows, 1024), jnp.bfloat16) for rows in (512, 256, 256)],
         scratch_shapes=[
-            pltpu.VMEM((2, 2048, 512), jnp.bfloat16),
+            pltpu.VMEM((2, 2048, 256), jnp.bfloat16),
             pltpu.VMEM((1024, 2048), jnp.bfloat16),
             pltpu.SemaphoreType.DMA((4,)),
             pltpu.SemaphoreType.DMA((2,)),
@@ -286,13 +285,10 @@
 def own_kernel(table_ref, rows_ref, row_ref, col_ref, *refs, sizes):
     count = 2 * sum(sizes)
     parts, pieces, refs = refs[:8], refs[8:8 + count], refs[8 + count:]
-    own_ref, total_ref, rows, metric, own, buf, total, sems, piece_sems, more = refs
-    take = pltpu.make_async_copy(rows_ref, rows, more.at[0])
-    take.start()
+    own_ref, total_ref, metric, own, buf, total, sems, piece_sems, more = refs
     place(table_ref, parts, 0, metric, sems)
     groups = fetch(grouped(pieces, sizes), buf, piece_sems)
-    take.wait()
-    left = rows[...].T
+    left = rows_ref[...].T
     for half in range(2):
         placed(parts[half * 4:half * 4 + 4], half * 4, metric, sems)
         for block in range(2):
@@ -334,14 +330,13 @@
 
     return pl.pallas_call(
         body,
-        in_specs=[smem, hbm, vmem, vmem] + [hbm] * (8 + len(pieces)),
+        in_specs=[smem, vmem, vmem, vmem] + [hbm] * (8 + len(pieces)),
         out_specs=[hbm] * 2,
         out_shape=[
             jax.ShapeDtypeStruct((512, 2048), jnp.bfloat16),
             jax.ShapeDtypeStruct((512, 2048), jnp.float32),
         ],
         scratch_shapes=[
-            pltpu.VMEM((2048, 512), jnp.bfloat16),
             pltpu.VMEM((2048, 2048), jnp.bfloat16),
             pltpu.VMEM((512, 2048), jnp.bfloat16),
             pltpu.VMEM((count, 2048), jnp.bfloat16),
@@ -354,7 +349,7 @@
     )(table, own, row, col, *parts, *pieces)
 
 
-def pair_kernel(table_ref, own_ref, total_ref, row_ref, col_ref, *refs, sizes):
+def pair_kernel(table_ref, own_ref, total_ref, row_ref, col_ref, *refs, sizes, final):
     count = 2 * sum(sizes)
     pieces, (out_ref, own, buf, before, total, piece_sems, more) = refs[:count], refs[count:]
     core = table_ref[128]
@@ -374,8 +369,10 @@
         def finished(chunk, last=index == len(groups) - 1):
             if last:
                 for tile in range(chunk * 4, chunk * 4 + 4):
-                    half = core if tile < 8 else 1 - core
-                    to = pl.multiple_of(((tile % 8) * 2 + half) * 128, 128)
+                    to = tile * 128
+                    if final:
+                        half = core if tile < 8 else 1 - core
+                        to = pl.multiple_of(((tile % 8) * 2 + half) * 128, 128)
                     sends.append(
                         pltpu.make_async_copy(
                             total.at[:, pl.ds(tile * 128, 128)],
@@ -393,7 +390,7 @@
         send.wait()
 
 
-def paired(table, own, total, row, col, groups):
+def paired(table, own, total, row, col, groups, final):
     smem, vmem = pl.BlockSpec(memory_space=pltpu.SMEM), pl.BlockSpec(memory_space=pltpu.VMEM)
     hbm = pl.BlockSpec(memory_space=pl.ANY)
     sizes = tuple(len(group) for group in groups)
@@ -401,7 +398,7 @@
     count = sum(piece.shape[0] for piece in pieces) // 2
 
     def body(*refs):
-        pair_kernel(*refs, sizes=sizes)
+        pair_kernel(*refs, sizes=sizes, final=final)
 
     return pl.pallas_call(
         body,
@@ -416,7 +413,7 @@
             pltpu.SemaphoreType.DMA((len(pieces),)),
             pltpu.SemaphoreType.DMA((18,)),
         ],
-        name="pair",
+        name="pair_last" if final else "pair",
     )(table, own, total, row, col, *pieces)
 
 
@@ -431,12 +428,15 @@
     partner_eps = jnp.concatenate(
         [lax.dynamic_slice_in_dim(eps, pair_order[s] * 8 + vir_idx, 1, 0) for s in range(4)]
     )
-    blocks = partner_eps[None, None, :, None] - vir_energy.reshape(2, 2, 1, 128)
-    odd = occ_idx // 4 % 2 == 1
-    near = jnp.where(odd, blocks[1], blocks[0])
-    far = jnp.where(odd, blocks[0], blocks[1])
-    far = far.reshape(2, 2, 2, 128).transpose(1, 0, 2, 3)
-    return row, near.reshape(1, 1024), far.reshape(1, 1024)
+    mine = (occ_idx // 4 + occ_idx // 2 % 2 * 2) % 4
+    virtuals = jnp.concatenate([vir_energy, vir_energy]).reshape(8, 128)
+    virtuals = lax.dynamic_slice_in_dim(virtuals, mine, 4, 0)
+    near = partner_eps[:, None] - virtuals[:1]
+    beside = partner_eps[None, :, None] - jnp.stack([virtuals[3], virtuals[1]])[:, None, :]
+    across = partner_eps[:, None] - virtuals[2:3]
+    first = beside[:, :2].reshape(1, 512)
+    second = jnp.concatenate([beside[:, 2:].reshape(1, 512), across.reshape(1, 512)], axis=1)
+    return row, near.reshape(1, 512), first, second
 
 
 def whole(three_index, virt_coeff, metric_root, owner_table, pair_order, occ_energy, vir_energy):
@@ -445,26 +445,28 @@
     part, own = transformed(pair_order, owner_table, three_index, virt_coeff)
     part = lax.all_to_all(part, AXES, split_axis=0, concat_axis=0, tiled=True)
     own = lax.all_to_all(own, AXES, split_axis=0, concat_axis=0, tiled=True)
-    part, own = part.reshape(2048, 512), own.reshape(2048, 512)
-
-    row, near, far = energies(me, owner_table, pair_order, occ_energy, vir_energy)
+    part, own = part.reshape(2048, 256), own.reshape(2048, 512)
+
+    energy = energies(me, owner_table, pair_order, occ_energy, vir_energy)
     table = lax.dynamic_slice_in_dim(jnp.asarray(metric_table()), me, 1, 0).reshape(129)
-    part, row, near, far, table = lax.optimization_barrier((part, row, near, far, table))
+    part, table, *energy = lax.optimization_barrier((part, table, *energy))
+    row, near, first, second = energy
     other = swapped(part)
-    here = partner_fit(table, part, other, mine_parts)
-
-    there = []
-    for i, by in ((0, 1), (2, 3), (1, 1), (3, 3)):
-        there.append(shifted(here[i], ("y", "y"), by))
+    here, *halves = partner_fit(table, part, other, mine_parts)
 
     def whole_rows(part):
         return part, swapped(part)
 
-    here, there = [whole_rows(part) for part in here], [whole_rows(part) for part in there]
-    own, density = own_and_pair(
-        table, own, row, near, mine_parts + other_parts, [here[:2], here[2:]]
-    )
-    density = paired(table, own, density, row, far, [there[:2], there[2:]])
+    beside = []
+    for half in range(2):
+        beside.append([shifted(halves[half], ("y", "y"), by) for by in (1, 3)])
+    across = shifted(here, ("z", "z"), 2)
+    here = whole_rows(here)
+    beside = [[whole_rows(part) for part in beside[i]] for i in range(2)]
+    across = whole_rows(across)
+    own, density = own_and_pair(table, own, row, near, mine_parts + other_parts, [[here]])
+    density = paired(table, own, density, row, first, [beside[0]], False)
+    density = paired(table, own, density, row, second, [beside[1], [across]], True)
     return density.reshape(8, 64, 2048)
 
 

time: 173 us -> 176 us (1.017)
  waiting for transfers between devices: 59.4 us -> 71.9 us
  starting transfers between devices: 54.7 us -> 42.9 us
  Pallas kernels: 42.6 us -> 44.6 us
    ppermute x13 -> x14, waiting for transfers between devices: 59.3 us -> 71.8 us  [shifted(): return lax.ppermute(value, AXES, pairs)]
    ppermute x13 -> x11, starting transfers between devices: 16.4 us -> 5.67 us  [swapped(): return lax.ppermute(value, AXES, pairs)]
    pallas_call x1 -> x2, Pallas kernels: 9.86 us -> 16.6 us  [paired(): pl.pallas_call(body, in_specs=[smem, hbm, hbm, vmem, vmem] + [hbm] * len(...]
    pallas_call x1, Pallas kernels: 9.54 us -> 7.11 us  [partner_fit(): pl.pallas_call(partner_kernel, in_specs=[smem] + [pl.BlockSpec(memory_spa...]
    all_to_all x1, starting transfers between devices: 11.5 us -> 9.17 us  [whole(): part = lax.all_to_all(part, AXES, split_axis=0, concat_axis=0, tiled=True)]
    pallas_call x1, Pallas kernels: 14.7 us -> 12.4 us  [own_and_pair(): pl.pallas_call(body, in_specs=[smem, vmem, vmem, vmem] + [hbm] * (8 + len...]
    unnamed x31 -> x27, local copies, waits for them, and re-layouts: 2.96 us -> 4.43 us
    ppermute x13 -> x14, starting transfers between devices: 21 us -> 22.4 us  [shifted(): return lax.ppermute(value, AXES, pairs)]
  transfers between devices with their start and end apart: 28 -> 27, of which waited for: 7 -> 9; matrix products, arithmetic and copies ran while one was open for 7% -> 5% of each run, Pallas kernels for 14% -> 20%
where the time goes in v3:
time: 176 us
  waiting for transfers between devices  71.9 us (41%)
  Pallas kernels  44.6 us (25%)
  starting transfers between devices  42.9 us (24%)
  local copies, waits for them, and re-layouts  8.86 us (5%)
  other arithmetic  3.98 us (2%)
  between operations  3.1 us (2%)
    ppermute x14, waiting for transfers between devices, shifted(): return lax.ppermute(value, AXES, pairs)  71.8 us
    ppermute x14, starting transfers between devices, shifted(): return lax.ppermute(value, AXES, pairs)  22.4 us
    pallas_call x2, Pallas kernels, paired(): pl.pallas_call(body, in_specs=[smem, hbm, hbm, vmem, vmem] + [hbm] * len(...  16.6 us
    pallas_call x1, Pallas kernels, own_and_pair(): pl.pallas_call(body, in_specs=[smem, vmem, vmem, vmem] + [hbm] * (8 + len...  12.4 us
    all_to_all x1, starting transfers between devices, whole(): part = lax.all_to_all(part, AXES, split_axis=0, concat_axis=0, tiled=True)  9.17 us
    pallas_call x1, Pallas kernels, transformed(): pl.pallas_call(half_kernel, in_specs=[pl.BlockSpec(memory_space=pltpu.SME...  8.47 us
    pallas_call x1, Pallas kernels, partner_fit(): pl.pallas_call(partner_kernel, in_specs=[smem] + [pl.BlockSpec(memory_spa...  7.11 us
    ppermute x11, starting transfers between devices, swapped(): return lax.ppermute(value, AXES, pairs)  5.67 us
  transfers between devices with their start and end apart: 27, of which 9 were waited for; matrix products, arithmetic and copies ran while one was open for 5% of the time, Pallas kernels for 20%

profile of v3, /device:TPU:1, one launch (start us, length us, event | category | flops | bytes accessed | tf_op | source)
XLA Modules:
  0.0 175.5 jit_solution(2042751590483670631)
XLA Ops:
  0.0 2.1 %collective-permute-start = (bf16[16,2048]{1,0:T(8,128)(2,1)}, bf16[16,2048]{1,0:T(8,128)(2,1)S(1)}, u32[]{:S(2)}, u32[]{:S(2)}) collective-permute-start(bf16[16,2048]{1,0:T(8,128)(2,1)} %param.10), channel_id=1, source_target_pairs={{0,1},{8,40},{1,16},{9,41},{16,17},{24,56},{17,0},{25,57},{32,33},... | collective-permute-start | bytes 196616 | tf_op jit(solution)/shard_map/ppermute | solution.py:37
  2.1 2.6 %collective-permute-start.1 = (bf16[16,2048]{1,0:T(8,128)(2,1)}, bf16[16,2048]{1,0:T(8,128)(2,1)S(1)}, u32[]{:S(2)}, u32[]{:S(2)}) collective-permute-start(bf16[16,2048]{1,0:T(8,128)(2,1)} %param.10), channel_id=1, source_target_pairs={{0,16},{8,72},{1,17},{9,73},{16,0},{24,88},{17,1},{25,89},{32,48},... | collective-permute-start | bytes 196616 | tf_op jit(solution)/shard_map/ppermute | solution.py:37
  4.7 1.1 collective-permute-start.2
  5.8 8.5 %half.1 = (bf16[128,16,256]{2,1,0:T(8,128)(2,1)}, bf16[128,16,512]{2,1,0:T(8,128)(2,1)}) custom-call(s32[4]{0:T(128)} %order_ref.1, s32[1,128]{1,0:T(1,128)} %bitcast.35, bf16[16,128,640]{2,1,0:T(8,128)(2,1)} %ints_ref.1, bf16[640,512]{1,0:T(8,128)(2,1)} %coeff_ref.1), custom_call_target="tpu_custom_call" | custom-call | tf_op jit(solution)/shard_map/half/pallas_call | solution.py:159
  14.3 9.2 %all-to-all-start = ((bf16[128,16,256]{2,1,0:T(8,128)(2,1)}), bf16[128,16,256]{2,1,0:T(8,128)(2,1)S(1)}, u32[]{:S(2)}, u32[]{:S(2)}) async-start(bf16[128,16,256]{2,1,0:T(8,128)(2,1)} %get-tuple-element.18), calls=%async_computation | async-start | bytes 2097152 | tf_op jit(solution)/shard_map/all_to_all | solution.py:446
  23.6 0.7 fusion.4
  26.8 0.2 convolution_bitcast_fusion
  27.1 0.7 fusion.3
  27.8 2.5 %pad_maximum_fusion.3 = f32[4]{0:T(128)S(1)} fusion(f32[1]{0:T(128)} %get-tuple-element.48, f32[1]{0:T(128)} %get-tuple-element.49, f32[1]{0:T(128)} %get-tuple-element.50, f32[1]{0:T(128)} %get-tuple-element.47), kind=kLoop, calls=%fused_computation.21 | loop fusion | flops 12 | bytes 32 | tf_op jit(solution)/shard_map/concatenate | solution.py:428
  30.3 0.1 broadcast_subtract_fusion
  30.4 0.1 dynamic_slice.26
  30.5 0.1 dynamic_slice.25
  30.6 0.0 collective-permute-done.1
  30.6 0.0 collective-permute-done.2
  30.6 1.6 collective-permute-start.3
  32.2 0.1 broadcast_subtract_fusion.1
  32.3 2.9 %collective-permute-start.4 = (bf16[64,2048]{1,0:T(8,128)(2,1)S(1)}, bf16[64,2048]{1,0:T(8,128)(2,1)S(1)}, u32[]{:S(2)}, u32[]{:S(2)}) collective-permute-start(bf16[64,2048]{1,0:T(8,128)(2,1)S(1)} %get-tuple-element.31), channel_id=1, source_target_pairs={{0,4},{8,24},{1,5},{9,25},{16,20},{24,8},{17,21},{25,9},{32,36},{4... | collective-permute-start | bytes 786440 | tf_op jit(solution)/shard_map/ppermute | solution.py:37
  35.2 1.2 constant_dynamic-slice_fusion.1
  36.4 0.1 sub.95
  36.5 0.9 collective-permute-start.5
  37.4 5.7 %collective-permute-done.3 = bf16[64,2048]{1,0:T(8,128)(2,1)S(1)} collective-permute-done((bf16[64,2048]{1,0:T(8,128)(2,1)S(1)}, bf16[64,2048]{1,0:T(8,128)(2,1)S(1)}, u32[]{:S(2)}, u32[]{:S(2)}) %collective-permute-start.3) | collective-permute-done | bytes 262176 | tf_op jit(solution)/shard_map/ppermute | solution.py:37
  43.1 2.6 %collective-permute-done.4 = bf16[64,2048]{1,0:T(8,128)(2,1)S(1)} collective-permute-done((bf16[64,2048]{1,0:T(8,128)(2,1)S(1)}, bf16[64,2048]{1,0:T(8,128)(2,1)S(1)}, u32[]{:S(2)}, u32[]{:S(2)}) %collective-permute-start.4) | collective-permute-done | bytes 262176 | tf_op jit(solution)/shard_map/ppermute | solution.py:37
  45.7 0.0 collective-permute-done.5
  45.7 1.0 collective-permute-start.6
  46.8 0.6 broadcast_subtract_fusion.2
  47.4 0.6 fusion.2
  48.0 0.6 pad_maximum_fusion.1.refs_4_
  48.6 2.6 %collective-permute-start.7 = (bf16[256,2048]{1,0:T(8,128)(2,1)S(1)}, bf16[256,2048]{1,0:T(8,128)(2,1)}, u32[]{:S(2)}, u32[]{:S(2)}) collective-permute-start(bf16[256,2048]{1,0:T(8,128)(2,1)S(1)} %constant_dynamic-update-slice_fusion.4.refs_0_.refs_4_), channel_id=1, source_target_pairs={{0,64},{8,12},{1,65},{9,13},{16,80},{24,28},{17,81},{25,29},{32,96... | collective-permute-start | bytes 3145736 | tf_op jit(solution)/shard_map/ppermute | solution.py:37
  51.2 0.9 collective-permute-start.8
  52.1 0.0 all-to-all-done
  52.1 1.0 broadcast_in_dim.2.refs_2_.refs_3_
  53.1 0.5 collective-permute-start.9
  53.6 7.5 %collective-permute-done.6.refs_1_.refs_5_ = bf16[256,2048]{1,0:T(8,128)(2,1)} collective-permute-done((bf16[256,2048]{1,0:T(8,128)(2,1)S(1)}, bf16[256,2048]{1,0:T(8,128)(2,1)}, u32[]{:S(2)}, u32[]{:S(2)}) %collective-permute-start.6) | collective-permute-done | bytes 1048608 | tf_op jit(solution)/shard_map/ppermute | solution.py:37
  61.1 0.0 collective-permute-start.10
  61.1 11.8 %collective-permute-done.7.refs_2_.refs_6_ = bf16[256,2048]{1,0:T(8,128)(2,1)} collective-permute-done((bf16[256,2048]{1,0:T(8,128)(2,1)S(1)}, bf16[256,2048]{1,0:T(8,128)(2,1)}, u32[]{:S(2)}, u32[]{:S(2)}) %collective-permute-start.7) | collective-permute-done | bytes 1048608 | tf_op jit(solution)/shard_map/ppermute | solution.py:37
  72.9 0.0 collective-permute-start.11
  72.9 1.6 collective-permute-done.8.refs_3_.refs_7_
  74.5 0.0 collective-permute-start.12
  74.5 0.0 collective-permute-done.13.other_ref
  74.5 1.0 copy-done.5
  75.5 7.1 %fit_partner.1 = (bf16[512,1024]{1,0:T(8,128)(2,1)}, bf16[256,1024]{1,0:T(8,128)(2,1)}, bf16[256,1024]{1,0:T(8,128)(2,1)}) custom-call(s32[129]{0:T(256)} %bitcast.26, bf16[2048,256]{1,0:T(8,128)(2,1)} %bitcast.25, bf16[2048,256]{1,0:T(8,128)(2,1)} %copy-done.5, bf16[256,2048]{1,0:T(8,128)(2,1)} %copy-done.2, ...), custom_call_target="tpu_custom_call" | custom-call | tf_op jit(solution)/shard_map/fit_partner/pallas_call | solution.py:227
  82.6 3.1 %collective-permute-start.23 = (bf16[512,1024]{1,0:T(8,128)(2,1)}, bf16[512,1024]{1,0:T(8,128)(2,1)}, u32[]{:S(2)}, u32[]{:S(2)}) collective-permute-start(bf16[512,1024]{1,0:T(8,128)(2,1)} %get-tuple-element.24.refs_12_), channel_id=1, source_target_pairs={{0,16},{8,24},{1,17},{9,25},{16,0},{24,8},{17,1},{25,9},{32,48},{4... | collective-permute-start | bytes 3145736 | tf_op jit(solution)/shard_map/ppermute | solution.py:37
  85.7 5.7 %all-to-all-start.1 = ((bf16[128,16,512]{2,1,0:T(8,128)(2,1)}), bf16[128,16,512]{2,1,0:T(8,128)(2,1)S(1)}, u32[]{:S(2)}, u32[]{:S(2)}) async-start(bf16[128,16,512]{2,1,0:T(8,128)(2,1)} %get-tuple-element.20), calls=%async_computation.1 | async-start | bytes 4194304 | tf_op jit(solution)/shard_map/all_to_all | solution.py:447
  91.4 0.0 collective-permute-done.9.refs_8_
  91.4 1.4 collective-permute-start.15
  92.8 0.0 collective-permute-done.10.refs_9_
  92.8 0.7 collective-permute-start.14
  93.5 2.0 %collective-permute-start.17 = (bf16[256,1024]{1,0:T(8,128)(2,1)}, bf16[256,1024]{1,0:T(8,128)(2,1)}, u32[]{:S(2)}, u32[]{:S(2)}) collective-permute-start(bf16[256,1024]{1,0:T(8,128)(2,1)} %get-tuple-element.28), channel_id=1, source_target_pairs={{0,96},{8,104},{1,97},{9,105},{16,112},{24,120},{17,113},{25,121},... | collective-permute-start | bytes 1572872 | tf_op jit(solution)/shard_map/ppermute | solution.py:37
  95.5 32.7 %collective-permute-done.15.refs_5_ = bf16[256,1024]{1,0:T(8,128)(2,1)} collective-permute-done((bf16[256,1024]{1,0:T(8,128)(2,1)}, bf16[256,1024]{1,0:T(8,128)(2,1)}, u32[]{:S(2)}, u32[]{:S(2)}) %collective-permute-start.15) | collective-permute-done | bytes 524320 | tf_op jit(solution)/shard_map/ppermute | solution.py:37
  128.2 0.2 collective-permute-start.21
  128.4 2.1 %collective-permute-done.23.refs_9_ = bf16[512,1024]{1,0:T(8,128)(2,1)} collective-permute-done((bf16[512,1024]{1,0:T(8,128)(2,1)}, bf16[512,1024]{1,0:T(8,128)(2,1)}, u32[]{:S(2)}, u32[]{:S(2)}) %collective-permute-start.23) | collective-permute-done | bytes 1048608 | tf_op jit(solution)/shard_map/ppermute | solution.py:37
  130.4 2.0 %collective-permute-start.24 = (bf16[512,1024]{1,0:T(8,128)(2,1)}, bf16[512,1024]{1,0:T(8,128)(2,1)S(1)}, u32[]{:S(2)}, u32[]{:S(2)}) collective-permute-start(bf16[512,1024]{1,0:T(8,128)(2,1)} %collective-permute-done.23.refs_9_), channel_id=1, source_target_pairs={{0,8},{8,0},{1,9},{9,1},{16,24},{24,16},{17,25},{25,17},{32,40},{4... | collective-permute-start | bytes 3145736 | tf_op jit(solution)/shard_map/ppermute | solution.py:42
  132.4 0.0 collective-permute-start.16
  132.4 7.0 %collective-permute-done.19.refs_5_ = bf16[256,1024]{1,0:T(8,128)(2,1)} collective-permute-done((bf16[256,1024]{1,0:T(8,128)(2,1)}, bf16[256,1024]{1,0:T(8,128)(2,1)}, u32[]{:S(2)}, u32[]{:S(2)}) %collective-permute-start.19) | collective-permute-done | bytes 524320 | tf_op jit(solution)/shard_map/ppermute | solution.py:37
  139.4 0.7 collective-permute-start.18
  140.1 1.0 collective-permute-done.21.refs_7_
  141.1 1.8 %collective-permute-start.20 = (bf16[256,1024]{1,0:T(8,128)(2,1)}, bf16[256,1024]{1,0:T(8,128)(2,1)}, u32[]{:S(2)}, u32[]{:S(2)}) collective-permute-start(bf16[256,1024]{1,0:T(8,128)(2,1)} %collective-permute-done.19.refs_5_), channel_id=1, source_target_pairs={{0,8},{8,0},{1,9},{9,1},{16,24},{24,16},{17,25},{25,17},{32,40},{4... | collective-permute-start | bytes 1572872 | tf_op jit(solution)/shard_map/ppermute | solution.py:42
  142.9 1.0 copy-done.6
  143.9 0.0 collective-permute-start.22
  143.9 1.3 copy-done.1
  145.2 12.4 %own_and_pair.1 = (bf16[512,2048]{1,0:T(8,128)(2,1)}, f32[512,2048]{1,0:T(8,128)}) custom-call(s32[129]{0:T(256)} %bitcast.27, bf16[2048,512]{1,0:T(8,128)(2,1)} %bitcast.23, f32[512,128]{1,0:T(8,128)} %broadcast_in_dim.2.refs_2_.refs_3_, f32[1,512]{1,0:T(1,128)} %bitcast.33, bf16[256,2048]{1,0:T(8,128)(2,1)} %copy-done.2, ...), custom_call_target="tpu_custom_call" | custom-call | tf_op jit(solution)/shard_map/own_and_pair/pallas_call | solution.py:331
  157.6 7.1 %pair.1.refs_2_ = f32[512,2048]{1,0:T(8,128)} custom-call(s32[129]{0:T(256)} %bitcast.28, bf16[512,2048]{1,0:T(8,128)(2,1)} %get-tuple-element.25.refs_1_, f32[512,2048]{1,0:T(8,128)} %get-tuple-element.26.refs_2_, f32[512,128]{1,0:T(8,128)} %broadcast_in_dim.2.refs_2_.refs_3_, f32[1,512]{1,0:T(1,128)} %bitcast.32, ...), custom_call_target="tpu_custom_call" | custom-call | tf_op jit(solution)/shard_map/pair/pallas_call | solution.py:403
  164.8 1.0 copy-done.4
  165.8 9.5 %pair_last.1 = f32[512,2048]{1,0:T(8,128)} custom-call(s32[129]{0:T(256)} %bitcast.29, bf16[512,2048]{1,0:T(8,128)(2,1)} %get-tuple-element.25.refs_1_, f32[512,2048]{1,0:T(8,128)} %pair.1.refs_2_, f32[512,128]{1,0:T(8,128)} %broadcast_in_dim.2.refs_2_.refs_3_, f32[1,1024]{1,0:T(1,128)} %pad_maximum_fusion.1.refs_4_, ...), custom_call_target="tpu_custom_call" | custom-call | tf_op jit(solution)/shard_map/pair_last/pallas_call | solution.py:403
  (42 shorter events, 0.2 us)
Async XLA Ops:
  0.0 26.8 %copy-start = (f32[128]{0:T(128)S(1)}, f32[128]{0:T(128)}, u32[]{:S(2)}) copy-start(f32[128]{0:T(128)} %param.13) | copy-start | bytes 1540
  0.0 30.6 %collective-permute-start = (bf16[16,2048]{1,0:T(8,128)(2,1)}, bf16[16,2048]{1,0:T(8,128)(2,1)S(1)}, u32[]{:S(2)}, u32[]{:S(2)}) collective-permute-start(bf16[16,2048]{1,0:T(8,128)(2,1)} %param.10), channel_id=1, source_target_pairs={{0,1},{8,40},{1,16},{9,41},{16,17},{24,56},{17,0},{25,57},{32,33},... | collective-permute-start | bytes 196616 | tf_op jit(solution)/shard_map/ppermute | solution.py:37
  2.1 28.5 %collective-permute-start.1 = (bf16[16,2048]{1,0:T(8,128)(2,1)}, bf16[16,2048]{1,0:T(8,128)(2,1)S(1)}, u32[]{:S(2)}, u32[]{:S(2)}) collective-permute-start(bf16[16,2048]{1,0:T(8,128)(2,1)} %param.10), channel_id=1, source_target_pairs={{0,16},{8,72},{1,17},{9,73},{16,0},{24,88},{17,1},{25,89},{32,48},... | collective-permute-start | bytes 196616 | tf_op jit(solution)/shard_map/ppermute | solution.py:37
  4.7 25.9 %collective-permute-start.2 = (bf16[16,2048]{1,0:T(8,128)(2,1)}, bf16[16,2048]{1,0:T(8,128)(2,1)S(1)}, u32[]{:S(2)}, u32[]{:S(2)}) collective-permute-start(bf16[16,2048]{1,0:T(8,128)(2,1)} %param.10), channel_id=1, source_target_pairs={{0,17},{8,104},{1,0},{9,105},{16,1},{24,120},{17,16},{25,121},{32,... | collective-permute-start | bytes 196616 | tf_op jit(solution)/shard_map/ppermute | solution.py:37
  5.8 17.8 %copy-start.8 = (s32[4]{0:T(128)S(1)}, s32[4]{0:T(128)}, u32[]{:S(2)}) copy-start(s32[4]{0:T(128)} %order_ref.1) | copy-start | bytes 52
  5.8 20.9 %copy-start.7 = (bf16[16,2048]{1,0:T(8,128)(2,1)S(1)}, bf16[16,2048]{1,0:T(8,128)(2,1)}, u32[]{:S(2)}) copy-start(bf16[16,2048]{1,0:T(8,128)(2,1)} %param.10) | copy-start | bytes 196612
  5.8 21.0 %copy-start.9 = (f32[512]{0:T(512)S(1)}, f32[512]{0:T(512)}, u32[]{:S(2)}) copy-start(f32[512]{0:T(512)} %param.14) | copy-start | bytes 6148
  5.8 21.0 %copy-start.10 = (s32[128]{0:T(128)S(1)}, s32[128]{0:T(128)}, u32[]{:S(2)}) copy-start(s32[128]{0:T(128)} %param.11) | copy-start | bytes 1540
  14.3 37.8 %all-to-all-start = ((bf16[128,16,256]{2,1,0:T(8,128)(2,1)}), bf16[128,16,256]{2,1,0:T(8,128)(2,1)S(1)}, u32[]{:S(2)}, u32[]{:S(2)}) async-start(bf16[128,16,256]{2,1,0:T(8,128)(2,1)} %get-tuple-element.18), calls=%async_computation | async-start | bytes 2097152 | tf_op jit(solution)/shard_map/all_to_all | solution.py:446
  30.6 12.5 %collective-permute-start.3 = (bf16[64,2048]{1,0:T(8,128)(2,1)S(1)}, bf16[64,2048]{1,0:T(8,128)(2,1)S(1)}, u32[]{:S(2)}, u32[]{:S(2)}) collective-permute-start(bf16[64,2048]{1,0:T(8,128)(2,1)S(1)} %get-tuple-element.31), channel_id=1, source_target_pairs={{0,2},{8,9},{1,3},{9,24},{16,18},{24,25},{17,19},{25,8},{32,34},{4... | collective-permute-start | bytes 786440 | tf_op jit(solution)/shard_map/ppermute | solution.py:37
  32.3 13.4 %collective-permute-start.4 = (bf16[64,2048]{1,0:T(8,128)(2,1)S(1)}, bf16[64,2048]{1,0:T(8,128)(2,1)S(1)}, u32[]{:S(2)}, u32[]{:S(2)}) collective-permute-start(bf16[64,2048]{1,0:T(8,128)(2,1)S(1)} %get-tuple-element.31), channel_id=1, source_target_pairs={{0,4},{8,24},{1,5},{9,25},{16,20},{24,8},{17,21},{25,9},{32,36},{4... | collective-permute-start | bytes 786440 | tf_op jit(solution)/shard_map/ppermute | solution.py:37
  36.5 9.2 %collective-permute-start.5 = (bf16[64,2048]{1,0:T(8,128)(2,1)S(1)}, bf16[64,2048]{1,0:T(8,128)(2,1)S(1)}, u32[]{:S(2)}, u32[]{:S(2)}) collective-permute-start(bf16[64,2048]{1,0:T(8,128)(2,1)S(1)} %get-tuple-element.31), channel_id=1, source_target_pairs={{0,6},{8,25},{1,7},{9,8},{16,22},{24,9},{17,23},{25,24},{32,38},{4... | collective-permute-start | bytes 786440 | tf_op jit(solution)/shard_map/ppermute | solution.py:37
  45.7 28.7 %copy-start.2 = (bf16[256,2048]{1,0:T(8,128)(2,1)}, bf16[256,2048]{1,0:T(8,128)(2,1)S(1)}, u32[]{:S(2)}) copy-start(bf16[256,2048]{1,0:T(8,128)(2,1)S(1)} %constant_dynamic-update-slice_fusion.4.refs_0_.refs_4_) | copy-start | bytes 3145732
  45.7 15.3 %collective-permute-start.6 = (bf16[256,2048]{1,0:T(8,128)(2,1)S(1)}, bf16[256,2048]{1,0:T(8,128)(2,1)}, u32[]{:S(2)}, u32[]{:S(2)}) collective-permute-start(bf16[256,2048]{1,0:T(8,128)(2,1)S(1)} %constant_dynamic-update-slice_fusion.4.refs_0_.refs_4_), channel_id=1, source_target_pairs={{0,32},{8,10},{1,33},{9,11},{16,48},{24,26},{17,49},{25,27},{32,64... | collective-permute-start | bytes 3145736 | tf_op jit(solution)/shard_map/ppermute | solution.py:37
  48.6 24.3 %collective-permute-start.7 = (bf16[256,2048]{1,0:T(8,128)(2,1)S(1)}, bf16[256,2048]{1,0:T(8,128)(2,1)}, u32[]{:S(2)}, u32[]{:S(2)}) collective-permute-start(bf16[256,2048]{1,0:T(8,128)(2,1)S(1)} %constant_dynamic-update-slice_fusion.4.refs_0_.refs_4_), channel_id=1, source_target_pairs={{0,64},{8,12},{1,65},{9,13},{16,80},{24,28},{17,81},{25,29},{32,96... | collective-permute-start | bytes 3145736 | tf_op jit(solution)/shard_map/ppermute | solution.py:37
  51.2 23.3 %collective-permute-start.8 = (bf16[256,2048]{1,0:T(8,128)(2,1)S(1)}, bf16[256,2048]{1,0:T(8,128)(2,1)}, u32[]{:S(2)}, u32[]{:S(2)}) collective-permute-start(bf16[256,2048]{1,0:T(8,128)(2,1)S(1)} %constant_dynamic-update-slice_fusion.4.refs_0_.refs_4_), channel_id=1, source_target_pairs={{0,96},{8,14},{1,97},{9,15},{16,112},{24,30},{17,113},{25,31},{32,... | collective-permute-start | bytes 3145736 | tf_op jit(solution)/shard_map/ppermute | solution.py:37
  52.1 22.4 %copy-start.3 = (bf16[128,16,256]{2,1,0:T(8,128)(2,1)}, bf16[128,16,256]{2,1,0:T(8,128)(2,1)S(1)}, u32[]{:S(2)}) copy-start(bf16[128,16,256]{2,1,0:T(8,128)(2,1)S(1)} %all-to-all-done) | copy-start | bytes 3145732
  53.1 21.4 %collective-permute-start.13 = (bf16[2048,256]{1,0:T(8,128)(2,1)S(1)}, bf16[2048,256]{1,0:T(8,128)(2,1)S(1)}, u32[]{:S(2)}, u32[]{:S(2)}) collective-permute-start(bf16[2048,256]{1,0:T(8,128)(2,1)S(1)} %bitcast.24), channel_id=1, source_target_pairs={{0,8},{8,0},{1,9},{9,1},{16,24},{24,16},{17,25},{25,17},{32,40},{4... | collective-permute-start | bytes 3145736 | tf_op jit(solution)/shard_map/ppermute | solution.py:42
  53.1 38.3 %collective-permute-start.9 = (bf16[256,2048]{1,0:T(8,128)(2,1)S(1)}, bf16[256,2048]{1,0:T(8,128)(2,1)}, u32[]{:S(2)}, u32[]{:S(2)}) collective-permute-start(bf16[256,2048]{1,0:T(8,128)(2,1)S(1)} %constant_dynamic-update-slice_fusion.4.refs_0_.refs_4_), channel_id=1, source_target_pairs={{0,8},{8,0},{1,9},{9,1},{16,24},{24,16},{17,25},{25,17},{32,40},{4... | collective-permute-start | bytes 3145736 | tf_op jit(solution)/shard_map/ppermute | solution.py:42
  61.1 31.7 %collective-permute-start.10 = (bf16[256,2048]{1,0:T(8,128)(2,1)}, bf16[256,2048]{1,0:T(8,128)(2,1)}, u32[]{:S(2)}, u32[]{:S(2)}) collective-permute-start(bf16[256,2048]{1,0:T(8,128)(2,1)} %collective-permute-done.6.refs_1_.refs_5_), channel_id=1, source_target_pairs={{0,8},{8,0},{1,9},{9,1},{16,24},{24,16},{17,25},{25,17},{32,40},{4... | collective-permute-start | bytes 3145736 | tf_op jit(solution)/shard_map/ppermute | solution.py:42
  72.9 20.6 %collective-permute-start.11 = (bf16[256,2048]{1,0:T(8,128)(2,1)}, bf16[256,2048]{1,0:T(8,128)(2,1)}, u32[]{:S(2)}, u32[]{:S(2)}) collective-permute-start(bf16[256,2048]{1,0:T(8,128)(2,1)} %collective-permute-done.7.refs_2_.refs_6_), channel_id=1, source_target_pairs={{0,8},{8,0},{1,9},{9,1},{16,24},{24,16},{17,25},{25,17},{32,40},{4... | collective-permute-start | bytes 3145736 | tf_op jit(solution)/shard_map/ppermute | solution.py:42
  74.5 21.0 %collective-permute-start.12 = (bf16[256,2048]{1,0:T(8,128)(2,1)}, bf16[256,2048]{1,0:T(8,128)(2,1)}, u32[]{:S(2)}, u32[]{:S(2)}) collective-permute-start(bf16[256,2048]{1,0:T(8,128)(2,1)} %collective-permute-done.8.refs_3_.refs_7_), channel_id=1, source_target_pairs={{0,8},{8,0},{1,9},{9,1},{16,24},{24,16},{17,25},{25,17},{32,40},{4... | collective-permute-start | bytes 3145736 | tf_op jit(solution)/shard_map/ppermute | solution.py:42
  74.5 1.0 copy-start.5
  82.6 47.8 %collective-permute-start.23 = (bf16[512,1024]{1,0:T(8,128)(2,1)}, bf16[512,1024]{1,0:T(8,128)(2,1)}, u32[]{:S(2)}, u32[]{:S(2)}) collective-permute-start(bf16[512,1024]{1,0:T(8,128)(2,1)} %get-tuple-element.24.refs_12_), channel_id=1, source_target_pairs={{0,16},{8,24},{1,17},{9,25},{16,0},{24,8},{17,1},{25,9},{32,48},{4... | collective-permute-start | bytes 3145736 | tf_op jit(solution)/shard_map/ppermute | solution.py:37
  85.7 58.1 %all-to-all-start.1 = ((bf16[128,16,512]{2,1,0:T(8,128)(2,1)}), bf16[128,16,512]{2,1,0:T(8,128)(2,1)S(1)}, u32[]{:S(2)}, u32[]{:S(2)}) async-start(bf16[128,16,512]{2,1,0:T(8,128)(2,1)} %get-tuple-element.20), calls=%async_computation.1 | async-start | bytes 4194304 | tf_op jit(solution)/shard_map/all_to_all | solution.py:447
  91.4 36.8 %collective-permute-start.15 = (bf16[256,1024]{1,0:T(8,128)(2,1)}, bf16[256,1024]{1,0:T(8,128)(2,1)}, u32[]{:S(2)}, u32[]{:S(2)}) collective-permute-start(bf16[256,1024]{1,0:T(8,128)(2,1)} %get-tuple-element.28), channel_id=1, source_target_pairs={{0,32},{8,40},{1,33},{9,41},{16,48},{24,56},{17,49},{25,57},{32,64... | collective-permute-start | bytes 1572872 | tf_op jit(solution)/shard_map/ppermute | solution.py:37
  92.8 50.0 %collective-permute-start.14 = (bf16[512,1024]{1,0:T(8,128)(2,1)}, bf16[512,1024]{1,0:T(8,128)(2,1)S(1)}, u32[]{:S(2)}, u32[]{:S(2)}) collective-permute-start(bf16[512,1024]{1,0:T(8,128)(2,1)} %get-tuple-element.24.refs_12_), channel_id=1, source_target_pairs={{0,8},{8,0},{1,9},{9,1},{16,24},{24,16},{17,25},{25,17},{32,40},{4... | collective-permute-start | bytes 3145736 | tf_op jit(solution)/shard_map/ppermute | solution.py:42
  93.5 38.9 %collective-permute-start.17 = (bf16[256,1024]{1,0:T(8,128)(2,1)}, bf16[256,1024]{1,0:T(8,128)(2,1)}, u32[]{:S(2)}, u32[]{:S(2)}) collective-permute-start(bf16[256,1024]{1,0:T(8,128)(2,1)} %get-tuple-element.28), channel_id=1, source_target_pairs={{0,96},{8,104},{1,97},{9,105},{16,112},{24,120},{17,113},{25,121},... | collective-permute-start | bytes 1572872 | tf_op jit(solution)/shard_map/ppermute | solution.py:37
  95.5 43.9 %collective-permute-start.19 = (bf16[256,1024]{1,0:T(8,128)(2,1)}, bf16[256,1024]{1,0:T(8,128)(2,1)}, u32[]{:S(2)}, u32[]{:S(2)}) collective-permute-start(bf16[256,1024]{1,0:T(8,128)(2,1)} %get-tuple-element.30), channel_id=1, source_target_pairs={{0,32},{8,40},{1,33},{9,41},{16,48},{24,56},{17,49},{25,57},{32,64... | collective-permute-start | bytes 1572872 | tf_op jit(solution)/shard_map/ppermute | solution.py:37
  128.2 12.9 %collective-permute-start.21 = (bf16[256,1024]{1,0:T(8,128)(2,1)}, bf16[256,1024]{1,0:T(8,128)(2,1)}, u32[]{:S(2)}, u32[]{:S(2)}) collective-permute-start(bf16[256,1024]{1,0:T(8,128)(2,1)} %get-tuple-element.30), channel_id=1, source_target_pairs={{0,96},{8,104},{1,97},{9,105},{16,112},{24,120},{17,113},{25,121},... | collective-permute-start | bytes 1572872 | tf_op jit(solution)/shard_map/ppermute | solution.py:37
  130.4 34.4 %collective-permute-start.24 = (bf16[512,1024]{1,0:T(8,128)(2,1)}, bf16[512,1024]{1,0:T(8,128)(2,1)S(1)}, u32[]{:S(2)}, u32[]{:S(2)}) collective-permute-start(bf16[512,1024]{1,0:T(8,128)(2,1)} %collective-permute-done.23.refs_9_), channel_id=1, source_target_pairs={{0,8},{8,0},{1,9},{9,1},{16,24},{24,16},{17,25},{25,17},{32,40},{4... | collective-permute-start | bytes 3145736 | tf_op jit(solution)/shard_map/ppermute | solution.py:42
  132.4 25.2 %collective-permute-start.16 = (bf16[256,1024]{1,0:T(8,128)(2,1)}, bf16[256,1024]{1,0:T(8,128)(2,1)}, u32[]{:S(2)}, u32[]{:S(2)}) collective-permute-start(bf16[256,1024]{1,0:T(8,128)(2,1)} %collective-permute-done.15.refs_5_), channel_id=1, source_target_pairs={{0,8},{8,0},{1,9},{9,1},{16,24},{24,16},{17,25},{25,17},{32,40},{4... | collective-permute-start | bytes 1572872 | tf_op jit(solution)/shard_map/ppermute | solution.py:42
  139.4 18.2 %collective-permute-start.18 = (bf16[256,1024]{1,0:T(8,128)(2,1)}, bf16[256,1024]{1,0:T(8,128)(2,1)}, u32[]{:S(2)}, u32[]{:S(2)}) collective-permute-start(bf16[256,1024]{1,0:T(8,128)(2,1)} %collective-permute-done.17.refs_7_), channel_id=1, source_target_pairs={{0,8},{8,0},{1,9},{9,1},{16,24},{24,16},{17,25},{25,17},{32,40},{4... | collective-permute-start | bytes 1572872 | tf_op jit(solution)/shard_map/ppermute | solution.py:42
  141.1 23.7 %collective-permute-start.20 = (bf16[256,1024]{1,0:T(8,128)(2,1)}, bf16[256,1024]{1,0:T(8,128)(2,1)}, u32[]{:S(2)}, u32[]{:S(2)}) collective-permute-start(bf16[256,1024]{1,0:T(8,128)(2,1)} %collective-permute-done.19.refs_5_), channel_id=1, source_target_pairs={{0,8},{8,0},{1,9},{9,1},{16,24},{24,16},{17,25},{25,17},{32,40},{4... | collective-permute-start | bytes 1572872 | tf_op jit(solution)/shard_map/ppermute | solution.py:42
  142.9 1.0 copy-start.6
  143.9 20.9 %collective-permute-start.22 = (bf16[256,1024]{1,0:T(8,128)(2,1)}, bf16[256,1024]{1,0:T(8,128)(2,1)}, u32[]{:S(2)}, u32[]{:S(2)}) collective-permute-start(bf16[256,1024]{1,0:T(8,128)(2,1)} %collective-permute-done.21.refs_7_), channel_id=1, source_target_pairs={{0,8},{8,0},{1,9},{9,1},{16,24},{24,16},{17,25},{25,17},{32,40},{4... | collective-permute-start | bytes 1572872 | tf_op jit(solution)/shard_map/ppermute | solution.py:42
  143.9 1.3 copy-start.1
  164.8 1.0 copy-start.4

commit v4 on v3

--- a/solution.py
+++ b/solution.py
@@ -121,7 +121,7 @@
                     part[owner * 8 + v, :, at] = tile
         return carry
 
-    lax.fori_loop(0, 8, emit_partner, 0)
+    lax.fori_loop(0, 8, emit_partner, 0, unroll=2)
     send_part = pltpu.make_async_copy(part, part_ref, out_sems.at[0])
     send_part.start()
 
@@ -145,7 +145,7 @@
         for h in range(2)
     ]
     for h in range(2):
-        lax.fori_loop(8 * h, 8 * h + 8, emit, 0)
+        lax.fori_loop(8 * h, 8 * h + 8, emit, 0, unroll=2)
         sends[h].start()
     send_part.wait()
     for send in sends:
@@ -346,7 +346,7 @@
             pltpu.SemaphoreType.DMA((6,)),
         ],
         name="own_and_pair",
-    )(table, own, row, col, *parts, *pieces)
+    )(table, on_chip(own), row, col, *parts, *pieces)
 
 
 def pair_kernel(table_ref, own_ref, total_ref, row_ref, col_ref, *refs, sizes, final):
@@ -415,6 +415,10 @@
         ],
         name="pair_last" if final else "pair",
     )(table, own, total, row, col, *pieces)
+
+
+def on_chip(value):
+    return pltpu.with_memory_space_constraint(value, pltpu.VMEM)
 
 
 def energies(me, owner_table, pair_order, occ_energy, vir_energy):
@@ -464,6 +468,7 @@
     here = whole_rows(here)
     beside = [[whole_rows(part) for part in beside[i]] for i in range(2)]
     across = whole_rows(across)
+    across = tuple(on_chip(half) for half in across)
     own, density = own_and_pair(table, own, row, near, mine_parts + other_parts, [[here]])
     density = paired(table, own, density, row, first, [beside[0]], False)
     density = paired(table, own, density, row, second, [beside[1], [across]], True)

time: 176 us -> 176 us (level)
  local copies, waits for them, and re-layouts: 8.86 us -> 11.2 us
  waiting for transfers between devices: 71.9 us -> 69.7 us
    ppermute x14, waiting for transfers between devices: 71.8 us -> 69.7 us  [shifted(): return lax.ppermute(value, AXES, pairs)]
    unnamed x27 -> x21, local copies, waits for them, and re-layouts: 4.43 us -> 5.39 us
  transfers between devices with their start and end apart: 27 -> 27, of which waited for: 9 -> 9; matrix products, arithmetic and copies ran while one was open for 5% -> 8% of each run, Pallas kernels for 20% -> 19%
where the time goes in v4:
time: 176 us
  waiting for transfers between devices  69.7 us (40%)
  starting transfers between devices  43.7 us (25%)
  Pallas kernels  43.4 us (25%)
  local copies, waits for them, and re-layouts  11.2 us (6%)
  other arithmetic  4.19 us (2%)
  between operations  3.19 us (2%)
    ppermute x14, waiting for transfers between devices, shifted(): return lax.ppermute(value, AXES, pairs)  69.7 us
    ppermute x14, starting transfers between devices, shifted(): return lax.ppermute(value, AXES, pairs)  21.8 us
    pallas_call x2, Pallas kernels, paired(): pl.pallas_call(body, in_specs=[smem, hbm, hbm, vmem, vmem] + [hbm] * len(...  16.6 us
    pallas_call x1, Pallas kernels, own_and_pair(): pl.pallas_call(body, in_specs=[smem, vmem, vmem, vmem] + [hbm] * (8 + len...  11.7 us
    all_to_all x1, starting transfers between devices, whole(): part = lax.all_to_all(part, AXES, split_axis=0, concat_axis=0, tiled=True)  9.17 us
    pallas_call x1, Pallas kernels, transformed(): pl.pallas_call(half_kernel, in_specs=[pl.BlockSpec(memory_space=pltpu.SME...  7.97 us
    pallas_call x1, Pallas kernels, partner_fit(): pl.pallas_call(partner_kernel, in_specs=[smem] + [pl.BlockSpec(memory_spa...  7.14 us
    all_to_all x1, starting transfers between devices, whole(): own = lax.all_to_all(own, AXES, split_axis=0, concat_axis=0, tiled=True)  6.6 us
  transfers between devices with their start and end apart: 27, of which 9 were waited for; matrix products, arithmetic and copies ran while one was open for 8% of the time, Pallas kernels for 19%

profile of v4, /device:TPU:1, one launch (start us, length us, event | category | flops | bytes accessed | tf_op | source)
XLA Modules:
  0.0 175.6 jit_solution(14769504953499991468)
XLA Ops:
  0.0 2.1 %collective-permute-start = (bf16[16,2048]{1,0:T(8,128)(2,1)}, bf16[16,2048]{1,0:T(8,128)(2,1)S(1)}, u32[]{:S(2)}, u32[]{:S(2)}) collective-permute-start(bf16[16,2048]{1,0:T(8,128)(2,1)} %param.10), channel_id=1, source_target_pairs={{0,1},{8,40},{1,16},{9,41},{16,17},{24,56},{17,0},{25,57},{32,33},... | collective-permute-start | bytes 196616 | tf_op jit(solution)/shard_map/ppermute | solution.py:37
  2.1 2.6 %collective-permute-start.1 = (bf16[16,2048]{1,0:T(8,128)(2,1)}, bf16[16,2048]{1,0:T(8,128)(2,1)S(1)}, u32[]{:S(2)}, u32[]{:S(2)}) collective-permute-start(bf16[16,2048]{1,0:T(8,128)(2,1)} %param.10), channel_id=1, source_target_pairs={{0,16},{8,72},{1,17},{9,73},{16,0},{24,88},{17,1},{25,89},{32,48},... | collective-permute-start | bytes 196616 | tf_op jit(solution)/shard_map/ppermute | solution.py:37
  4.7 1.1 collective-permute-start.2
  5.8 8.0 %half.1 = (bf16[128,16,256]{2,1,0:T(8,128)(2,1)}, bf16[128,16,512]{2,1,0:T(8,128)(2,1)}) custom-call(s32[4]{0:T(128)} %order_ref.1, s32[1,128]{1,0:T(1,128)} %bitcast.35, bf16[16,128,640]{2,1,0:T(8,128)(2,1)} %ints_ref.1, bf16[640,512]{1,0:T(8,128)(2,1)} %coeff_ref.1), custom_call_target="tpu_custom_call" | custom-call | tf_op jit(solution)/shard_map/half/pallas_call | solution.py:159
  13.8 9.2 %all-to-all-start = ((bf16[128,16,256]{2,1,0:T(8,128)(2,1)}), bf16[128,16,256]{2,1,0:T(8,128)(2,1)S(1)}, u32[]{:S(2)}, u32[]{:S(2)}) async-start(bf16[128,16,256]{2,1,0:T(8,128)(2,1)} %get-tuple-element.18), calls=%async_computation | async-start | bytes 2097152 | tf_op jit(solution)/shard_map/all_to_all | solution.py:450
  23.1 0.7 fusion.4
  26.5 0.6 constant_dynamic-update-slice_fusion.3
  27.2 0.2 convolution_bitcast_fusion
  27.4 0.7 fusion.3
  28.1 2.7 %pad_maximum_fusion.3 = f32[4]{0:T(128)S(1)} fusion(f32[1]{0:T(128)} %get-tuple-element.48, f32[1]{0:T(128)} %get-tuple-element.49, f32[1]{0:T(128)} %get-tuple-element.50, f32[1]{0:T(128)} %get-tuple-element.47), kind=kLoop, calls=%fused_computation.21 | loop fusion | flops 12 | bytes 32 | tf_op jit(solution)/shard_map/concatenate | solution.py:432
  30.9 0.1 broadcast_subtract_fusion
  30.9 0.1 dynamic_slice.26
  31.0 0.1 dynamic_slice.25
  31.1 0.0 collective-permute-done
  31.1 0.6 constant_dynamic-update-slice_fusion.2
  31.7 0.0 collective-permute-done.1
  31.7 0.6 constant_dynamic-update-slice_fusion.1
  32.4 0.0 collective-permute-done.2
  32.4 0.6 constant_dynamic-update-slice_fusion
  33.0 1.5 collective-permute-start.3
  34.5 0.1 broadcast_subtract_fusion.1
  34.6 2.9 %collective-permute-start.4 = (bf16[64,2048]{1,0:T(8,128)(2,1)S(1)}, bf16[64,2048]{1,0:T(8,128)(2,1)S(1)}, u32[]{:S(2)}, u32[]{:S(2)}) collective-permute-start(bf16[64,2048]{1,0:T(8,128)(2,1)S(1)} %get-tuple-element.31), channel_id=1, source_target_pairs={{0,4},{8,24},{1,5},{9,25},{16,20},{24,8},{17,21},{25,9},{32,36},{4... | collective-permute-start | bytes 786440 | tf_op jit(solution)/shard_map/ppermute | solution.py:37
  37.5 1.3 constant_dynamic-slice_fusion.1
  38.8 0.1 sub.95
  38.8 0.9 collective-permute-start.5
  39.7 3.5 %collective-permute-done.3 = bf16[64,2048]{1,0:T(8,128)(2,1)S(1)} collective-permute-done((bf16[64,2048]{1,0:T(8,128)(2,1)S(1)}, bf16[64,2048]{1,0:T(8,128)(2,1)S(1)}, u32[]{:S(2)}, u32[]{:S(2)}) %collective-permute-start.3) | collective-permute-done | bytes 262176 | tf_op jit(solution)/shard_map/ppermute | solution.py:37
  43.3 0.7 constant_dynamic-update-slice_fusion.6
  44.0 2.1 %collective-permute-done.4 = bf16[64,2048]{1,0:T(8,128)(2,1)S(1)} collective-permute-done((bf16[64,2048]{1,0:T(8,128)(2,1)S(1)}, bf16[64,2048]{1,0:T(8,128)(2,1)S(1)}, u32[]{:S(2)}, u32[]{:S(2)}) %collective-permute-start.4) | collective-permute-done | bytes 262176 | tf_op jit(solution)/shard_map/ppermute | solution.py:37
  46.1 0.7 constant_dynamic-update-slice_fusion.5
  46.8 0.7 constant_dynamic-update-slice_fusion.4.refs_0_.refs_4_
  47.5 0.1 collective-permute-start.6
  47.6 0.7 broadcast_subtract_fusion.2
  48.3 0.6 fusion.2
  48.9 0.6 pad_maximum_fusion.1.refs_4_
  49.5 2.5 %collective-permute-start.7 = (bf16[256,2048]{1,0:T(8,128)(2,1)}, bf16[256,2048]{1,0:T(8,128)(2,1)}, u32[]{:S(2)}, u32[]{:S(2)}) collective-permute-start(bf16[256,2048]{1,0:T(8,128)(2,1)} %constant_dynamic-update-slice_fusion.4.refs_0_.refs_4_), channel_id=1, source_target_pairs={{0,64},{8,12},{1,65},{9,13},{16,80},{24,28},{17,81},{25,29},{32,96... | collective-permute-start | bytes 3145736 | tf_op jit(solution)/shard_map/ppermute | solution.py:37
  52.0 1.2 collective-permute-start.8
  53.2 1.0 broadcast_in_dim.2.refs_2_.refs_3_
  54.2 0.6 collective-permute-start.13
  54.8 7.9 %collective-permute-done.6.refs_1_.refs_5_ = bf16[256,2048]{1,0:T(8,128)(2,1)} collective-permute-done((bf16[256,2048]{1,0:T(8,128)(2,1)}, bf16[256,2048]{1,0:T(8,128)(2,1)}, u32[]{:S(2)}, u32[]{:S(2)}) %collective-permute-start.6) | collective-permute-done | bytes 1048608 | tf_op jit(solution)/shard_map/ppermute | solution.py:37
  62.7 11.5 %collective-permute-done.7.refs_2_.refs_6_ = bf16[256,2048]{1,0:T(8,128)(2,1)} collective-permute-done((bf16[256,2048]{1,0:T(8,128)(2,1)}, bf16[256,2048]{1,0:T(8,128)(2,1)}, u32[]{:S(2)}, u32[]{:S(2)}) %collective-permute-start.7) | collective-permute-done | bytes 1048608 | tf_op jit(solution)/shard_map/ppermute | solution.py:37
  74.2 0.7 collective-permute-start.11
  74.9 1.5 collective-permute-done.8.refs_3_.refs_7_
  76.4 0.2 collective-permute-start.12
  76.6 1.0 copy-done.2
  77.6 7.1 %fit_partner.1 = (bf16[512,1024]{1,0:T(8,128)(2,1)}, bf16[256,1024]{1,0:T(8,128)(2,1)}, bf16[256,1024]{1,0:T(8,128)(2,1)}) custom-call(s32[129]{0:T(256)} %bitcast.26, bf16[2048,256]{1,0:T(8,128)(2,1)} %bitcast.25, bf16[2048,256]{1,0:T(8,128)(2,1)} %copy-done.2, bf16[256,2048]{1,0:T(8,128)(2,1)} %constant_dynamic-update-slice_fusion.4.refs_0_.refs_4_, ...), custom_call_target="tpu_custom_call" | custom-call | tf_op jit(solution)/shard_map/fit_partner/pallas_call | solution.py:227
  84.8 3.2 %collective-permute-start.23 = (bf16[512,1024]{1,0:T(8,128)(2,1)}, bf16[512,1024]{1,0:T(8,128)(2,1)S(1)}, u32[]{:S(2)}, u32[]{:S(2)}) collective-permute-start(bf16[512,1024]{1,0:T(8,128)(2,1)} %get-tuple-element.24.refs_12_), channel_id=1, source_target_pairs={{0,16},{8,24},{1,17},{9,25},{16,0},{24,8},{17,1},{25,9},{32,48},{4... | collective-permute-start | bytes 3145736 | tf_op jit(solution)/shard_map/ppermute | solution.py:37
  88.0 6.6 %all-to-all-start.1 = ((bf16[128,16,512]{2,1,0:T(8,128)(2,1)}), bf16[128,16,512]{2,1,0:T(8,128)(2,1)S(1)}, u32[]{:S(2)}, u32[]{:S(2)}) async-start(bf16[128,16,512]{2,1,0:T(8,128)(2,1)} %get-tuple-element.20), calls=%async_computation.1 | async-start | bytes 4194304 | tf_op jit(solution)/shard_map/all_to_all | solution.py:451
  94.6 1.4 collective-permute-start.15
  96.0 0.7 collective-permute-start.14
  96.7 2.0 %collective-permute-start.17 = (bf16[256,1024]{1,0:T(8,128)(2,1)}, bf16[256,1024]{1,0:T(8,128)(2,1)}, u32[]{:S(2)}, u32[]{:S(2)}) collective-permute-start(bf16[256,1024]{1,0:T(8,128)(2,1)} %get-tuple-element.28), channel_id=1, source_target_pairs={{0,96},{8,104},{1,97},{9,105},{16,112},{24,120},{17,113},{25,121},... | collective-permute-start | bytes 1572872 | tf_op jit(solution)/shard_map/ppermute | solution.py:37
  98.7 32.7 %collective-permute-done.15.refs_5_ = bf16[256,1024]{1,0:T(8,128)(2,1)} collective-permute-done((bf16[256,1024]{1,0:T(8,128)(2,1)}, bf16[256,1024]{1,0:T(8,128)(2,1)}, u32[]{:S(2)}, u32[]{:S(2)}) %collective-permute-start.15) | collective-permute-done | bytes 524320 | tf_op jit(solution)/shard_map/ppermute | solution.py:37
  131.4 0.2 collective-permute-start.21
  131.5 1.3 collective-permute-done.23.refs_9_
  132.8 1.6 collective-permute-start.24
  134.4 0.0 collective-permute-start.16
  134.5 8.2 %collective-permute-done.19.refs_5_ = bf16[256,1024]{1,0:T(8,128)(2,1)} collective-permute-done((bf16[256,1024]{1,0:T(8,128)(2,1)}, bf16[256,1024]{1,0:T(8,128)(2,1)}, u32[]{:S(2)}, u32[]{:S(2)}) %collective-permute-start.19) | collective-permute-done | bytes 524320 | tf_op jit(solution)/shard_map/ppermute | solution.py:37
  142.6 0.7 collective-permute-start.18
  143.3 1.0 collective-permute-done.21.refs_7_
  144.2 1.8 %collective-permute-start.20 = (bf16[256,1024]{1,0:T(8,128)(2,1)}, bf16[256,1024]{1,0:T(8,128)(2,1)}, u32[]{:S(2)}, u32[]{:S(2)}) collective-permute-start(bf16[256,1024]{1,0:T(8,128)(2,1)} %collective-permute-done.19.refs_5_), channel_id=1, source_target_pairs={{0,8},{8,0},{1,9},{9,1},{16,24},{24,16},{17,25},{25,17},{32,40},{4... | collective-permute-start | bytes 1572872 | tf_op jit(solution)/shard_map/ppermute | solution.py:42
  146.0 1.0 copy-done.3
  147.1 0.0 collective-permute-start.22
  147.1 11.7 %own_and_pair.1 = (bf16[512,2048]{1,0:T(8,128)(2,1)}, f32[512,2048]{1,0:T(8,128)}) custom-call(s32[129]{0:T(256)} %bitcast.27, bf16[2048,512]{1,0:T(8,128)(2,1)S(1)} %bitcast.23, f32[512,128]{1,0:T(8,128)} %broadcast_in_dim.2.refs_2_.refs_3_, f32[1,512]{1,0:T(1,128)} %bitcast.33, bf16[256,2048]{1,0:T(8,128)(2,1)} %constant_dynamic-update-slice_fusion.4.refs_0_.refs_4_, ...), custom_call_target="tpu_custom_call" | custom-call | tf_op jit(solution)/shard_map/own_and_pair/pallas_call | solution.py:331
  158.8 7.2 %pair.1.refs_2_ = f32[512,2048]{1,0:T(8,128)} custom-call(s32[129]{0:T(256)} %bitcast.28, bf16[512,2048]{1,0:T(8,128)(2,1)} %get-tuple-element.25.refs_1_, f32[512,2048]{1,0:T(8,128)} %get-tuple-element.26.refs_2_, f32[512,128]{1,0:T(8,128)} %broadcast_in_dim.2.refs_2_.refs_3_, f32[1,512]{1,0:T(1,128)} %bitcast.32, ...), custom_call_target="tpu_custom_call" | custom-call | tf_op jit(solution)/shard_map/pair/pallas_call | solution.py:403
  166.0 9.4 %pair_last.1 = f32[512,2048]{1,0:T(8,128)} custom-call(s32[129]{0:T(256)} %bitcast.29, bf16[512,2048]{1,0:T(8,128)(2,1)} %get-tuple-element.25.refs_1_, f32[512,2048]{1,0:T(8,128)} %pair.1.refs_2_, f32[512,128]{1,0:T(8,128)} %broadcast_in_dim.2.refs_2_.refs_3_, f32[1,1024]{1,0:T(1,128)} %pad_maximum_fusion.1.refs_4_, ...), custom_call_target="tpu_custom_call" | custom-call | tf_op jit(solution)/shard_map/pair_last/pallas_call | solution.py:403
  (36 shorter events, 0.1 us)
Async XLA Ops:
  0.0 27.1 %copy-start = (f32[128]{0:T(128)S(1)}, f32[128]{0:T(128)}, u32[]{:S(2)}) copy-start(f32[128]{0:T(128)} %param.13) | copy-start | bytes 1540
  0.0 31.1 %collective-permute-start = (bf16[16,2048]{1,0:T(8,128)(2,1)}, bf16[16,2048]{1,0:T(8,128)(2,1)S(1)}, u32[]{:S(2)}, u32[]{:S(2)}) collective-permute-start(bf16[16,2048]{1,0:T(8,128)(2,1)} %param.10), channel_id=1, source_target_pairs={{0,1},{8,40},{1,16},{9,41},{16,17},{24,56},{17,0},{25,57},{32,33},... | collective-permute-start | bytes 196616 | tf_op jit(solution)/shard_map/ppermute | solution.py:37
  2.1 29.6 %collective-permute-start.1 = (bf16[16,2048]{1,0:T(8,128)(2,1)}, bf16[16,2048]{1,0:T(8,128)(2,1)S(1)}, u32[]{:S(2)}, u32[]{:S(2)}) collective-permute-start(bf16[16,2048]{1,0:T(8,128)(2,1)} %param.10), channel_id=1, source_target_pairs={{0,16},{8,72},{1,17},{9,73},{16,0},{24,88},{17,1},{25,89},{32,48},... | collective-permute-start | bytes 196616 | tf_op jit(solution)/shard_map/ppermute | solution.py:37
  4.7 27.6 %collective-permute-start.2 = (bf16[16,2048]{1,0:T(8,128)(2,1)}, bf16[16,2048]{1,0:T(8,128)(2,1)S(1)}, u32[]{:S(2)}, u32[]{:S(2)}) collective-permute-start(bf16[16,2048]{1,0:T(8,128)(2,1)} %param.10), channel_id=1, source_target_pairs={{0,17},{8,104},{1,0},{9,105},{16,1},{24,120},{17,16},{25,121},{32,... | collective-permute-start | bytes 196616 | tf_op jit(solution)/shard_map/ppermute | solution.py:37
  5.8 17.3 %copy-start.5 = (s32[4]{0:T(128)S(1)}, s32[4]{0:T(128)}, u32[]{:S(2)}) copy-start(s32[4]{0:T(128)} %order_ref.1) | copy-start | bytes 52
  5.8 20.6 %copy-start.4 = (bf16[16,2048]{1,0:T(8,128)(2,1)S(1)}, bf16[16,2048]{1,0:T(8,128)(2,1)}, u32[]{:S(2)}) copy-start(bf16[16,2048]{1,0:T(8,128)(2,1)} %param.10) | copy-start | bytes 196612
  5.8 21.3 %copy-start.6 = (f32[512]{0:T(512)S(1)}, f32[512]{0:T(512)}, u32[]{:S(2)}) copy-start(f32[512]{0:T(512)} %param.14) | copy-start | bytes 6148
  5.8 21.3 %copy-start.7 = (s32[128]{0:T(128)S(1)}, s32[128]{0:T(128)}, u32[]{:S(2)}) copy-start(s32[128]{0:T(128)} %param.11) | copy-start | bytes 1540
  13.8 39.4 %all-to-all-start = ((bf16[128,16,256]{2,1,0:T(8,128)(2,1)}), bf16[128,16,256]{2,1,0:T(8,128)(2,1)S(1)}, u32[]{:S(2)}, u32[]{:S(2)}) async-start(bf16[128,16,256]{2,1,0:T(8,128)(2,1)} %get-tuple-element.18), calls=%async_computation | async-start | bytes 2097152 | tf_op jit(solution)/shard_map/all_to_all | solution.py:450
  33.0 10.3 %collective-permute-start.3 = (bf16[64,2048]{1,0:T(8,128)(2,1)S(1)}, bf16[64,2048]{1,0:T(8,128)(2,1)S(1)}, u32[]{:S(2)}, u32[]{:S(2)}) collective-permute-start(bf16[64,2048]{1,0:T(8,128)(2,1)S(1)} %get-tuple-element.31), channel_id=1, source_target_pairs={{0,2},{8,9},{1,3},{9,24},{16,18},{24,25},{17,19},{25,8},{32,34},{4... | collective-permute-start | bytes 786440 | tf_op jit(solution)/shard_map/ppermute | solution.py:37
  34.6 11.5 %collective-permute-start.4 = (bf16[64,2048]{1,0:T(8,128)(2,1)S(1)}, bf16[64,2048]{1,0:T(8,128)(2,1)S(1)}, u32[]{:S(2)}, u32[]{:S(2)}) collective-permute-start(bf16[64,2048]{1,0:T(8,128)(2,1)S(1)} %get-tuple-element.31), channel_id=1, source_target_pairs={{0,4},{8,24},{1,5},{9,25},{16,20},{24,8},{17,21},{25,9},{32,36},{4... | collective-permute-start | bytes 786440 | tf_op jit(solution)/shard_map/ppermute | solution.py:37
  38.8 8.0 %collective-permute-start.5 = (bf16[64,2048]{1,0:T(8,128)(2,1)S(1)}, bf16[64,2048]{1,0:T(8,128)(2,1)S(1)}, u32[]{:S(2)}, u32[]{:S(2)}) collective-permute-start(bf16[64,2048]{1,0:T(8,128)(2,1)S(1)} %get-tuple-element.31), channel_id=1, source_target_pairs={{0,6},{8,25},{1,7},{9,8},{16,22},{24,9},{17,23},{25,24},{32,38},{4... | collective-permute-start | bytes 786440 | tf_op jit(solution)/shard_map/ppermute | solution.py:37
  47.5 15.2 %collective-permute-start.6 = (bf16[256,2048]{1,0:T(8,128)(2,1)}, bf16[256,2048]{1,0:T(8,128)(2,1)}, u32[]{:S(2)}, u32[]{:S(2)}) collective-permute-start(bf16[256,2048]{1,0:T(8,128)(2,1)} %constant_dynamic-update-slice_fusion.4.refs_0_.refs_4_), channel_id=1, source_target_pairs={{0,32},{8,10},{1,33},{9,11},{16,48},{24,26},{17,49},{25,27},{32,64... | collective-permute-start | bytes 3145736 | tf_op jit(solution)/shard_map/ppermute | solution.py:37
  49.5 24.7 %collective-permute-start.7 = (bf16[256,2048]{1,0:T(8,128)(2,1)}, bf16[256,2048]{1,0:T(8,128)(2,1)}, u32[]{:S(2)}, u32[]{:S(2)}) collective-permute-start(bf16[256,2048]{1,0:T(8,128)(2,1)} %constant_dynamic-update-slice_fusion.4.refs_0_.refs_4_), channel_id=1, source_target_pairs={{0,64},{8,12},{1,65},{9,13},{16,80},{24,28},{17,81},{25,29},{32,96... | collective-permute-start | bytes 3145736 | tf_op jit(solution)/shard_map/ppermute | solution.py:37
  52.0 24.4 %collective-permute-start.8 = (bf16[256,2048]{1,0:T(8,128)(2,1)}, bf16[256,2048]{1,0:T(8,128)(2,1)}, u32[]{:S(2)}, u32[]{:S(2)}) collective-permute-start(bf16[256,2048]{1,0:T(8,128)(2,1)} %constant_dynamic-update-slice_fusion.4.refs_0_.refs_4_), channel_id=1, source_target_pairs={{0,96},{8,14},{1,97},{9,15},{16,112},{24,30},{17,113},{25,31},{32,... | collective-permute-start | bytes 3145736 | tf_op jit(solution)/shard_map/ppermute | solution.py:37
  53.2 23.4 %copy-start.1 = (bf16[128,16,256]{2,1,0:T(8,128)(2,1)}, bf16[128,16,256]{2,1,0:T(8,128)(2,1)S(1)}, u32[]{:S(2)}) copy-start(bf16[128,16,256]{2,1,0:T(8,128)(2,1)S(1)} %all-to-all-done) | copy-start | bytes 3145732
  54.2 22.4 %collective-permute-start.13 = (bf16[2048,256]{1,0:T(8,128)(2,1)S(1)}, bf16[2048,256]{1,0:T(8,128)(2,1)S(1)}, u32[]{:S(2)}, u32[]{:S(2)}) collective-permute-start(bf16[2048,256]{1,0:T(8,128)(2,1)S(1)} %bitcast.24), channel_id=1, source_target_pairs={{0,8},{8,0},{1,9},{9,1},{16,24},{24,16},{17,25},{25,17},{32,40},{4... | collective-permute-start | bytes 3145736 | tf_op jit(solution)/shard_map/ppermute | solution.py:42
  54.8 39.8 %collective-permute-start.9 = (bf16[256,2048]{1,0:T(8,128)(2,1)}, bf16[256,2048]{1,0:T(8,128)(2,1)}, u32[]{:S(2)}, u32[]{:S(2)}) collective-permute-start(bf16[256,2048]{1,0:T(8,128)(2,1)} %constant_dynamic-update-slice_fusion.4.refs_0_.refs_4_), channel_id=1, source_target_pairs={{0,8},{8,0},{1,9},{9,1},{16,24},{24,16},{17,25},{25,17},{32,40},{4... | collective-permute-start | bytes 3145736 | tf_op jit(solution)/shard_map/ppermute | solution.py:42
  62.7 33.3 %collective-permute-start.10 = (bf16[256,2048]{1,0:T(8,128)(2,1)}, bf16[256,2048]{1,0:T(8,128)(2,1)}, u32[]{:S(2)}, u32[]{:S(2)}) collective-permute-start(bf16[256,2048]{1,0:T(8,128)(2,1)} %collective-permute-done.6.refs_1_.refs_5_), channel_id=1, source_target_pairs={{0,8},{8,0},{1,9},{9,1},{16,24},{24,16},{17,25},{25,17},{32,40},{4... | collective-permute-start | bytes 3145736 | tf_op jit(solution)/shard_map/ppermute | solution.py:42
  74.2 22.5 %collective-permute-start.11 = (bf16[256,2048]{1,0:T(8,128)(2,1)}, bf16[256,2048]{1,0:T(8,128)(2,1)}, u32[]{:S(2)}, u32[]{:S(2)}) collective-permute-start(bf16[256,2048]{1,0:T(8,128)(2,1)} %collective-permute-done.7.refs_2_.refs_6_), channel_id=1, source_target_pairs={{0,8},{8,0},{1,9},{9,1},{16,24},{24,16},{17,25},{25,17},{32,40},{4... | collective-permute-start | bytes 3145736 | tf_op jit(solution)/shard_map/ppermute | solution.py:42
  76.4 22.3 %collective-permute-start.12 = (bf16[256,2048]{1,0:T(8,128)(2,1)}, bf16[256,2048]{1,0:T(8,128)(2,1)}, u32[]{:S(2)}, u32[]{:S(2)}) collective-permute-start(bf16[256,2048]{1,0:T(8,128)(2,1)} %collective-permute-done.8.refs_3_.refs_7_), channel_id=1, source_target_pairs={{0,8},{8,0},{1,9},{9,1},{16,24},{24,16},{17,25},{25,17},{32,40},{4... | collective-permute-start | bytes 3145736 | tf_op jit(solution)/shard_map/ppermute | solution.py:42
  76.6 1.0 copy-start.2
  84.8 48.1 %collective-permute-start.23 = (bf16[512,1024]{1,0:T(8,128)(2,1)}, bf16[512,1024]{1,0:T(8,128)(2,1)S(1)}, u32[]{:S(2)}, u32[]{:S(2)}) collective-permute-start(bf16[512,1024]{1,0:T(8,128)(2,1)} %get-tuple-element.24.refs_12_), channel_id=1, source_target_pairs={{0,16},{8,24},{1,17},{9,25},{16,0},{24,8},{17,1},{25,9},{32,48},{4... | collective-permute-start | bytes 3145736 | tf_op jit(solution)/shard_map/ppermute | solution.py:37
  88.0 59.1 %all-to-all-start.1 = ((bf16[128,16,512]{2,1,0:T(8,128)(2,1)}), bf16[128,16,512]{2,1,0:T(8,128)(2,1)S(1)}, u32[]{:S(2)}, u32[]{:S(2)}) async-start(bf16[128,16,512]{2,1,0:T(8,128)(2,1)} %get-tuple-element.20), calls=%async_computation.1 | async-start | bytes 4194304 | tf_op jit(solution)/shard_map/all_to_all | solution.py:451
  94.6 36.8 %collective-permute-start.15 = (bf16[256,1024]{1,0:T(8,128)(2,1)}, bf16[256,1024]{1,0:T(8,128)(2,1)}, u32[]{:S(2)}, u32[]{:S(2)}) collective-permute-start(bf16[256,1024]{1,0:T(8,128)(2,1)} %get-tuple-element.28), channel_id=1, source_target_pairs={{0,32},{8,40},{1,33},{9,41},{16,48},{24,56},{17,49},{25,57},{32,64... | collective-permute-start | bytes 1572872 | tf_op jit(solution)/shard_map/ppermute | solution.py:37
  96.0 50.0 %collective-permute-start.14 = (bf16[512,1024]{1,0:T(8,128)(2,1)}, bf16[512,1024]{1,0:T(8,128)(2,1)S(1)}, u32[]{:S(2)}, u32[]{:S(2)}) collective-permute-start(bf16[512,1024]{1,0:T(8,128)(2,1)} %get-tuple-element.24.refs_12_), channel_id=1, source_target_pairs={{0,8},{8,0},{1,9},{9,1},{16,24},{24,16},{17,25},{25,17},{32,40},{4... | collective-permute-start | bytes 3145736 | tf_op jit(solution)/shard_map/ppermute | solution.py:42
  96.7 37.8 %collective-permute-start.17 = (bf16[256,1024]{1,0:T(8,128)(2,1)}, bf16[256,1024]{1,0:T(8,128)(2,1)}, u32[]{:S(2)}, u32[]{:S(2)}) collective-permute-start(bf16[256,1024]{1,0:T(8,128)(2,1)} %get-tuple-element.28), channel_id=1, source_target_pairs={{0,96},{8,104},{1,97},{9,105},{16,112},{24,120},{17,113},{25,121},... | collective-permute-start | bytes 1572872 | tf_op jit(solution)/shard_map/ppermute | solution.py:37
  98.7 43.9 %collective-permute-start.19 = (bf16[256,1024]{1,0:T(8,128)(2,1)}, bf16[256,1024]{1,0:T(8,128)(2,1)}, u32[]{:S(2)}, u32[]{:S(2)}) collective-permute-start(bf16[256,1024]{1,0:T(8,128)(2,1)} %get-tuple-element.30), channel_id=1, source_target_pairs={{0,32},{8,40},{1,33},{9,41},{16,48},{24,56},{17,49},{25,57},{32,64... | collective-permute-start | bytes 1572872 | tf_op jit(solution)/shard_map/ppermute | solution.py:37
  131.4 12.9 %collective-permute-start.21 = (bf16[256,1024]{1,0:T(8,128)(2,1)}, bf16[256,1024]{1,0:T(8,128)(2,1)}, u32[]{:S(2)}, u32[]{:S(2)}) collective-permute-start(bf16[256,1024]{1,0:T(8,128)(2,1)} %get-tuple-element.30), channel_id=1, source_target_pairs={{0,96},{8,104},{1,97},{9,105},{16,112},{24,120},{17,113},{25,121},... | collective-permute-start | bytes 1572872 | tf_op jit(solution)/shard_map/ppermute | solution.py:37
  132.8 33.1 %collective-permute-start.24 = (bf16[512,1024]{1,0:T(8,128)(2,1)S(1)}, bf16[512,1024]{1,0:T(8,128)(2,1)}, u32[]{:S(2)}, u32[]{:S(2)}) collective-permute-start(bf16[512,1024]{1,0:T(8,128)(2,1)S(1)} %collective-permute-done.23.refs_9_), channel_id=1, source_target_pairs={{0,8},{8,0},{1,9},{9,1},{16,24},{24,16},{17,25},{25,17},{32,40},{4... | collective-permute-start | bytes 3145736 | tf_op jit(solution)/shard_map/ppermute | solution.py:42
  134.4 24.3 %collective-permute-start.16 = (bf16[256,1024]{1,0:T(8,128)(2,1)}, bf16[256,1024]{1,0:T(8,128)(2,1)}, u32[]{:S(2)}, u32[]{:S(2)}) collective-permute-start(bf16[256,1024]{1,0:T(8,128)(2,1)} %collective-permute-done.15.refs_5_), channel_id=1, source_target_pairs={{0,8},{8,0},{1,9},{9,1},{16,24},{24,16},{17,25},{25,17},{32,40},{4... | collective-permute-start | bytes 1572872 | tf_op jit(solution)/shard_map/ppermute | solution.py:42
  142.6 16.2 %collective-permute-start.18 = (bf16[256,1024]{1,0:T(8,128)(2,1)}, bf16[256,1024]{1,0:T(8,128)(2,1)}, u32[]{:S(2)}, u32[]{:S(2)}) collective-permute-start(bf16[256,1024]{1,0:T(8,128)(2,1)} %collective-permute-done.17.refs_7_), channel_id=1, source_target_pairs={{0,8},{8,0},{1,9},{9,1},{16,24},{24,16},{17,25},{25,17},{32,40},{4... | collective-permute-start | bytes 1572872 | tf_op jit(solution)/shard_map/ppermute | solution.py:42
  144.2 21.7 %collective-permute-start.20 = (bf16[256,1024]{1,0:T(8,128)(2,1)}, bf16[256,1024]{1,0:T(8,128)(2,1)}, u32[]{:S(2)}, u32[]{:S(2)}) collective-permute-start(bf16[256,1024]{1,0:T(8,128)(2,1)} %collective-permute-done.19.refs_5_), channel_id=1, source_target_pairs={{0,8},{8,0},{1,9},{9,1},{16,24},{24,16},{17,25},{25,17},{32,40},{4... | collective-permute-start | bytes 1572872 | tf_op jit(solution)/shard_map/ppermute | solution.py:42
  146.0 1.0 copy-start.3
  147.1 18.9 %collective-permute-start.22 = (bf16[256,1024]{1,0:T(8,128)(2,1)}, bf16[256,1024]{1,0:T(8,128)(2,1)}, u32[]{:S(2)}, u32[]{:S(2)}) collective-permute-start(bf16[256,1024]{1,0:T(8,128)(2,1)} %collective-permute-done.21.refs_7_), channel_id=1, source_target_pairs={{0,8},{8,0},{1,9},{9,1},{16,24},{24,16},{17,25},{25,17},{32,40},{4... | collective-permute-start | bytes 1572872 | tf_op jit(solution)/shard_map/ppermute | solution.py:42

commit v5 on v4

--- a/solution.py
+++ b/solution.py
@@ -145,7 +145,7 @@
         for h in range(2)
     ]
     for h in range(2):
-        lax.fori_loop(8 * h, 8 * h + 8, emit, 0, unroll=2)
+        lax.fori_loop(8 * h, 8 * h + 8, emit, 0, unroll=4)
         sends[h].start()
     send_part.wait()
     for send in sends:
@@ -439,7 +439,7 @@
     beside = partner_eps[None, :, None] - jnp.stack([virtuals[3], virtuals[1]])[:, None, :]
     across = partner_eps[:, None] - virtuals[2:3]
     first = beside[:, :2].reshape(1, 512)
-    second = jnp.concatenate([beside[:, 2:].reshape(1, 512), across.reshape(1, 512)], axis=1)
+    second = jnp.concatenate([across.reshape(1, 512), beside[:, 2:].reshape(1, 512)], axis=1)
     return row, near.reshape(1, 512), first, second
 
 
@@ -456,7 +456,7 @@
     part, table, *energy = lax.optimization_barrier((part, table, *energy))
     row, near, first, second = energy
     other = swapped(part)
-    here, *halves = partner_fit(table, part, other, mine_parts)
+    here, *halves = partner_fit(table, on_chip(part), other, mine_parts)
 
     def whole_rows(part):
         return part, swapped(part)
@@ -471,7 +471,7 @@
     across = tuple(on_chip(half) for half in across)
     own, density = own_and_pair(table, own, row, near, mine_parts + other_parts, [[here]])
     density = paired(table, own, density, row, first, [beside[0]], False)
-    density = paired(table, own, density, row, second, [beside[1], [across]], True)
+    density = paired(table, own, density, row, second, [[across], beside[1]], True)
     return density.reshape(8, 64, 2048)
 
 

time: 176 us -> 175 us (level)
    unnamed x21 -> x19, local copies, waits for them, and re-layouts: 5.39 us -> 5.37 us
where the time goes in v5:
time: 175 us
  waiting for transfers between devices  70 us (40%)
  starting transfers between devices  43.6 us (25%)
  Pallas kernels  42.7 us (24%)
  local copies, waits for them, and re-layouts  11 us (6%)
  other arithmetic  4.07 us (2%)
  between operations  3.1 us (2%)
    ppermute x14, waiting for transfers between devices, shifted(): return lax.ppermute(value, AXES, pairs)  70 us
    ppermute x14, starting transfers between devices, shifted(): return lax.ppermute(value, AXES, pairs)  21.8 us
    pallas_call x2, Pallas kernels, paired(): pl.pallas_call(body, in_specs=[smem, hbm, hbm, vmem, vmem] + [hbm] * len(...  16.3 us
    pallas_call x1, Pallas kernels, own_and_pair(): pl.pallas_call(body, in_specs=[smem, vmem, vmem, vmem] + [hbm] * (8 + len...  11.7 us
    all_to_all x1, starting transfers between devices, whole(): part = lax.all_to_all(part, AXES, split_axis=0, concat_axis=0, tiled=True)  9.17 us
    pallas_call x1, Pallas kernels, transformed(): pl.pallas_call(half_kernel, in_specs=[pl.BlockSpec(memory_space=pltpu.SME...  7.81 us
    pallas_call x1, Pallas kernels, partner_fit(): pl.pallas_call(partner_kernel, in_specs=[smem] + [pl.BlockSpec(memory_spa...  6.95 us
    all_to_all x1, starting transfers between devices, whole(): own = lax.all_to_all(own, AXES, split_axis=0, concat_axis=0, tiled=True)  6.62 us
  transfers between devices with their start and end apart: 27, of which 9 were waited for; matrix products, arithmetic and copies ran while one was open for 8% of the time, Pallas kernels for 19%

profile of v5, /device:TPU:1, one launch (start us, length us, event | category | flops | bytes accessed | tf_op | source)
XLA Modules:
  0.0 174.7 jit_solution(3656534845073017844)
XLA Ops:
  0.0 2.1 %collective-permute-start = (bf16[16,2048]{1,0:T(8,128)(2,1)}, bf16[16,2048]{1,0:T(8,128)(2,1)S(1)}, u32[]{:S(2)}, u32[]{:S(2)}) collective-permute-start(bf16[16,2048]{1,0:T(8,128)(2,1)} %param.10), channel_id=1, source_target_pairs={{0,1},{8,40},{1,16},{9,41},{16,17},{24,56},{17,0},{25,57},{32,33},... | collective-permute-start | bytes 196616 | tf_op jit(solution)/shard_map/ppermute | solution.py:37
  2.1 2.6 %collective-permute-start.1 = (bf16[16,2048]{1,0:T(8,128)(2,1)}, bf16[16,2048]{1,0:T(8,128)(2,1)S(1)}, u32[]{:S(2)}, u32[]{:S(2)}) collective-permute-start(bf16[16,2048]{1,0:T(8,128)(2,1)} %param.10), channel_id=1, source_target_pairs={{0,16},{8,72},{1,17},{9,73},{16,0},{24,88},{17,1},{25,89},{32,48},... | collective-permute-start | bytes 196616 | tf_op jit(solution)/shard_map/ppermute | solution.py:37
  4.7 1.1 collective-permute-start.2
  5.8 7.8 %half.1 = (bf16[128,16,256]{2,1,0:T(8,128)(2,1)}, bf16[128,16,512]{2,1,0:T(8,128)(2,1)}) custom-call(s32[4]{0:T(128)} %order_ref.1, s32[1,128]{1,0:T(1,128)} %bitcast.35, bf16[16,128,640]{2,1,0:T(8,128)(2,1)} %ints_ref.1, bf16[640,512]{1,0:T(8,128)(2,1)} %coeff_ref.1), custom_call_target="tpu_custom_call" | custom-call | tf_op jit(solution)/shard_map/half/pallas_call | solution.py:159
  13.6 9.2 %all-to-all-start = ((bf16[128,16,256]{2,1,0:T(8,128)(2,1)}), bf16[128,16,256]{2,1,0:T(8,128)(2,1)S(1)}, u32[]{:S(2)}, u32[]{:S(2)}) async-start(bf16[128,16,256]{2,1,0:T(8,128)(2,1)} %get-tuple-element.18), calls=%async_computation | async-start | bytes 2097152 | tf_op jit(solution)/shard_map/all_to_all | solution.py:450
  22.9 0.7 fusion.4
  26.2 0.6 constant_dynamic-update-slice_fusion.3
  26.9 0.2 convolution_bitcast_fusion
  27.1 0.7 fusion.3
  27.8 2.6 %pad_maximum_fusion.3 = f32[4]{0:T(128)S(1)} fusion(f32[1]{0:T(128)} %get-tuple-element.48, f32[1]{0:T(128)} %get-tuple-element.49, f32[1]{0:T(128)} %get-tuple-element.50, f32[1]{0:T(128)} %get-tuple-element.47), kind=kLoop, calls=%fused_computation.21 | loop fusion | flops 12 | bytes 32 | tf_op jit(solution)/shard_map/concatenate | solution.py:432
  30.5 0.1 broadcast_subtract_fusion
  30.5 0.1 dynamic_slice.26
  30.6 0.1 dynamic_slice.25
  30.7 0.6 constant_dynamic-update-slice_fusion.2
  31.3 0.0 collective-permute-done.1
  31.3 0.6 constant_dynamic-update-slice_fusion.1
  31.9 0.0 collective-permute-done.2
  32.0 0.6 constant_dynamic-update-slice_fusion
  32.6 1.5 collective-permute-start.3
  34.1 0.1 broadcast_subtract_fusion.1
  34.1 2.9 %collective-permute-start.4 = (bf16[64,2048]{1,0:T(8,128)(2,1)S(1)}, bf16[64,2048]{1,0:T(8,128)(2,1)S(1)}, u32[]{:S(2)}, u32[]{:S(2)}) collective-permute-start(bf16[64,2048]{1,0:T(8,128)(2,1)S(1)} %get-tuple-element.31), channel_id=1, source_target_pairs={{0,4},{8,24},{1,5},{9,25},{16,20},{24,8},{17,21},{25,9},{32,36},{4... | collective-permute-start | bytes 786440 | tf_op jit(solution)/shard_map/ppermute | solution.py:37
  37.1 1.3 constant_dynamic-slice_fusion.1
  38.4 0.1 sub.95
  38.5 0.9 collective-permute-start.5
  39.4 3.7 %collective-permute-done.3 = bf16[64,2048]{1,0:T(8,128)(2,1)S(1)} collective-permute-done((bf16[64,2048]{1,0:T(8,128)(2,1)S(1)}, bf16[64,2048]{1,0:T(8,128)(2,1)S(1)}, u32[]{:S(2)}, u32[]{:S(2)}) %collective-permute-start.3) | collective-permute-done | bytes 262176 | tf_op jit(solution)/shard_map/ppermute | solution.py:37
  43.0 0.7 constant_dynamic-update-slice_fusion.6
  43.8 2.1 %collective-permute-done.4 = bf16[64,2048]{1,0:T(8,128)(2,1)S(1)} collective-permute-done((bf16[64,2048]{1,0:T(8,128)(2,1)S(1)}, bf16[64,2048]{1,0:T(8,128)(2,1)S(1)}, u32[]{:S(2)}, u32[]{:S(2)}) %collective-permute-start.4) | collective-permute-done | bytes 262176 | tf_op jit(solution)/shard_map/ppermute | solution.py:37
  45.9 0.7 constant_dynamic-update-slice_fusion.5
  46.6 0.7 constant_dynamic-update-slice_fusion.4.refs_0_.refs_4_
  47.3 0.2 collective-permute-start.6
  47.5 0.7 broadcast_subtract_fusion.2
  48.1 0.6 fusion.2
  48.7 0.6 pad_maximum_fusion.1.refs_4_
  49.3 2.5 %collective-permute-start.7 = (bf16[256,2048]{1,0:T(8,128)(2,1)}, bf16[256,2048]{1,0:T(8,128)(2,1)}, u32[]{:S(2)}, u32[]{:S(2)}) collective-permute-start(bf16[256,2048]{1,0:T(8,128)(2,1)} %constant_dynamic-update-slice_fusion.4.refs_0_.refs_4_), channel_id=1, source_target_pairs={{0,64},{8,12},{1,65},{9,13},{16,80},{24,28},{17,81},{25,29},{32,96... | collective-permute-start | bytes 3145736 | tf_op jit(solution)/shard_map/ppermute | solution.py:37
  51.8 1.2 collective-permute-start.8
  53.0 0.8 broadcast_in_dim.2.refs_2_.refs_3_
  53.9 0.3 collective-permute-start.13
  54.2 0.2 collective-permute-start.9
  54.4 8.1 %collective-permute-done.6.refs_1_.refs_5_ = bf16[256,2048]{1,0:T(8,128)(2,1)} collective-permute-done((bf16[256,2048]{1,0:T(8,128)(2,1)}, bf16[256,2048]{1,0:T(8,128)(2,1)}, u32[]{:S(2)}, u32[]{:S(2)}) %collective-permute-start.6) | collective-permute-done | bytes 1048608 | tf_op jit(solution)/shard_map/ppermute | solution.py:37
  62.5 11.5 %collective-permute-done.7.refs_2_.refs_6_ = bf16[256,2048]{1,0:T(8,128)(2,1)} collective-permute-done((bf16[256,2048]{1,0:T(8,128)(2,1)}, bf16[256,2048]{1,0:T(8,128)(2,1)}, u32[]{:S(2)}, u32[]{:S(2)}) %collective-permute-start.7) | collective-permute-done | bytes 1048608 | tf_op jit(solution)/shard_map/ppermute | solution.py:37
  74.0 0.4 collective-permute-start.11
  74.4 1.7 collective-permute-done.8.refs_3_.refs_7_
  76.2 0.0 collective-permute-start.12
  76.2 1.0 copy-done.1
  77.2 6.9 %fit_partner.1 = (bf16[512,1024]{1,0:T(8,128)(2,1)}, bf16[256,1024]{1,0:T(8,128)(2,1)}, bf16[256,1024]{1,0:T(8,128)(2,1)}) custom-call(s32[129]{0:T(256)} %bitcast.26, bf16[2048,256]{1,0:T(8,128)(2,1)S(1)} %bitcast.25, bf16[2048,256]{1,0:T(8,128)(2,1)} %copy-done.1, bf16[256,2048]{1,0:T(8,128)(2,1)} %constant_dynamic-update-slice_fusion.4.refs_0_.refs_4_, ...), custom_call_target="tpu_custom_call" | custom-call | tf_op jit(solution)/shard_map/fit_partner/pallas_call | solution.py:227
  84.2 3.2 %collective-permute-start.19 = (bf16[512,1024]{1,0:T(8,128)(2,1)}, bf16[512,1024]{1,0:T(8,128)(2,1)S(1)}, u32[]{:S(2)}, u32[]{:S(2)}) collective-permute-start(bf16[512,1024]{1,0:T(8,128)(2,1)} %get-tuple-element.24.refs_12_), channel_id=1, source_target_pairs={{0,16},{8,24},{1,17},{9,25},{16,0},{24,8},{17,1},{25,9},{32,48},{4... | collective-permute-start | bytes 3145736 | tf_op jit(solution)/shard_map/ppermute | solution.py:37
  87.4 6.6 %all-to-all-start.1 = ((bf16[128,16,512]{2,1,0:T(8,128)(2,1)}), bf16[128,16,512]{2,1,0:T(8,128)(2,1)S(1)}, u32[]{:S(2)}, u32[]{:S(2)}) async-start(bf16[128,16,512]{2,1,0:T(8,128)(2,1)} %get-tuple-element.20), calls=%async_computation.1 | async-start | bytes 4194304 | tf_op jit(solution)/shard_map/all_to_all | solution.py:451
  94.0 1.4 collective-permute-start.15
  95.4 0.7 collective-permute-start.14
  96.1 2.0 %collective-permute-start.17 = (bf16[256,1024]{1,0:T(8,128)(2,1)}, bf16[256,1024]{1,0:T(8,128)(2,1)}, u32[]{:S(2)}, u32[]{:S(2)}) collective-permute-start(bf16[256,1024]{1,0:T(8,128)(2,1)} %get-tuple-element.28), channel_id=1, source_target_pairs={{0,96},{8,104},{1,97},{9,105},{16,112},{24,120},{17,113},{25,121},... | collective-permute-start | bytes 1572872 | tf_op jit(solution)/shard_map/ppermute | solution.py:37
  98.1 32.7 %collective-permute-done.15.refs_5_ = bf16[256,1024]{1,0:T(8,128)(2,1)} collective-permute-done((bf16[256,1024]{1,0:T(8,128)(2,1)}, bf16[256,1024]{1,0:T(8,128)(2,1)}, u32[]{:S(2)}, u32[]{:S(2)}) %collective-permute-start.15) | collective-permute-done | bytes 524320 | tf_op jit(solution)/shard_map/ppermute | solution.py:37
  130.8 0.2 collective-permute-start.23
  131.0 1.1 collective-permute-done.19.refs_5_
  132.1 1.9 %collective-permute-start.20 = (bf16[512,1024]{1,0:T(8,128)(2,1)S(1)}, bf16[512,1024]{1,0:T(8,128)(2,1)}, u32[]{:S(2)}, u32[]{:S(2)}) collective-permute-start(bf16[512,1024]{1,0:T(8,128)(2,1)S(1)} %collective-permute-done.19.refs_5_), channel_id=1, source_target_pairs={{0,8},{8,0},{1,9},{9,1},{16,24},{24,16},{17,25},{25,17},{32,40},{4... | collective-permute-start | bytes 3145736 | tf_op jit(solution)/shard_map/ppermute | solution.py:42
  134.0 0.0 collective-permute-start.16
  134.0 8.1 %collective-permute-done.21.refs_7_ = bf16[256,1024]{1,0:T(8,128)(2,1)} collective-permute-done((bf16[256,1024]{1,0:T(8,128)(2,1)}, bf16[256,1024]{1,0:T(8,128)(2,1)}, u32[]{:S(2)}, u32[]{:S(2)}) %collective-permute-start.21) | collective-permute-done | bytes 524320 | tf_op jit(solution)/shard_map/ppermute | solution.py:37
  142.0 0.7 collective-permute-start.18
  142.7 1.0 collective-permute-done.23.refs_9_
  143.7 1.8 %collective-permute-start.22 = (bf16[256,1024]{1,0:T(8,128)(2,1)}, bf16[256,1024]{1,0:T(8,128)(2,1)}, u32[]{:S(2)}, u32[]{:S(2)}) collective-permute-start(bf16[256,1024]{1,0:T(8,128)(2,1)} %collective-permute-done.21.refs_7_), channel_id=1, source_target_pairs={{0,8},{8,0},{1,9},{9,1},{16,24},{24,16},{17,25},{25,17},{32,40},{4... | collective-permute-start | bytes 1572872 | tf_op jit(solution)/shard_map/ppermute | solution.py:42
  145.5 1.0 copy-done.2
  146.5 0.0 collective-permute-start.24
  146.5 11.7 %own_and_pair.1 = (bf16[512,2048]{1,0:T(8,128)(2,1)}, f32[512,2048]{1,0:T(8,128)}) custom-call(s32[129]{0:T(256)} %bitcast.27, bf16[2048,512]{1,0:T(8,128)(2,1)S(1)} %bitcast.23, f32[512,128]{1,0:T(8,128)} %broadcast_in_dim.2.refs_2_.refs_3_, f32[1,512]{1,0:T(1,128)} %bitcast.33, bf16[256,2048]{1,0:T(8,128)(2,1)} %constant_dynamic-update-slice_fusion.4.refs_0_.refs_4_, ...), custom_call_target="tpu_custom_call" | custom-call | tf_op jit(solution)/shard_map/own_and_pair/pallas_call | solution.py:331
  158.2 7.1 %pair.1.refs_2_ = f32[512,2048]{1,0:T(8,128)} custom-call(s32[129]{0:T(256)} %bitcast.28, bf16[512,2048]{1,0:T(8,128)(2,1)} %get-tuple-element.25.refs_1_, f32[512,2048]{1,0:T(8,128)} %get-tuple-element.26.refs_2_, f32[512,128]{1,0:T(8,128)} %broadcast_in_dim.2.refs_2_.refs_3_, f32[1,512]{1,0:T(1,128)} %bitcast.32, ...), custom_call_target="tpu_custom_call" | custom-call | tf_op jit(solution)/shard_map/pair/pallas_call | solution.py:403
  165.4 9.2 %pair_last.1 = f32[512,2048]{1,0:T(8,128)} custom-call(s32[129]{0:T(256)} %bitcast.29, bf16[512,2048]{1,0:T(8,128)(2,1)} %get-tuple-element.25.refs_1_, f32[512,2048]{1,0:T(8,128)} %pair.1.refs_2_, f32[512,128]{1,0:T(8,128)} %broadcast_in_dim.2.refs_2_.refs_3_, f32[1,1024]{1,0:T(1,128)} %pad_maximum_fusion.1.refs_4_, ...), custom_call_target="tpu_custom_call" | custom-call | tf_op jit(solution)/shard_map/pair_last/pallas_call | solution.py:403
  (34 shorter events, 0.1 us)
Async XLA Ops:
  0.0 26.9 %copy-start = (f32[128]{0:T(128)S(1)}, f32[128]{0:T(128)}, u32[]{:S(2)}) copy-start(f32[128]{0:T(128)} %param.13) | copy-start | bytes 1540
  0.0 30.7 %collective-permute-start = (bf16[16,2048]{1,0:T(8,128)(2,1)}, bf16[16,2048]{1,0:T(8,128)(2,1)S(1)}, u32[]{:S(2)}, u32[]{:S(2)}) collective-permute-start(bf16[16,2048]{1,0:T(8,128)(2,1)} %param.10), channel_id=1, source_target_pairs={{0,1},{8,40},{1,16},{9,41},{16,17},{24,56},{17,0},{25,57},{32,33},... | collective-permute-start | bytes 196616 | tf_op jit(solution)/shard_map/ppermute | solution.py:37
  2.1 29.2 %collective-permute-start.1 = (bf16[16,2048]{1,0:T(8,128)(2,1)}, bf16[16,2048]{1,0:T(8,128)(2,1)S(1)}, u32[]{:S(2)}, u32[]{:S(2)}) collective-permute-start(bf16[16,2048]{1,0:T(8,128)(2,1)} %param.10), channel_id=1, source_target_pairs={{0,16},{8,72},{1,17},{9,73},{16,0},{24,88},{17,1},{25,89},{32,48},... | collective-permute-start | bytes 196616 | tf_op jit(solution)/shard_map/ppermute | solution.py:37
  4.7 27.2 %collective-permute-start.2 = (bf16[16,2048]{1,0:T(8,128)(2,1)}, bf16[16,2048]{1,0:T(8,128)(2,1)S(1)}, u32[]{:S(2)}, u32[]{:S(2)}) collective-permute-start(bf16[16,2048]{1,0:T(8,128)(2,1)} %param.10), channel_id=1, source_target_pairs={{0,17},{8,104},{1,0},{9,105},{16,1},{24,120},{17,16},{25,121},{32,... | collective-permute-start | bytes 196616 | tf_op jit(solution)/shard_map/ppermute | solution.py:37
  5.8 17.1 %copy-start.4 = (s32[4]{0:T(128)S(1)}, s32[4]{0:T(128)}, u32[]{:S(2)}) copy-start(s32[4]{0:T(128)} %order_ref.1) | copy-start | bytes 52
  5.8 20.4 %copy-start.3 = (bf16[16,2048]{1,0:T(8,128)(2,1)S(1)}, bf16[16,2048]{1,0:T(8,128)(2,1)}, u32[]{:S(2)}) copy-start(bf16[16,2048]{1,0:T(8,128)(2,1)} %param.10) | copy-start | bytes 196612
  5.8 21.0 %copy-start.5 = (f32[512]{0:T(512)S(1)}, f32[512]{0:T(512)}, u32[]{:S(2)}) copy-start(f32[512]{0:T(512)} %param.14) | copy-start | bytes 6148
  5.8 21.0 %copy-start.6 = (s32[128]{0:T(128)S(1)}, s32[128]{0:T(128)}, u32[]{:S(2)}) copy-start(s32[128]{0:T(128)} %param.11) | copy-start | bytes 1540
  13.6 39.4 %all-to-all-start = ((bf16[128,16,256]{2,1,0:T(8,128)(2,1)}), bf16[128,16,256]{2,1,0:T(8,128)(2,1)S(1)}, u32[]{:S(2)}, u32[]{:S(2)}) async-start(bf16[128,16,256]{2,1,0:T(8,128)(2,1)} %get-tuple-element.18), calls=%async_computation | async-start | bytes 2097152 | tf_op jit(solution)/shard_map/all_to_all | solution.py:450
  32.6 10.5 %collective-permute-start.3 = (bf16[64,2048]{1,0:T(8,128)(2,1)S(1)}, bf16[64,2048]{1,0:T(8,128)(2,1)S(1)}, u32[]{:S(2)}, u32[]{:S(2)}) collective-permute-start(bf16[64,2048]{1,0:T(8,128)(2,1)S(1)} %get-tuple-element.31), channel_id=1, source_target_pairs={{0,2},{8,9},{1,3},{9,24},{16,18},{24,25},{17,19},{25,8},{32,34},{4... | collective-permute-start | bytes 786440 | tf_op jit(solution)/shard_map/ppermute | solution.py:37
  34.1 11.7 %collective-permute-start.4 = (bf16[64,2048]{1,0:T(8,128)(2,1)S(1)}, bf16[64,2048]{1,0:T(8,128)(2,1)S(1)}, u32[]{:S(2)}, u32[]{:S(2)}) collective-permute-start(bf16[64,2048]{1,0:T(8,128)(2,1)S(1)} %get-tuple-element.31), channel_id=1, source_target_pairs={{0,4},{8,24},{1,5},{9,25},{16,20},{24,8},{17,21},{25,9},{32,36},{4... | collective-permute-start | bytes 786440 | tf_op jit(solution)/shard_map/ppermute | solution.py:37
  38.5 8.1 %collective-permute-start.5 = (bf16[64,2048]{1,0:T(8,128)(2,1)S(1)}, bf16[64,2048]{1,0:T(8,128)(2,1)S(1)}, u32[]{:S(2)}, u32[]{:S(2)}) collective-permute-start(bf16[64,2048]{1,0:T(8,128)(2,1)S(1)} %get-tuple-element.31), channel_id=1, source_target_pairs={{0,6},{8,25},{1,7},{9,8},{16,22},{24,9},{17,23},{25,24},{32,38},{4... | collective-permute-start | bytes 786440 | tf_op jit(solution)/shard_map/ppermute | solution.py:37
  47.3 15.2 %collective-permute-start.6 = (bf16[256,2048]{1,0:T(8,128)(2,1)}, bf16[256,2048]{1,0:T(8,128)(2,1)}, u32[]{:S(2)}, u32[]{:S(2)}) collective-permute-start(bf16[256,2048]{1,0:T(8,128)(2,1)} %constant_dynamic-update-slice_fusion.4.refs_0_.refs_4_), channel_id=1, source_target_pairs={{0,32},{8,10},{1,33},{9,11},{16,48},{24,26},{17,49},{25,27},{32,64... | collective-permute-start | bytes 3145736 | tf_op jit(solution)/shard_map/ppermute | solution.py:37
  49.3 24.7 %collective-permute-start.7 = (bf16[256,2048]{1,0:T(8,128)(2,1)}, bf16[256,2048]{1,0:T(8,128)(2,1)}, u32[]{:S(2)}, u32[]{:S(2)}) collective-permute-start(bf16[256,2048]{1,0:T(8,128)(2,1)} %constant_dynamic-update-slice_fusion.4.refs_0_.refs_4_), channel_id=1, source_target_pairs={{0,64},{8,12},{1,65},{9,13},{16,80},{24,28},{17,81},{25,29},{32,96... | collective-permute-start | bytes 3145736 | tf_op jit(solution)/shard_map/ppermute | solution.py:37
  51.8 24.3 %collective-permute-start.8 = (bf16[256,2048]{1,0:T(8,128)(2,1)}, bf16[256,2048]{1,0:T(8,128)(2,1)}, u32[]{:S(2)}, u32[]{:S(2)}) collective-permute-start(bf16[256,2048]{1,0:T(8,128)(2,1)} %constant_dynamic-update-slice_fusion.4.refs_0_.refs_4_), channel_id=1, source_target_pairs={{0,96},{8,14},{1,97},{9,15},{16,112},{24,30},{17,113},{25,31},{32,... | collective-permute-start | bytes 3145736 | tf_op jit(solution)/shard_map/ppermute | solution.py:37
  53.9 22.3 %collective-permute-start.13 = (bf16[2048,256]{1,0:T(8,128)(2,1)S(1)}, bf16[2048,256]{1,0:T(8,128)(2,1)S(1)}, u32[]{:S(2)}, u32[]{:S(2)}) collective-permute-start(bf16[2048,256]{1,0:T(8,128)(2,1)S(1)} %bitcast.24), channel_id=1, source_target_pairs={{0,8},{8,0},{1,9},{9,1},{16,24},{24,16},{17,25},{25,17},{32,40},{4... | collective-permute-start | bytes 3145736 | tf_op jit(solution)/shard_map/ppermute | solution.py:42
  54.2 39.8 %collective-permute-start.9 = (bf16[256,2048]{1,0:T(8,128)(2,1)}, bf16[256,2048]{1,0:T(8,128)(2,1)}, u32[]{:S(2)}, u32[]{:S(2)}) collective-permute-start(bf16[256,2048]{1,0:T(8,128)(2,1)} %constant_dynamic-update-slice_fusion.4.refs_0_.refs_4_), channel_id=1, source_target_pairs={{0,8},{8,0},{1,9},{9,1},{16,24},{24,16},{17,25},{25,17},{32,40},{4... | collective-permute-start | bytes 3145736 | tf_op jit(solution)/shard_map/ppermute | solution.py:42
  62.5 33.0 %collective-permute-start.10 = (bf16[256,2048]{1,0:T(8,128)(2,1)}, bf16[256,2048]{1,0:T(8,128)(2,1)}, u32[]{:S(2)}, u32[]{:S(2)}) collective-permute-start(bf16[256,2048]{1,0:T(8,128)(2,1)} %collective-permute-done.6.refs_1_.refs_5_), channel_id=1, source_target_pairs={{0,8},{8,0},{1,9},{9,1},{16,24},{24,16},{17,25},{25,17},{32,40},{4... | collective-permute-start | bytes 3145736 | tf_op jit(solution)/shard_map/ppermute | solution.py:42
  74.0 22.1 %collective-permute-start.11 = (bf16[256,2048]{1,0:T(8,128)(2,1)}, bf16[256,2048]{1,0:T(8,128)(2,1)}, u32[]{:S(2)}, u32[]{:S(2)}) collective-permute-start(bf16[256,2048]{1,0:T(8,128)(2,1)} %collective-permute-done.7.refs_2_.refs_6_), channel_id=1, source_target_pairs={{0,8},{8,0},{1,9},{9,1},{16,24},{24,16},{17,25},{25,17},{32,40},{4... | collective-permute-start | bytes 3145736 | tf_op jit(solution)/shard_map/ppermute | solution.py:42
  76.2 21.9 %collective-permute-start.12 = (bf16[256,2048]{1,0:T(8,128)(2,1)}, bf16[256,2048]{1,0:T(8,128)(2,1)}, u32[]{:S(2)}, u32[]{:S(2)}) collective-permute-start(bf16[256,2048]{1,0:T(8,128)(2,1)} %collective-permute-done.8.refs_3_.refs_7_), channel_id=1, source_target_pairs={{0,8},{8,0},{1,9},{9,1},{16,24},{24,16},{17,25},{25,17},{32,40},{4... | collective-permute-start | bytes 3145736 | tf_op jit(solution)/shard_map/ppermute | solution.py:42
  76.2 1.0 copy-start.1
  84.2 47.9 %collective-permute-start.19 = (bf16[512,1024]{1,0:T(8,128)(2,1)}, bf16[512,1024]{1,0:T(8,128)(2,1)S(1)}, u32[]{:S(2)}, u32[]{:S(2)}) collective-permute-start(bf16[512,1024]{1,0:T(8,128)(2,1)} %get-tuple-element.24.refs_12_), channel_id=1, source_target_pairs={{0,16},{8,24},{1,17},{9,25},{16,0},{24,8},{17,1},{25,9},{32,48},{4... | collective-permute-start | bytes 3145736 | tf_op jit(solution)/shard_map/ppermute | solution.py:37
  87.4 59.1 %all-to-all-start.1 = ((bf16[128,16,512]{2,1,0:T(8,128)(2,1)}), bf16[128,16,512]{2,1,0:T(8,128)(2,1)S(1)}, u32[]{:S(2)}, u32[]{:S(2)}) async-start(bf16[128,16,512]{2,1,0:T(8,128)(2,1)} %get-tuple-element.20), calls=%async_computation.1 | async-start | bytes 4194304 | tf_op jit(solution)/shard_map/all_to_all | solution.py:451
  94.0 36.8 %collective-permute-start.15 = (bf16[256,1024]{1,0:T(8,128)(2,1)}, bf16[256,1024]{1,0:T(8,128)(2,1)}, u32[]{:S(2)}, u32[]{:S(2)}) collective-permute-start(bf16[256,1024]{1,0:T(8,128)(2,1)} %get-tuple-element.28), channel_id=1, source_target_pairs={{0,32},{8,40},{1,33},{9,41},{16,48},{24,56},{17,49},{25,57},{32,64... | collective-permute-start | bytes 1572872 | tf_op jit(solution)/shard_map/ppermute | solution.py:37
  95.4 50.0 %collective-permute-start.14 = (bf16[512,1024]{1,0:T(8,128)(2,1)}, bf16[512,1024]{1,0:T(8,128)(2,1)S(1)}, u32[]{:S(2)}, u32[]{:S(2)}) collective-permute-start(bf16[512,1024]{1,0:T(8,128)(2,1)} %get-tuple-element.24.refs_12_), channel_id=1, source_target_pairs={{0,8},{8,0},{1,9},{9,1},{16,24},{24,16},{17,25},{25,17},{32,40},{4... | collective-permute-start | bytes 3145736 | tf_op jit(solution)/shard_map/ppermute | solution.py:42
  96.1 37.8 %collective-permute-start.17 = (bf16[256,1024]{1,0:T(8,128)(2,1)}, bf16[256,1024]{1,0:T(8,128)(2,1)}, u32[]{:S(2)}, u32[]{:S(2)}) collective-permute-start(bf16[256,1024]{1,0:T(8,128)(2,1)} %get-tuple-element.28), channel_id=1, source_target_pairs={{0,96},{8,104},{1,97},{9,105},{16,112},{24,120},{17,113},{25,121},... | collective-permute-start | bytes 1572872 | tf_op jit(solution)/shard_map/ppermute | solution.py:37
  98.1 43.9 %collective-permute-start.21 = (bf16[256,1024]{1,0:T(8,128)(2,1)}, bf16[256,1024]{1,0:T(8,128)(2,1)}, u32[]{:S(2)}, u32[]{:S(2)}) collective-permute-start(bf16[256,1024]{1,0:T(8,128)(2,1)} %get-tuple-element.30), channel_id=1, source_target_pairs={{0,32},{8,40},{1,33},{9,41},{16,48},{24,56},{17,49},{25,57},{32,64... | collective-permute-start | bytes 1572872 | tf_op jit(solution)/shard_map/ppermute | solution.py:37
  130.8 12.9 %collective-permute-start.23 = (bf16[256,1024]{1,0:T(8,128)(2,1)}, bf16[256,1024]{1,0:T(8,128)(2,1)}, u32[]{:S(2)}, u32[]{:S(2)}) collective-permute-start(bf16[256,1024]{1,0:T(8,128)(2,1)} %get-tuple-element.30), channel_id=1, source_target_pairs={{0,96},{8,104},{1,97},{9,105},{16,112},{24,120},{17,113},{25,121},... | collective-permute-start | bytes 1572872 | tf_op jit(solution)/shard_map/ppermute | solution.py:37
  132.1 33.3 %collective-permute-start.20 = (bf16[512,1024]{1,0:T(8,128)(2,1)S(1)}, bf16[512,1024]{1,0:T(8,128)(2,1)}, u32[]{:S(2)}, u32[]{:S(2)}) collective-permute-start(bf16[512,1024]{1,0:T(8,128)(2,1)S(1)} %collective-permute-done.19.refs_5_), channel_id=1, source_target_pairs={{0,8},{8,0},{1,9},{9,1},{16,24},{24,16},{17,25},{25,17},{32,40},{4... | collective-permute-start | bytes 3145736 | tf_op jit(solution)/shard_map/ppermute | solution.py:42
  134.0 24.2 %collective-permute-start.16 = (bf16[256,1024]{1,0:T(8,128)(2,1)}, bf16[256,1024]{1,0:T(8,128)(2,1)}, u32[]{:S(2)}, u32[]{:S(2)}) collective-permute-start(bf16[256,1024]{1,0:T(8,128)(2,1)} %collective-permute-done.15.refs_5_), channel_id=1, source_target_pairs={{0,8},{8,0},{1,9},{9,1},{16,24},{24,16},{17,25},{25,17},{32,40},{4... | collective-permute-start | bytes 1572872 | tf_op jit(solution)/shard_map/ppermute | solution.py:42
  142.0 16.2 %collective-permute-start.18 = (bf16[256,1024]{1,0:T(8,128)(2,1)}, bf16[256,1024]{1,0:T(8,128)(2,1)}, u32[]{:S(2)}, u32[]{:S(2)}) collective-permute-start(bf16[256,1024]{1,0:T(8,128)(2,1)} %collective-permute-done.17.refs_7_), channel_id=1, source_target_pairs={{0,8},{8,0},{1,9},{9,1},{16,24},{24,16},{17,25},{25,17},{32,40},{4... | collective-permute-start | bytes 1572872 | tf_op jit(solution)/shard_map/ppermute | solution.py:42
  143.7 21.7 %collective-permute-start.22 = (bf16[256,1024]{1,0:T(8,128)(2,1)}, bf16[256,1024]{1,0:T(8,128)(2,1)}, u32[]{:S(2)}, u32[]{:S(2)}) collective-permute-start(bf16[256,1024]{1,0:T(8,128)(2,1)} %collective-permute-done.21.refs_7_), channel_id=1, source_target_pairs={{0,8},{8,0},{1,9},{9,1},{16,24},{24,16},{17,25},{25,17},{32,40},{4... | collective-permute-start | bytes 1572872 | tf_op jit(solution)/shard_map/ppermute | solution.py:42
  145.5 1.0 copy-start.2
  146.5 18.9 %collective-permute-start.24 = (bf16[256,1024]{1,0:T(8,128)(2,1)}, bf16[256,1024]{1,0:T(8,128)(2,1)}, u32[]{:S(2)}, u32[]{:S(2)}) collective-permute-start(bf16[256,1024]{1,0:T(8,128)(2,1)} %collective-permute-done.23.refs_9_), channel_id=1, source_target_pairs={{0,8},{8,0},{1,9},{9,1},{16,24},{24,16},{17,25},{25,17},{32,40},{4... | collective-permute-start | bytes 1572872 | tf_op jit(solution)/shard_map/ppermute | solution.py:42
